TPU v7x, 32 devices: a whole 2x2x4 slice. The times are simulated.
32 devices in a mesh: seq: 16 (over z, y, x), mp: 2 (over core).
Axes of the slice: x: 2, y: 2, z: 4, core: 2. Of those that a mesh axis runs over, the one named last changes fastest.
Arguments:
- bytes_in: bfloat16 [16384, 1024], P('seq'), may hold values from -6 to 6
- out_grad: bfloat16 [16384, 1024], P('seq'), may hold values from -6 to 6
- seq_ids: int32 [2048], replicated, may hold values from 0 to 5, never falling along the last dimension, each value on 1 to 1024 neighbouring positions
- norm_gain: float32 [1024], P('seq'), may hold values from 0.5 to 1.5
- w_z: float32 [1024, 2048], P('seq', 'mp'), may hold values from -0.1875 to 0.1875
- w_x: float32 [1024, 2048], P('seq', 'mp'), may hold values from -0.1875 to 0.1875
- w_bc: float32 [1024, 256], P('seq'), may hold values from -0.1875 to 0.1875
- w_dt: float32 [1024, 32], P('seq', 'mp'), may hold values from -0.1875 to 0.1875
- w_out: float32 [2048, 1024], P('mp', 'seq'), may hold values from -0.125 to 0.125
- attn_gain: float32 [1024], P('seq'), may hold values from 0.5 to 1.5
- w_q: float32 [1024, 1024], P('seq', 'mp'), may hold values from -0.1875 to 0.1875
- w_k: float32 [1024, 1024], P('seq', 'mp'), may hold values from -0.1875 to 0.1875
- w_v: float32 [1024, 1024], P('seq', 'mp'), may hold values from -0.1875 to 0.1875
- w_o: float32 [1024, 1024], P('mp', 'seq'), may hold values from -0.5 to 0.5
- mlp_gain: float32 [1024], P('seq'), may hold values from 0.5 to 1.5
- w_gate: float32 [1024, 4096], P('seq', 'mp'), may hold values from -0.1875 to 0.1875
- w_up: float32 [1024, 4096], P('seq', 'mp'), may hold values from -0.1875 to 0.1875
- w_down: float32 [4096, 1024], P('mp', 'seq'), may hold values from -0.09375 to 0.09375
- dt_bias: float32 [32], P('mp'), may hold values from -1 to 1
- a_log: float32 [32], P('mp')
- d_skip: float32 [32], P('mp'), may hold values from 0.5 to 1.5
- conv_x: float32 [4, 2048], P(None, 'mp'), may hold values from -3 to 3
- conv_bc: float32 [4, 256], replicated, may hold values from -3 to 3
- inner_gain: float32 [2048], P('mp'), may hold values from 0.5 to 1.5
Outputs:
- block_out: float32 [16384, 1024], P('seq')
- bytes_grad: float32 [16384, 1024], P('seq')
- norm_gain_grad: float32 [1024], P('seq')
- w_z_grad: float32 [1024, 2048], P('seq', 'mp')
- w_x_grad: float32 [1024, 2048], P('seq', 'mp')
- w_bc_grad: float32 [1024, 256], P('seq')
- w_dt_grad: float32 [1024, 32], P('seq', 'mp')
- w_out_grad: float32 [2048, 1024], P('mp', 'seq')
- attn_gain_grad: float32 [1024], P('seq')
- w_q_grad: float32 [1024, 1024], P('seq', 'mp')
- w_k_grad: float32 [1024, 1024], P('seq', 'mp')
- w_v_grad: float32 [1024, 1024], P('seq', 'mp')
- w_o_grad: float32 [1024, 1024], P('mp', 'seq')
- mlp_gain_grad: float32 [1024], P('seq')
- w_gate_grad: float32 [1024, 4096], P('seq', 'mp')
- w_up_grad: float32 [1024, 4096], P('seq', 'mp')
- w_down_grad: float32 [4096, 1024], P('mp', 'seq')
- dt_bias_grad: float32 [32], P('mp')
- a_log_grad: float32 [32], P('mp')
- d_skip_grad: float32 [32], P('mp')
- conv_x_grad: float32 [4, 2048], P(None, 'mp')
- conv_bc_grad: float32 [4, 256], replicated
- inner_gain_grad: float32 [2048], P('mp')
Inputs may be any that keep to these rules, and one draw needn't show every extreme that they name: `seq_ids`: patches of one sequence are contiguous and ids never fall; every id appears; one sequence has exactly 1024 patches.
All inputs are finite; a program needn't handle non-finite values.
Results may differ from a plain program's by a relative error of at most 0.022.
Values may be sent and summed in bfloat16 or wider, within the bound.
No kernel may reach another device: no remote copies, remote signals or barrier semaphores. Data moves between devices by JAX's collectives and lax.ppermute only.
A program may use at most 256 MiB of HBM per device.

v0:
```python
import jax
import jax.numpy as jnp
from jax import lax
from jax.sharding import PartitionSpec as P

LHD = 64
PATCH = 8


EPS = 1e-05
BIG = 1e30
PRECISE = lax.Precision.HIGHEST


def passed_along(shard, axis, by):
    peers = lax.axis_size(axis)
    pairs = [(i, i + by) for i in range(peers) if 0 <= i + by < peers]
    return lax.ppermute(shard, axis, pairs)


def prefix(shard, axis, combine, identity):
    peers, index = (lax.axis_size(axis), lax.axis_index(axis))
    everything = jax.tree.map(lambda part: lax.all_gather(part, axis), shard)
    start = jax.tree.map(
        lambda part, zero: jnp.broadcast_to(jnp.asarray(zero, part.dtype), part.shape),
        shard,
        identity,
    )

    def turn(k, before):
        reached = k < index
        new = combine(before, jax.tree.map(lambda part: part[k], everything))
        return jax.tree.map(lambda a, b: jnp.where(reached, a, b), new, before)

    return lax.fori_loop(0, peers, turn, start)


def carried_in(shard, axis, join, neutral):
    count = lax.axis_size(axis)
    place = lax.axis_index(axis)
    ahead = count - 1 - place
    gathered = jax.tree.map(
        lambda a, kind: lax.all_gather(a.astype(kind), axis),
        shard,
        jax.tree.map(lambda a: jnp.bfloat16 if a.dtype == jnp.float32 else a.dtype, shard),
    )
    state = jax.tree.map(lambda a, e: jnp.zeros_like(a) + jnp.asarray(e, a.dtype), shard, neutral)

    def one(turn, state):
        source = count - 1 - turn
        return join(
            state,
            jax.tree.map(
                lambda a, own: lax.dynamic_index_in_dim(a, source, 0, False).astype(own.dtype),
                gathered,
                shard,
            ),
        )

    return lax.fori_loop(0, ahead, one, state)


def bf_dot(left, right):
    return jnp.dot(left, right, preferred_element_type=jnp.float32)


def rms_rows(values):
    return lax.rsqrt(jnp.mean(values * values, axis=-1, keepdims=True) + EPS)


def norm_back(grad_in, values, rstd_rows, gain_row):
    normed_rows = values * rstd_rows
    gain_grad = jnp.sum(grad_in * normed_rows, axis=0)
    scaled = grad_in * gain_row[None, :]
    input_grad = rstd_rows * (
        scaled - normed_rows * jnp.mean(scaled * normed_rows, axis=-1, keepdims=True)
    )
    return (input_grad, gain_grad)


def softplus_fn(values):
    return jnp.log1p(jnp.exp(-jnp.abs(values))) + jnp.maximum(values, 0.0)


def conv_taps(extended, ids_ext, kernel):
    conv_width = kernel.shape[0]
    row_count = extended.shape[0] - conv_width + 1
    target = ids_ext[conv_width - 1 :]
    summed = jnp.zeros((row_count, extended.shape[1]), jnp.float32)
    for tap_index in range(conv_width):
        same_seg = (ids_ext[tap_index : tap_index + row_count] == target).astype(jnp.float32)
        summed = (
            summed
            + extended[tap_index : tap_index + row_count]
            * kernel[tap_index][None, :]
            * same_seg[:, None]
        )
    return summed


def ssd_block(x_heads, b_rows, c_rows, step_size, log_decay, seg_rows, prev_seg, d_skip):
    length = x_heads.shape[0]
    cum_decay = jnp.cumsum(log_decay, axis=0)
    cum_heads = cum_decay.T
    same_seg = seg_rows[:, None] == seg_rows[None, :]
    row_pos = lax.broadcasted_iota(jnp.int32, (length, length), 0)
    col_pos = lax.broadcasted_iota(jnp.int32, (length, length), 1)
    live_mask = same_seg & (row_pos >= col_pos)
    decay_gaps = cum_heads[:, :, None] - cum_heads[:, None, :]
    decay_mat = jnp.exp(jnp.where(live_mask[None], decay_gaps, -BIG))
    inner_prod = jnp.dot(c_rows, b_rows.T, precision=PRECISE, preferred_element_type=jnp.float32)
    mix_mat = inner_prod[None] * decay_mat * step_size.T[:, None, :]
    y_local = (
        jnp.einsum("hts,shp->thp", mix_mat, x_heads, precision=PRECISE)
        + d_skip[None, :, None] * x_heads
    )
    carried = (seg_rows == prev_seg).astype(jnp.float32)
    decay_in = carried[:, None] * jnp.exp(cum_decay)
    end_same = seg_rows == seg_rows[length - 1]
    end_gap = cum_decay[length - 1][None, :] - cum_decay
    tail_w = jnp.exp(jnp.where(end_same[:, None], end_gap, -BIG)) * step_size
    state_local = jnp.einsum("shp,sn->hpn", x_heads * tail_w[:, :, None], b_rows, precision=PRECISE)
    return (y_local, decay_in, state_local, decay_in[length - 1])


def carry_combine(earlier, later):
    return (earlier[0] * later[0], later[0][:, None, None] * earlier[1] + later[1])


def head_total(values):
    return lax.psum(values, "mp")


def fetch_first(masters):
    lowered = [master.astype(jnp.bfloat16) for master in masters]
    return (
        lax.all_gather(lowered[0], "seq", axis=0, tiled=True),
        lax.all_gather(lowered[1], "seq", axis=0, tiled=True),
        lax.all_gather(lowered[2], "seq", axis=0, tiled=True),
        lax.all_gather(lowered[3], "seq", axis=0, tiled=True),
        lax.all_gather(lowered[4], "seq", axis=0, tiled=True),
        lax.all_gather(lowered[5], "seq", axis=1, tiled=True),
        lax.all_gather(lowered[6], "seq", axis=0, tiled=True),
        lax.all_gather(lowered[7], "seq", axis=0, tiled=True),
        lax.all_gather(lowered[8], "seq", axis=0, tiled=True),
        lax.all_gather(lowered[9], "seq", axis=0, tiled=True),
        lax.all_gather(lowered[10], "seq", axis=1, tiled=True),
        lax.all_gather(lowered[11], "seq", axis=0, tiled=True),
        lax.all_gather(lowered[12], "seq", axis=0, tiled=True),
        lax.all_gather(lowered[13], "seq", axis=0, tiled=True),
        lax.all_gather(lowered[14], "seq", axis=1, tiled=True),
    )


def fetch_again(masters):
    lowered = [master.astype(jnp.bfloat16) for master in masters]
    return (
        lax.all_gather(lowered[0], "seq", axis=0, tiled=True),
        lax.all_gather(lowered[1], "seq", axis=0, tiled=True),
        lax.all_gather(lowered[2], "seq", axis=0, tiled=True),
        lax.all_gather(lowered[3], "seq", axis=0, tiled=True),
        lax.all_gather(lowered[4], "seq", axis=0, tiled=True),
        lax.all_gather(lowered[5], "seq", axis=1, tiled=True),
        lax.all_gather(lowered[6], "seq", axis=0, tiled=True),
        lax.all_gather(lowered[7], "seq", axis=0, tiled=True),
        lax.all_gather(lowered[8], "seq", axis=0, tiled=True),
        lax.all_gather(lowered[9], "seq", axis=0, tiled=True),
        lax.all_gather(lowered[10], "seq", axis=1, tiled=True),
        lax.all_gather(lowered[11], "seq", axis=0, tiled=True),
        lax.all_gather(lowered[12], "seq", axis=0, tiled=True),
        lax.all_gather(lowered[13], "seq", axis=0, tiled=True),
        lax.all_gather(lowered[14], "seq", axis=1, tiled=True),
    )


def soft_scores(queries, key_rows, shape_four):
    scale = LHD ** (-0.5)
    scores = (
        jnp.einsum(
            "bqhd,bkhd->bhqk",
            queries.reshape(shape_four),
            key_rows.reshape(shape_four),
            preferred_element_type=jnp.float32,
        )
        * scale
    )
    row_pos = lax.broadcasted_iota(jnp.int32, (PATCH, PATCH), 0)
    col_pos = lax.broadcasted_iota(jnp.int32, (PATCH, PATCH), 1)
    masked = jnp.where((row_pos >= col_pos)[None, None], scores, -BIG)
    row_max = jnp.max(masked, axis=-1, keepdims=True)
    exp_scores = jnp.exp(masked - row_max)
    return exp_scores / jnp.sum(exp_scores, axis=-1, keepdims=True)


def local(
    bytes_in,
    out_grad,
    seq_ids,
    norm_gain,
    w_z,
    w_x,
    w_bc,
    w_dt,
    w_out,
    attn_gain,
    w_q,
    w_k,
    w_v,
    w_o,
    mlp_gain,
    w_gate,
    w_up,
    w_down,
    dt_bias,
    a_log,
    d_skip,
    conv_x,
    conv_bc,
    inner_gain,
):
    masters = (
        norm_gain,
        w_z,
        w_x,
        w_bc,
        w_dt,
        w_out,
        attn_gain,
        w_q,
        w_k,
        w_v,
        w_o,
        mlp_gain,
        w_gate,
        w_up,
        w_down,
    )
    gathered = fetch_first(masters)
    byte_rows = bytes_in.shape[0]
    patch_rows = byte_rows // PATCH
    model_width = bytes_in.shape[1]
    x_float = bytes_in.astype(jnp.float32)
    patch_in = jnp.mean(x_float.reshape(patch_rows, PATCH, model_width), axis=1)
    rstd_patch = rms_rows(patch_in)
    h_norm = (patch_in * rstd_patch * gathered[0].astype(jnp.float32)[None, :]).astype(jnp.bfloat16)
    gate_z = bf_dot(h_norm, gathered[1])
    inner_local = gathered[2].shape[1]
    mixed_in = jnp.concatenate(
        [bf_dot(h_norm, gathered[2]), bf_dot(h_norm, gathered[3])], axis=1
    ).astype(jnp.bfloat16)
    dt_raw = bf_dot(h_norm, gathered[4])
    conv_width = conv_x.shape[0]
    state_size = conv_bc.shape[1] // 2
    rim_rows = passed_along(mixed_in[patch_rows - (conv_width - 1) :], "seq", 1)
    extended = jnp.concatenate([rim_rows, mixed_in], axis=0).astype(jnp.float32)
    first_row = lax.axis_index("seq") * patch_rows
    ids_padded = jnp.concatenate([jnp.full((conv_width - 1,), -1, jnp.int32), seq_ids])
    ids_ext = lax.dynamic_slice_in_dim(ids_padded, first_row, patch_rows + conv_width - 1)
    seg_rows = ids_ext[conv_width - 1 :]
    prev_seg = ids_ext[conv_width - 2]
    head_count = a_log.shape[0]
    head_size = inner_local // head_count

    def mixer_core(ext_in, raw_in, kernel_x, kernel_bc, bias_in, rate_in, skip_in):
        kernel = jnp.concatenate([kernel_x, kernel_bc], axis=1)
        activated = jax.nn.silu(conv_taps(ext_in, ids_ext, kernel))
        x_heads = activated[:, :inner_local].reshape(patch_rows, head_count, head_size)
        b_rows = activated[:, inner_local : inner_local + state_size]
        c_rows = activated[:, inner_local + state_size :]
        step_size = softplus_fn(raw_in + bias_in[None, :])
        log_decay = -step_size * jnp.exp(rate_in)[None, :]
        y_local, decay_in, state_local, total_decay = ssd_block(
            x_heads, b_rows, c_rows, step_size, log_decay, seg_rows, prev_seg, skip_in
        )
        return (y_local, c_rows, decay_in, state_local, total_decay)

    core_out, core_back = jax.vjp(
        mixer_core, extended, dt_raw, conv_x, conv_bc, dt_bias, a_log, d_skip
    )
    y_local, c_rows, decay_in, state_local, total_decay = core_out
    identity = (jnp.ones_like(total_decay), jnp.zeros_like(state_local))
    incoming = prefix((total_decay, state_local), "seq", carry_combine, identity)
    state_in = incoming[1]

    def finish_mix(y_part, c_part, decay_part, state_part, z_part):
        y_full = y_part + decay_part[:, :, None] * jnp.einsum(
            "tn,hpn->thp", c_part, state_part, precision=PRECISE
        )
        return y_full.reshape(patch_rows, inner_local) * jax.nn.silu(z_part)

    gated_out, finish_back = jax.vjp(finish_mix, y_local, c_rows, decay_in, state_in, gate_z)
    square_sum = head_total(jnp.sum(gated_out * gated_out, axis=-1))
    inner_full = inner_local * lax.axis_size("mp")
    rstd_inner = lax.rsqrt(square_sum / inner_full + EPS)[:, None]
    y_norm = (gated_out * rstd_inner * inner_gain[None, :]).astype(jnp.bfloat16)
    mixer_out = head_total(bf_dot(y_norm, gathered[5]))
    patch_out = patch_in + mixer_out
    rows_in = x_float + jnp.repeat(patch_out, PATCH, axis=0)
    rstd_attn = rms_rows(rows_in)
    normed = (rows_in * rstd_attn * gathered[6].astype(jnp.float32)[None, :]).astype(jnp.bfloat16)
    queries = bf_dot(normed, gathered[7]).astype(jnp.bfloat16)
    key_rows = bf_dot(normed, gathered[8]).astype(jnp.bfloat16)
    value_rows = bf_dot(normed, gathered[9]).astype(jnp.bfloat16)
    attn_width = queries.shape[1]
    shape_four = (patch_rows, PATCH, attn_width // LHD, LHD)
    soft_weights = soft_scores(queries, key_rows, shape_four)
    soft_low = soft_weights.astype(jnp.bfloat16)
    attended = (
        jnp.einsum(
            "bhqk,bkhd->bqhd",
            soft_low,
            value_rows.reshape(shape_four),
            preferred_element_type=jnp.float32,
        )
        .astype(jnp.bfloat16)
        .reshape(byte_rows, attn_width)
    )
    after_attn = rows_in + head_total(bf_dot(attended, gathered[10]))
    rstd_mlp = rms_rows(after_attn)
    normed_mlp = (after_attn * rstd_mlp * gathered[11].astype(jnp.float32)[None, :]).astype(
        jnp.bfloat16
    )
    gate_val = bf_dot(normed_mlp, gathered[12])
    up_val = bf_dot(normed_mlp, gathered[13])
    hidden = (jax.nn.silu(gate_val) * up_val).astype(jnp.bfloat16)
    block_out = after_attn + head_total(bf_dot(hidden, gathered[14]))
    weights_back = fetch_again(masters)
    grad_float = out_grad.astype(jnp.float32)
    w_down_grad = jnp.einsum("rf,rd->fd", hidden, out_grad, preferred_element_type=jnp.float32)
    hidden_grad = jnp.einsum(
        "rd,fd->rf", out_grad, weights_back[14], preferred_element_type=jnp.float32
    )
    sigmoid_gate = jax.nn.sigmoid(gate_val)
    gate_grad = (
        hidden_grad * up_val * sigmoid_gate * (1.0 + gate_val * (1.0 - sigmoid_gate))
    ).astype(jnp.bfloat16)
    up_grad = (hidden_grad * gate_val * sigmoid_gate).astype(jnp.bfloat16)
    w_gate_grad = jnp.einsum("rd,rf->df", normed_mlp, gate_grad, preferred_element_type=jnp.float32)
    w_up_grad = jnp.einsum("rd,rf->df", normed_mlp, up_grad, preferred_element_type=jnp.float32)
    mlp_norm_grad = head_total(
        jnp.einsum("rf,df->rd", gate_grad, weights_back[12], preferred_element_type=jnp.float32)
        + jnp.einsum("rf,df->rd", up_grad, weights_back[13], preferred_element_type=jnp.float32)
    )
    mlp_in_grad, mlp_gain_grad = norm_back(
        mlp_norm_grad, after_attn, rstd_mlp, weights_back[11].astype(jnp.float32)
    )
    after_grad = grad_float + mlp_in_grad
    after_low = after_grad.astype(jnp.bfloat16)
    w_o_grad = jnp.einsum("ra,rd->ad", attended, after_low, preferred_element_type=jnp.float32)
    attended_grad = jnp.einsum(
        "rd,ad->ra", after_low, weights_back[10], preferred_element_type=jnp.float32
    ).astype(jnp.bfloat16)
    grad_four = attended_grad.reshape(shape_four)
    scale = LHD ** (-0.5)
    prob_grad = jnp.einsum(
        "bqhd,bkhd->bhqk",
        grad_four,
        value_rows.reshape(shape_four),
        preferred_element_type=jnp.float32,
    )
    score_grad = (
        soft_weights * (prob_grad - jnp.sum(soft_weights * prob_grad, axis=-1, keepdims=True))
    ).astype(jnp.bfloat16)
    query_grad = (
        (
            jnp.einsum(
                "bhqk,bkhd->bqhd",
                score_grad,
                key_rows.reshape(shape_four),
                preferred_element_type=jnp.float32,
            )
            * scale
        )
        .astype(jnp.bfloat16)
        .reshape(byte_rows, attn_width)
    )
    key_grad = (
        (
            jnp.einsum(
                "bhqk,bqhd->bkhd",
                score_grad,
                queries.reshape(shape_four),
                preferred_element_type=jnp.float32,
            )
            * scale
        )
        .astype(jnp.bfloat16)
        .reshape(byte_rows, attn_width)
    )
    value_grad = (
        jnp.einsum("bhqk,bqhd->bkhd", soft_low, grad_four, preferred_element_type=jnp.float32)
        .astype(jnp.bfloat16)
        .reshape(byte_rows, attn_width)
    )
    w_q_grad = jnp.einsum("rd,ra->da", normed, query_grad, preferred_element_type=jnp.float32)
    w_k_grad = jnp.einsum("rd,ra->da", normed, key_grad, preferred_element_type=jnp.float32)
    w_v_grad = jnp.einsum("rd,ra->da", normed, value_grad, preferred_element_type=jnp.float32)
    attn_norm_grad = head_total(
        jnp.einsum("ra,da->rd", query_grad, weights_back[7], preferred_element_type=jnp.float32)
        + jnp.einsum("ra,da->rd", key_grad, weights_back[8], preferred_element_type=jnp.float32)
        + jnp.einsum("ra,da->rd", value_grad, weights_back[9], preferred_element_type=jnp.float32)
    )
    attn_in_grad, attn_gain_grad = norm_back(
        attn_norm_grad, rows_in, rstd_attn, weights_back[6].astype(jnp.float32)
    )
    rows_grad = after_grad + attn_in_grad
    patch_grad = jnp.sum(rows_grad.reshape(patch_rows, PATCH, model_width), axis=1)
    patch_low = patch_grad.astype(jnp.bfloat16)
    w_out_grad = jnp.einsum("ri,rd->id", y_norm, patch_low, preferred_element_type=jnp.float32)
    y_norm_grad = jnp.einsum(
        "rd,id->ri", patch_low, weights_back[5], preferred_element_type=jnp.float32
    )
    inner_gain_grad = jnp.sum(y_norm_grad * gated_out * rstd_inner, axis=0)
    scaled = y_norm_grad * inner_gain[None, :]
    cross_sum = head_total(jnp.sum(scaled * gated_out, axis=-1))
    gated_grad = rstd_inner * scaled - gated_out * rstd_inner**3 * (cross_sum[:, None] / inner_full)
    y_grad, c_grad, decay_grad, state_in_grad, z_grad = finish_back(gated_grad)
    outgoing = carried_in((total_decay, state_in_grad), "seq", carry_combine, identity)
    state_grad = outgoing[1]
    total_grad = jnp.sum(state_grad * state_in, axis=(1, 2))
    ext_grad, raw_grad, conv_x_grad, conv_bc_part, dt_bias_grad, a_log_grad, d_skip_grad = (
        core_back((y_grad, c_grad, decay_grad, state_grad, total_grad))
    )
    bc_total, conv_bc_grad = (
        lax.psum(ext_grad[:, inner_local:].astype(jnp.bfloat16), "mp").astype(jnp.float32),
        lax.psum(conv_bc_part.astype(jnp.bfloat16), "mp").astype(jnp.float32),
    )
    ext_full = jnp.concatenate([ext_grad[:, :inner_local], bc_total], axis=1)
    rim_back = passed_along(ext_full[: conv_width - 1], "seq", -1)
    mixed_grad = ext_full[conv_width - 1 :] + jnp.concatenate(
        [jnp.zeros((patch_rows - (conv_width - 1), ext_full.shape[1]), jnp.float32), rim_back],
        axis=0,
    )
    mixed_low = mixed_grad.astype(jnp.bfloat16)
    x_in_grad = mixed_low[:, :inner_local]
    bc_grad = mixed_low[:, inner_local:]
    z_low = z_grad.astype(jnp.bfloat16)
    raw_low = raw_grad.astype(jnp.bfloat16)
    w_z_grad = jnp.einsum("rd,ri->di", h_norm, z_low, preferred_element_type=jnp.float32)
    w_x_grad = jnp.einsum("rd,ri->di", h_norm, x_in_grad, preferred_element_type=jnp.float32)
    w_bc_grad = jnp.einsum("rd,ri->di", h_norm, bc_grad, preferred_element_type=jnp.float32)
    w_dt_grad = jnp.einsum("rd,ri->di", h_norm, raw_low, preferred_element_type=jnp.float32)
    h_grad = head_total(
        jnp.einsum("ri,di->rd", z_low, weights_back[1], preferred_element_type=jnp.float32)
        + jnp.einsum("ri,di->rd", x_in_grad, weights_back[2], preferred_element_type=jnp.float32)
        + jnp.einsum("ri,di->rd", raw_low, weights_back[4], preferred_element_type=jnp.float32)
    )
    h_grad = h_grad + jnp.einsum(
        "ri,di->rd", bc_grad, weights_back[3], preferred_element_type=jnp.float32
    )
    patch_in_grad, norm_gain_grad = norm_back(
        h_grad, patch_in, rstd_patch, weights_back[0].astype(jnp.float32)
    )
    patch_total = patch_grad + patch_in_grad
    bytes_grad = rows_grad + jnp.repeat(patch_total / PATCH, PATCH, axis=0)
    grad_parts = (
        lax.psum_scatter(norm_gain_grad, "seq", scatter_dimension=0, tiled=True),
        lax.psum_scatter(w_z_grad, "seq", scatter_dimension=0, tiled=True),
        lax.psum_scatter(w_x_grad, "seq", scatter_dimension=0, tiled=True),
        lax.psum_scatter(w_bc_grad, "seq", scatter_dimension=0, tiled=True),
        lax.psum_scatter(w_dt_grad, "seq", scatter_dimension=0, tiled=True),
        lax.psum_scatter(w_out_grad, "seq", scatter_dimension=1, tiled=True),
        lax.psum_scatter(attn_gain_grad, "seq", scatter_dimension=0, tiled=True),
        lax.psum_scatter(w_q_grad, "seq", scatter_dimension=0, tiled=True),
        lax.psum_scatter(w_k_grad, "seq", scatter_dimension=0, tiled=True),
        lax.psum_scatter(w_v_grad, "seq", scatter_dimension=0, tiled=True),
        lax.psum_scatter(w_o_grad, "seq", scatter_dimension=1, tiled=True),
        lax.psum_scatter(mlp_gain_grad, "seq", scatter_dimension=0, tiled=True),
        lax.psum_scatter(w_gate_grad, "seq", scatter_dimension=0, tiled=True),
        lax.psum_scatter(w_up_grad, "seq", scatter_dimension=0, tiled=True),
        lax.psum_scatter(w_down_grad, "seq", scatter_dimension=1, tiled=True),
    )
    small_parts = lax.psum(
        (dt_bias_grad, a_log_grad, d_skip_grad, conv_x_grad, conv_bc_grad, inner_gain_grad), "seq"
    )
    return (
        block_out,
        bytes_grad,
        grad_parts[0],
        grad_parts[1],
        grad_parts[2],
        grad_parts[3],
        grad_parts[4],
        grad_parts[5],
        grad_parts[6],
        grad_parts[7],
        grad_parts[8],
        grad_parts[9],
        grad_parts[10],
        grad_parts[11],
        grad_parts[12],
        grad_parts[13],
        grad_parts[14],
        small_parts[0],
        small_parts[1],
        small_parts[2],
        small_parts[3],
        small_parts[4],
        small_parts[5],
    )


def solution(mesh):
    in_specs = (
        P("seq", None),
        P("seq", None),
        P(),
        P("seq"),
        P("seq", "mp"),
        P("seq", "mp"),
        P("seq", None),
        P("seq", "mp"),
        P("mp", "seq"),
        P("seq"),
        P("seq", "mp"),
        P("seq", "mp"),
        P("seq", "mp"),
        P("mp", "seq"),
        P("seq"),
        P("seq", "mp"),
        P("seq", "mp"),
        P("mp", "seq"),
        P("mp"),
        P("mp"),
        P("mp"),
        P(None, "mp"),
        P(),
        P("mp"),
    )
    out_specs = (
        P("seq", None),
        P("seq", None),
        P("seq"),
        P("seq", "mp"),
        P("seq", "mp"),
        P("seq", None),
        P("seq", "mp"),
        P("mp", "seq"),
        P("seq"),
        P("seq", "mp"),
        P("seq", "mp"),
        P("seq", "mp"),
        P("mp", "seq"),
        P("seq"),
        P("seq", "mp"),
        P("seq", "mp"),
        P("mp", "seq"),
        P("mp"),
        P("mp"),
        P("mp"),
        P(None, "mp"),
        P(),
        P("mp"),
    )
    return jax.shard_map(local, mesh=mesh, in_specs=in_specs, out_specs=out_specs, check_vma=False)
```

profile of v0, /device:TPU:0, one launch (start us, length us, event | category | flops | bytes accessed | tf_op | source)
XLA Modules:
  0.0 2568.4 jit_solution(9096403849109197615)
XLA Ops:
  13.6 44.9 %all-reduce.23 = (bf16[1024]{0:T(1024)(128)(2,1)}, bf16[1024]{0:T(1024)(128)(2,1)S(1)}, bf16[1024]{0:T(1024)(128)(2,1)S(1)}) all-reduce(bf16[1024]{0:T(1024)(128)(2,1)S(1)} %dynamic-update-slice.1, bf16[1024]{0:T(1024)(128)(2,1)S(1)} %dynamic-update-slice, ...), channel_id=1, replica_groups=mesh['seq'=16,'mp'=2] {'seq'}, use_global_device_ids=true, to_apply=%add.16 | all-reduce | flops 3072 | bytes 12288
  60.0 35.9 %all-gather.2 = bf16[16,64,16]{1,2,0:T(8,128)(2,1)S(1)} all-gather(bf16[1,64,16]{1,2,0:T(8,128)(2,1)S(1)} %convert_bitcast_fusion.3), channel_id=1, replica_groups=mesh['seq'=16,'mp'=2] {'seq'}, dimensions={0}, use_global_device_ids=true | all-gather | bytes 34816 | tf_op jit(solution)/shard_map/all_gather | solution.py:141
  103.9 40.9 %all_gather.81 = bf16[1024,256]{1,0:T(8,128)(2,1)S(1)} all-gather(bf16[64,256]{1,0:T(8,128)(2,1)S(1)} %convert_element_type.219), channel_id=1, replica_groups=mesh['seq'=16,'mp'=2] {'seq'}, dimensions={0}, use_global_device_ids=true | all-gather | bytes 557056 | tf_op jit(solution)/shard_map/all_gather | solution.py:140
  156.6 38.1 %all-gather.3 = f32[16,1,16]{2,1,0:T(1,128)S(1)} all-gather(f32[1,1,16]{2,1,0:T(1,128)S(1)} %bitcast.234), channel_id=1, replica_groups=mesh['seq'=16,'mp'=2] {'seq'}, dimensions={0}, use_global_device_ids=true | all-gather | bytes 1088 | tf_op jit(solution)/shard_map/all_gather | solution.py:23
  195.1 70.1 %all-gather.38.cloned.1.call-done = f32[256,64,128]{2,1,0:T(8,128)} async-done(((f32[16,64,128]{2,1,0:T(8,128)}), f32[256,64,128]{2,1,0:T(8,128)}) %all-gather.38.cloned.1.call-update) | async-done | bytes 8388624 | tf_op jit(solution)/shard_map/all_gather | solution.py:23
  265.2 19.4 while.29
  287.8 39.6 %all-gather.20.cloned.1.call-done = bf16[1024,1024]{1,0:T(8,128)(2,1)} async-done(((bf16[64,1024]{1,0:T(8,128)(2,1)}), bf16[1024,1024]{1,0:T(8,128)(2,1)}) %all-gather.20.cloned.1.call-update) | async-done | bytes 2097168 | tf_op jit(solution)/shard_map/all_gather | solution.py:138
  334.8 55.3 %all-gather.22.cloned.1.call-done = bf16[1024,1024]{0,1:T(8,128)(2,1)} async-done(((bf16[1024,64]{0,1:T(8,128)(2,1)}), bf16[1024,1024]{0,1:T(8,128)(2,1)}) %all-gather.22.cloned.1.call-update) | async-done | bytes 2097168 | tf_op jit(solution)/shard_map/all_gather | solution.py:142
  412.6 58.3 %all-gather.26.cloned.1.call-done = bf16[1024,512]{1,0:T(8,128)(2,1)} async-done(((bf16[64,512]{1,0:T(8,128)(2,1)}), bf16[1024,512]{1,0:T(8,128)(2,1)}) %all-gather.26.cloned.1.call-update) | async-done | bytes 1048592 | tf_op jit(solution)/shard_map/all_gather | solution.py:144
  478.3 50.4 %all-gather.28.cloned.1.call-done = bf16[1024,512]{1,0:T(8,128)(2,1)} async-done(((bf16[64,512]{1,0:T(8,128)(2,1)}), bf16[1024,512]{1,0:T(8,128)(2,1)}) %all-gather.28.cloned.1.call-update) | async-done | bytes 1048592 | tf_op jit(solution)/shard_map/all_gather | solution.py:145
  536.1 50.4 %all-gather.24.cloned.1.call-done = bf16[1024,512]{1,0:T(8,128)(2,1)} async-done(((bf16[64,512]{1,0:T(8,128)(2,1)}), bf16[1024,512]{1,0:T(8,128)(2,1)}) %all-gather.24.cloned.1.call-update) | async-done | bytes 1048592 | tf_op jit(solution)/shard_map/all_gather | solution.py:146
  620.6 23.7 all-gather.30.cloned.1.call-done
  655.3 21.3 all-reduce.33.cloned.1.call-done
  683.3 73.9 %all-gather.32.cloned.1.call-done = bf16[1024,2048]{1,0:T(8,128)(2,1)} async-done(((bf16[64,2048]{1,0:T(8,128)(2,1)}), bf16[1024,2048]{1,0:T(8,128)(2,1)}) %all-gather.32.cloned.1.call-update) | async-done | bytes 4194320 | tf_op jit(solution)/shard_map/all_gather | solution.py:149
  767.9 67.3 %all-gather.34.cloned.1.call-done = bf16[1024,2048]{1,0:T(8,128)(2,1)} async-done(((bf16[64,2048]{1,0:T(8,128)(2,1)}), bf16[1024,2048]{1,0:T(8,128)(2,1)}) %all-gather.34.cloned.1.call-update) | async-done | bytes 4194320 | tf_op jit(solution)/shard_map/all_gather | solution.py:150
  845.8 67.4 %all-gather.36.cloned.1.call-done = bf16[2048,1024]{0,1:T(8,128)(2,1)} async-done(((bf16[2048,64]{0,1:T(8,128)(2,1)}), bf16[2048,1024]{0,1:T(8,128)(2,1)}) %all-gather.36.cloned.1.call-update) | async-done | bytes 4194320 | tf_op jit(solution)/shard_map/all_gather | solution.py:151
  943.3 27.1 %all-reduce.35.cloned.1.call-done = f32[1024,1024]{1,0:T(8,128)} async-done(((f32[1024,1024]{1,0:T(8,128)}), f32[1024,1024]{1,0:T(8,128)}) %all-reduce.35.cloned.1.call-update) | async-done | bytes 4194320 | tf_op jit(solution)/shard_map/psum | solution.py:131
  1031.1 29.7 %all-reduce.37.cloned.1.call-done = f32[1024,1024]{1,0:T(8,128)} async-done(((f32[1024,1024]{1,0:T(8,128)}), f32[1024,1024]{1,0:T(8,128)}) %all-reduce.37.cloned.1.call-update) | async-done | bytes 4194320 | tf_op jit(solution)/shard_map/psum | solution.py:131
  1079.8 41.2 %all-gather.4 = bf16[16,1,16]{2,1,0:T(2,128)(2,1)S(1)} all-gather(bf16[1,1,16]{2,1,0:T(2,128)(2,1)S(1)} %bitcast.235), channel_id=1, replica_groups=mesh['seq'=16,'mp'=2] {'seq'}, dimensions={0}, use_global_device_ids=true | all-gather | bytes 544 | tf_op jit(solution)/shard_map/all_gather | solution.py:43
  1138.9 17.7 all-gather.40.cloned.1.call-done
  1291.0 26.9 %all-reduce.41.cloned.1.call-done = (f32[1024,1024]{1,0:T(8,128)}, f32[128,1024]{1,0:T(8,128)}) async-done(((f32[1024,1024]{1,0:T(8,128)}, f32[128,1024]{1,0:T(8,128)}), (f32[1024,1024]{1,0:T(8,128)}, f32[128,1024]{1,0:T(8,128)})) %all-reduce.41.cloned.1.call-update) | async-done | bytes 4718608 | tf_op jit(solution)/shard_map/psum | solution.py:131
  1319.4 78.4 %all-reduce.21 = (f32[1024]{0:T(1024)S(1)}, f32[1024]{0:T(1024)S(1)}, f32[1024]{0:T(1024)S(1)}, f32[16]{0:T(128)}, f32[16]{0:T(128)}, /*index=5*/f32[16]{0:T(128...) all-reduce(f32[1024]{0:T(1024)S(1)} %get-tuple-element.233, ...), channel_id=4, replica_groups=mesh['seq'=16,'mp'=2] {'seq'}, use_global_device_ids=true, to_apply=%region_37.38.clone | all-reduce | flops 9264 | bytes 72064
  1409.5 73.8 %reduce-scatter.25.cloned.1.call-done = f32[64,512]{1,0:T(8,128)} async-done(((f32[1024,512]{1,0:T(8,128)}), f32[64,512]{1,0:T(8,128)}) %reduce-scatter.25.cloned.1.call-update) | async-done | bytes 131088 | tf_op jit(solution)/shard_map/reduce_scatter | solution.py:465
  1483.3 80.8 %reduce-scatter.23.cloned.1.call-done = f32[64,512]{1,0:T(8,128)} async-done(((f32[1024,512]{1,0:T(8,128)}), f32[64,512]{1,0:T(8,128)}) %reduce-scatter.23.cloned.1.call-update) | async-done | bytes 131088 | tf_op jit(solution)/shard_map/reduce_scatter | solution.py:464
  1564.1 81.0 %reduce-scatter.29.cloned.1.call-done = f32[512,64]{0,1:T(8,128)} async-done(((f32[512,1024]{0,1:T(8,128)}), f32[512,64]{0,1:T(8,128)}) %reduce-scatter.29.cloned.1.call-update) | async-done | bytes 131088 | tf_op jit(solution)/shard_map/reduce_scatter | solution.py:467
  1645.1 94.8 %reduce-scatter.21.cloned.1.call-done = f32[1024,64]{0,1:T(8,128)} async-done(((f32[1024,1024]{0,1:T(8,128)}), f32[1024,64]{0,1:T(8,128)}) %reduce-scatter.21.cloned.1.call-update) | async-done | bytes 262160 | tf_op jit(solution)/shard_map/reduce_scatter | solution.py:462
  1739.8 97.6 %reduce-scatter.15.cloned.1.call-done = f32[64,1024]{1,0:T(8,128)} async-done(((f32[1024,1024]{1,0:T(8,128)}), f32[64,1024]{1,0:T(8,128)}) %reduce-scatter.15.cloned.1.call-update) | async-done | bytes 262160 | tf_op jit(solution)/shard_map/reduce_scatter | solution.py:458
  1837.4 180.2 %reduce-scatter.31.cloned.1.call-done = f32[64,2048]{1,0:T(8,128)} async-done(((f32[1024,2048]{1,0:T(8,128)}), f32[64,2048]{1,0:T(8,128)}) %reduce-scatter.31.cloned.1.call-update) | async-done | bytes 524304 | tf_op jit(solution)/shard_map/reduce_scatter | solution.py:469
  2017.6 183.0 %reduce-scatter.33.cloned.1.call-done = f32[64,2048]{1,0:T(8,128)} async-done(((f32[1024,2048]{1,0:T(8,128)}), f32[64,2048]{1,0:T(8,128)}) %reduce-scatter.33.cloned.1.call-update) | async-done | bytes 524304 | tf_op jit(solution)/shard_map/reduce_scatter | solution.py:470
  2200.6 183.1 %reduce-scatter.35.cloned.1.call-done = f32[2048,64]{0,1:T(8,128)} async-done(((f32[2048,1024]{0,1:T(8,128)}), f32[2048,64]{0,1:T(8,128)}) %reduce-scatter.35.cloned.1.call-update) | async-done | bytes 524304 | tf_op jit(solution)/shard_map/reduce_scatter | solution.py:471
  2383.7 83.1 %reduce-scatter.19.cloned.1.call-done = f32[64,256]{1,0:T(8,128)} async-done(((f32[1024,256]{1,0:T(8,128)}), f32[64,256]{1,0:T(8,128)}) %reduce-scatter.19.cloned.1.call-update) | async-done | bytes 65552 | tf_op jit(solution)/shard_map/reduce_scatter | solution.py:460
  2466.9 94.3 %reduce-scatter.17.cloned.1.call-done = f32[64,1024]{1,0:T(8,128)} async-done(((f32[1024,1024]{1,0:T(8,128)}), f32[64,1024]{1,0:T(8,128)}) %reduce-scatter.17.cloned.1.call-update) | async-done | bytes 262160 | tf_op jit(solution)/shard_map/reduce_scatter | solution.py:459
  (556 shorter events, 456.4 us)
Async XLA Ops:
  7.2 137.8 %all-gather.18.cloned.1.call-start = ((), (), s32[]{:S(2)}) async-start(), calls=%async_computation.12 | async-start | bytes 2228224 | tf_op jit(solution)/shard_map/all_gather | solution.py:139
  8.9 256.3 %all-gather.38.cloned.1.call-start = ((), (), s32[]{:S(2)}) async-start(), calls=%async_computation.38 | async-start | bytes 8912896 | tf_op jit(solution)/shard_map/all_gather | solution.py:23
  147.2 2.7 collective-permute-start
  153.8 173.7 %all-gather.20.cloned.1.call-start = ((), (), s32[]{:S(2)}) async-start(), calls=%async_computation.13 | async-start | bytes 2228224 | tf_op jit(solution)/shard_map/all_gather | solution.py:138
  154.6 235.5 %all-gather.22.cloned.1.call-start = ((), (), s32[]{:S(2)}) async-start(), calls=%async_computation.14 | async-start | bytes 2228224 | tf_op jit(solution)/shard_map/all_gather | solution.py:142
  156.3 254.6 %all-reduce.31.cloned.1.call-start = ((), (), s32[]{:S(2)}) async-start(), calls=%async_computation.15 | async-start | bytes 1048576 | tf_op jit(solution)/shard_map/psum | solution.py:131
  393.3 77.6 %all-gather.26.cloned.1.call-start = ((), (), s32[]{:S(2)}) async-start(), calls=%async_computation.17 | async-start | bytes 1114112 | tf_op jit(solution)/shard_map/all_gather | solution.py:144
  394.0 134.7 %all-gather.28.cloned.1.call-start = ((), (), s32[]{:S(2)}) async-start(), calls=%async_computation.18 | async-start | bytes 1114112 | tf_op jit(solution)/shard_map/all_gather | solution.py:145
  394.8 191.7 %all-gather.24.cloned.1.call-start = ((), (), s32[]{:S(2)}) async-start(), calls=%async_computation.16 | async-start | bytes 1114112 | tf_op jit(solution)/shard_map/all_gather | solution.py:146
  395.6 248.8 %all-gather.30.cloned.1.call-start = ((), (), s32[]{:S(2)}) async-start(), calls=%async_computation.19 | async-start | bytes 1114112 | tf_op jit(solution)/shard_map/all_gather | solution.py:147
  397.2 279.4 %all-reduce.33.cloned.1.call-start = ((), (), s32[]{:S(2)}) async-start(), calls=%async_computation.20 | async-start | bytes 8388608 | tf_op jit(solution)/shard_map/psum | solution.py:131
  649.2 108.0 %all-gather.32.cloned.1.call-start = ((), (), s32[]{:S(2)}) async-start(), calls=%async_computation.21 | async-start | bytes 4456448 | tf_op jit(solution)/shard_map/all_gather | solution.py:149
  651.1 184.1 %all-gather.34.cloned.1.call-start = ((), (), s32[]{:S(2)}) async-start(), calls=%async_computation.22 | async-start | bytes 4456448 | tf_op jit(solution)/shard_map/all_gather | solution.py:150
  652.9 260.3 %all-gather.36.cloned.1.call-start = ((), (), s32[]{:S(2)}) async-start(), calls=%async_computation.23 | async-start | bytes 4456448 | tf_op jit(solution)/shard_map/all_gather | solution.py:151
  654.8 315.6 %all-reduce.35.cloned.1.call-start = ((), (), s32[]{:S(2)}) async-start(), calls=%async_computation.24 | async-start | bytes 8388608 | tf_op jit(solution)/shard_map/psum | solution.py:131
  943.2 117.6 %all-reduce.37.cloned.1.call-start = ((), (), s32[]{:S(2)}) async-start(), calls=%async_computation.25 | async-start | bytes 8388608 | tf_op jit(solution)/shard_map/psum | solution.py:131
  1031.1 125.6 %all-gather.40.cloned.1.call-start = ((), (), s32[]{:S(2)}) async-start(), calls=%async_computation.39 | async-start | bytes 4456448 | tf_op jit(solution)/shard_map/all_gather | solution.py:43
  1079.6 127.5 %all-reduce.39.cloned.1.call-start = ((), (), s32[]{:S(2)}) async-start(), calls=%async_computation.26 | async-start | bytes 139264 | tf_op jit(solution)/shard_map/psum | solution.py:425
  1193.2 96.5 %reduce-scatter.37.cloned.1.call-start = ((), (), s32[]{:S(2)}) async-start(), calls=%async_computation.40 | async-start | bytes 557056
  1207.9 5.7 collective-permute-start.1
  1210.3 107.6 %all-reduce.41.cloned.1.call-start = ((), (), s32[]{:S(2)}) async-start(), calls=%async_computation.41 | async-start | bytes 9437184 | tf_op jit(solution)/shard_map/psum | solution.py:131
  1218.1 191.5 %reduce-scatter.27.cloned.1.call-start = ((), (), s32[]{:S(2)}) async-start(), calls=%async_computation.33 | async-start | bytes 2228224 | tf_op jit(solution)/shard_map/reduce_scatter | solution.py:466
  1222.2 261.1 %reduce-scatter.25.cloned.1.call-start = ((), (), s32[]{:S(2)}) async-start(), calls=%async_computation.32 | async-start | bytes 2228224 | tf_op jit(solution)/shard_map/reduce_scatter | solution.py:465
  1226.2 337.9 %reduce-scatter.23.cloned.1.call-start = ((), (), s32[]{:S(2)}) async-start(), calls=%async_computation.31 | async-start | bytes 2228224 | tf_op jit(solution)/shard_map/reduce_scatter | solution.py:464
  1230.4 414.7 %reduce-scatter.29.cloned.1.call-start = ((), (), s32[]{:S(2)}) async-start(), calls=%async_computation.34 | async-start | bytes 2228224 | tf_op jit(solution)/shard_map/reduce_scatter | solution.py:467
  1235.8 504.0 %reduce-scatter.21.cloned.1.call-start = ((), (), s32[]{:S(2)}) async-start(), calls=%async_computation.30 | async-start | bytes 4456448 | tf_op jit(solution)/shard_map/reduce_scatter | solution.py:462
  1238.7 598.7 %reduce-scatter.15.cloned.1.call-start = ((), (), s32[]{:S(2)}) async-start(), calls=%async_computation.27 | async-start | bytes 4456448 | tf_op jit(solution)/shard_map/reduce_scatter | solution.py:458
  1241.5 776.1 %reduce-scatter.31.cloned.1.call-start = ((), (), s32[]{:S(2)}) async-start(), calls=%async_computation.35 | async-start | bytes 8912896 | tf_op jit(solution)/shard_map/reduce_scatter | solution.py:469
  1252.3 948.3 %reduce-scatter.33.cloned.1.call-start = ((), (), s32[]{:S(2)}) async-start(), calls=%async_computation.36 | async-start | bytes 8912896 | tf_op jit(solution)/shard_map/reduce_scatter | solution.py:470
  1262.8 1120.9 %reduce-scatter.35.cloned.1.call-start = ((), (), s32[]{:S(2)}) async-start(), calls=%async_computation.37 | async-start | bytes 8912896 | tf_op jit(solution)/shard_map/reduce_scatter | solution.py:471
  1273.5 1193.4 %reduce-scatter.19.cloned.1.call-start = ((), (), s32[]{:S(2)}) async-start(), calls=%async_computation.29 | async-start | bytes 1114112 | tf_op jit(solution)/shard_map/reduce_scatter | solution.py:460
  1275.8 1285.4 %reduce-scatter.17.cloned.1.call-start = ((), (), s32[]{:S(2)}) async-start(), calls=%async_computation.28 | async-start | bytes 4456448 | tf_op jit(solution)/shard_map/reduce_scatter | solution.py:459
  (121 other events, 6046.9 us)
Sparse Core Ops, SparseCore 0:
  11.4 63.8 all-gather.17
  153.9 111.2 all-gather.37
  268.6 58.8 all-gather.19
  330.7 59.3 all-gather.21
  393.4 17.3 all-reduce.30
  414.4 56.4 all-gather.25
  474.6 54.0 all-gather.27
  532.4 54.0 all-gather.23
  590.3 54.0 all-gather.29
  649.4 27.1 all-reduce.32
  680.0 77.2 all-gather.31
  760.4 74.6 all-gather.33
  838.5 74.6 all-gather.35
  943.3 27.0 all-reduce.34
  1031.2 29.5 all-reduce.36
  1079.7 76.9 all-gather.39
  1193.3 13.6 all-reduce.38
  1210.5 79.1 reduce-scatter.36
  1292.3 25.5 all-reduce.40
  1320.6 81.7 reduce-scatter.26
  1405.3 77.9 reduce-scatter.24
  1486.2 77.8 reduce-scatter.22
  1567.0 78.0 reduce-scatter.28
  1647.8 91.9 reduce-scatter.20
  1742.7 94.6 reduce-scatter.14
  1840.1 177.4 reduce-scatter.30
  2020.3 180.2 reduce-scatter.32
  2203.5 180.2 reduce-scatter.34
  2386.6 80.2 reduce-scatter.18
  2469.7 91.4 reduce-scatter.16
where the time goes:
time: 2580 us; the launch traced here: 2570 us
  waiting for transfers between devices  1870 us (72%)
  blocking collectives  287 us (11%)
  matrix products  197 us (8%)
  other arithmetic  123 us (5%)
  local copies, waits for them, and re-layouts  67.5 us (3%)
    reduce_scatter x1, waiting for transfers between devices, local(): lax.psum_scatter(w_down_grad, 'seq', scatter_dimension=1, tiled=True)  183 us
    reduce_scatter x1, waiting for transfers between devices, local(): lax.psum_scatter(w_up_grad, 'seq', scatter_dimension=0, tiled=True)  183 us
    reduce_scatter x1, waiting for transfers between devices, local(): lax.psum_scatter(w_gate_grad, 'seq', scatter_dimension=0, tiled=True)  180 us
    unnamed x2, blocking collectives  123 us
    psum x5, waiting for transfers between devices, head_total(): return lax.psum(values, 'mp')  118 us
    reduce_scatter x1, waiting for transfers between devices, local(): lax.psum_scatter(w_z_grad, 'seq', scatter_dimension=0, tiled=True)  97.6 us
    reduce_scatter x1, waiting for transfers between devices, local(): lax.psum_scatter(w_out_grad, 'seq', scatter_dimension=1, tiled=True)  94.8 us
    reduce_scatter x1, waiting for transfers between devices, local(): lax.psum_scatter(w_x_grad, 'seq', scatter_dimension=0, tiled=True)  94.3 us
  transfers between devices with their start and end apart: 32, of which 30 were waited for; matrix products, arithmetic and copies ran while one was open for 9% of the time, Pallas kernels for 0%

commit v1 on v0

v1 whole, which is shorter than its diff:
```python
import functools

import jax
import jax.numpy as jnp
from jax import lax
from jax.sharding import PartitionSpec as P

LHD = 64
PATCH = 8
EPS = 1e-05
BIG = 1e30
PRECISE = lax.Precision.HIGHEST
BF = jnp.bfloat16
F32 = jnp.float32


def factors(count):
    root = 1
    while (root * 2) ** 3 <= count:
        root *= 2
    rest = count // root
    middle = root if rest % root == 0 and rest // root >= root else 1
    return (rest // middle, middle, root)


class Grid:
    def __init__(self, count):
        self.count = count
        self.sizes = factors(count)
        self.place = lax.axis_index("seq")
        n0, n1, n2 = self.sizes
        self.coord = (self.place // (n1 * n2), (self.place // n2) % n1, self.place % n2)

    def pairs(self, dim, by):
        n0, n1, n2 = self.sizes
        out = []
        for i in range(self.count):
            c = [i // (n1 * n2), (i // n2) % n1, i % n2]
            c[dim] = (c[dim] + by) % self.sizes[dim]
            out.append((i, (c[0] * n1 + c[1]) * n2 + c[2]))
        return out

    def shift(self, value, dim, by=1):
        return lax.ppermute(value, "seq", self.pairs(dim, by))


def spread(grid, block, dim):
    n = grid.sizes[dim]
    if n == 1:
        return block[None]
    got = [block]
    for _ in range(1, n):
        got.append(grid.shift(got[-1], dim))
    ring = jnp.stack(got[::-1] + got[:0:-1])
    return lax.dynamic_slice_in_dim(ring, n - 1 - grid.coord[dim], n, 0)


def gather_rows(grid, block, route, after=None):
    rows, width = block.shape
    if after is not None:
        block = lax.optimization_barrier((block, after))[0]
    mark = None
    for step, dim in enumerate(route):
        block = spread(grid, block, dim)
        if step == 1:
            mark = block
    order = list(reversed(route))
    block = jnp.transpose(block, [order.index(d) for d in range(3)] + [3, 4])
    return block.reshape(grid.count * rows, width), mark


def fold(grid, total, axis, dim):
    n = grid.sizes[dim]
    me = grid.coord[dim]

    def pick(k):
        return lax.dynamic_index_in_dim(total, (me + k) % n, axis, False)

    if n == 1:
        return pick(0)
    moving = pick(-1)
    for t in range(1, n):
        moving = grid.shift(moving, dim)
        moving = (moving.astype(F32) + pick(-1 - t).astype(F32)).astype(BF)
    return moving


def scatter_rows(grid, partial, route):
    n = partial.shape[1]
    rows = partial.shape[0] // grid.count
    left = [0, 1, 2]
    total = partial.astype(BF).reshape(grid.sizes + (rows, n))
    for dim in route:
        axis = left.index(dim)
        total = fold(grid, total, axis, dim)
        left.remove(dim)
    return total.astype(F32)


def swap_mp(value):
    size = lax.axis_size("mp")
    return lax.ppermute(value, "mp", [(i, (i + 1) % size) for i in range(size)])


def mp_sum(value):
    low = value.astype(BF)
    return low.astype(F32) + swap_mp(low).astype(F32)


def mp_sum_exact(value):
    return value + swap_mp(value)


def seq_sum(value):
    count = lax.axis_size("seq")
    by = 1
    while by < count:
        value = value + lax.ppermute(value, "seq", [(i, i ^ by) for i in range(count)])
        by *= 2
    return value


def combine(earlier, later):
    return (earlier[0] * later[0], later[0][:, None, None] * earlier[1] + later[1])


def pick_pair(flag, a, b):
    return jax.tree.map(lambda x, y: jnp.where(flag, x, y), a, b)


def scan_states(grid, decay, state, reverse):
    heads = decay.shape[0]
    shape = state.shape
    one = (jnp.ones_like(decay), jnp.zeros_like(state))

    def pack(pair):
        flat = pair[1].reshape(heads * shape[1], shape[2])
        tail = jnp.broadcast_to(pair[0][:, None], (heads, shape[2]))
        return jnp.concatenate([flat, tail], axis=0).astype(BF)

    def unpack(low):
        wide = low.astype(F32)
        return (wide[heads * shape[1] :, 0], wide[: heads * shape[1]].reshape(shape))

    total = (decay, state)
    enter = one
    dims = [d for d in (2, 1, 0) if grid.sizes[d] > 1]
    for dim in dims:
        n = grid.sizes[dim]
        me = grid.coord[dim]
        me = (n - 1 - me) if reverse else me
        moving = pack(total)
        before, after = one, one
        got = []
        for k in range(1, n):
            moving = grid.shift(moving, dim, -1 if reverse else 1)
            got.append(unpack(moving))
            enter_new = combine(got[-1], enter)
            enter = pick_pair(me >= k, enter_new, enter)
        if dim == dims[-1]:
            break
        own = unpack(pack(total))
        before = one
        for k in range(1, n):
            before = combine(pick_pair(me >= k, got[k - 1], one), before)
        after = one
        for k in range(n - 1, 0, -1):
            after = combine(after, pick_pair(me < k, got[k - 1], one))
        total = combine(before, combine(own, after))
    return enter


def bf_dot(left, right):
    return jnp.dot(left, right, preferred_element_type=F32)


def dot_t(left, right):
    return lax.dot_general(left, right, (((1,), (1,)), ((), ())), preferred_element_type=F32)


def grad_dot(left, right):
    return lax.dot_general(left, right, (((0,), (0,)), ((), ())), preferred_element_type=F32)


def rms_rows(values):
    return lax.rsqrt(jnp.mean(values * values, axis=-1, keepdims=True) + EPS)


def norm_back(grad_in, values, rstd_rows, gain_row):
    normed_rows = values * rstd_rows
    gain_grad = jnp.sum(grad_in * normed_rows, axis=0)
    scaled = grad_in * gain_row[None, :]
    input_grad = rstd_rows * (
        scaled - normed_rows * jnp.mean(scaled * normed_rows, axis=-1, keepdims=True)
    )
    return (input_grad, gain_grad)


def softplus_fn(values):
    return jnp.log1p(jnp.exp(-jnp.abs(values))) + jnp.maximum(values, 0.0)


def conv_taps(extended, ids_ext, kernel):
    conv_width = kernel.shape[0]
    row_count = extended.shape[0] - conv_width + 1
    target = ids_ext[conv_width - 1 :]
    summed = jnp.zeros((row_count, extended.shape[1]), F32)
    for tap_index in range(conv_width):
        same_seg = (ids_ext[tap_index : tap_index + row_count] == target).astype(F32)
        summed = (
            summed
            + extended[tap_index : tap_index + row_count]
            * kernel[tap_index][None, :]
            * same_seg[:, None]
        )
    return summed


def running_sum(values):
    length = values.shape[0]
    row = lax.broadcasted_iota(jnp.int32, (length, length), 0)
    col = lax.broadcasted_iota(jnp.int32, (length, length), 1)
    lower = (row >= col).astype(F32)
    return jnp.dot(lower, values, precision=PRECISE, preferred_element_type=F32)


def ssd_block(x_heads, b_rows, c_rows, step_size, log_decay, seg_rows, prev_seg, d_skip):
    length = x_heads.shape[0]
    cum_decay = running_sum(log_decay)
    cum_heads = cum_decay.T
    same_seg = seg_rows[:, None] == seg_rows[None, :]
    row_pos = lax.broadcasted_iota(jnp.int32, (length, length), 0)
    col_pos = lax.broadcasted_iota(jnp.int32, (length, length), 1)
    live_mask = same_seg & (row_pos >= col_pos)
    decay_gaps = cum_heads[:, :, None] - cum_heads[:, None, :]
    decay_mat = jnp.exp(jnp.where(live_mask[None], decay_gaps, -BIG))
    inner_prod = jnp.dot(c_rows, b_rows.T, precision=PRECISE, preferred_element_type=F32)
    mix_mat = inner_prod[None] * decay_mat * step_size.T[:, None, :]
    y_local = (
        jnp.einsum("hts,shp->thp", mix_mat, x_heads, precision=PRECISE)
        + d_skip[None, :, None] * x_heads
    )
    carried = (seg_rows == prev_seg).astype(F32)
    decay_in = carried[:, None] * jnp.exp(cum_decay)
    end_same = seg_rows == seg_rows[length - 1]
    end_gap = cum_decay[length - 1][None, :] - cum_decay
    tail_w = jnp.exp(jnp.where(end_same[:, None], end_gap, -BIG)) * step_size
    state_local = jnp.einsum("shp,sn->hpn", x_heads * tail_w[:, :, None], b_rows, precision=PRECISE)
    return (y_local, decay_in, state_local, decay_in[length - 1])


def soft_scores(queries, key_rows, shape_four):
    scale = LHD ** (-0.5)
    scores = (
        jnp.einsum(
            "bqhd,bkhd->bhqk",
            queries.reshape(shape_four),
            key_rows.reshape(shape_four),
            preferred_element_type=F32,
        )
        * scale
    )
    row_pos = lax.broadcasted_iota(jnp.int32, (PATCH, PATCH), 0)
    col_pos = lax.broadcasted_iota(jnp.int32, (PATCH, PATCH), 1)
    masked = jnp.where((row_pos >= col_pos)[None, None], scores, -BIG)
    row_max = jnp.max(masked, axis=-1, keepdims=True)
    exp_scores = jnp.exp(masked - row_max)
    return exp_scores / jnp.sum(exp_scores, axis=-1, keepdims=True)


def local(
    seq_count,
    bytes_in,
    out_grad,
    seq_ids,
    norm_gain,
    w_z,
    w_x,
    w_bc,
    w_dt,
    w_out,
    attn_gain,
    w_q,
    w_k,
    w_v,
    w_o,
    mlp_gain,
    w_gate,
    w_up,
    w_down,
    dt_bias,
    a_log,
    d_skip,
    conv_x,
    conv_bc,
    inner_gain,
):
    grid = Grid(seq_count)
    via_b, via_e, via_c, via_d = (1, 0, 2), (2, 0, 1), (0, 2, 1), (0, 1, 2)
    rows = w_z.shape[0]
    dt_width = w_dt.shape[1]
    side = jnp.concatenate(
        [
            w_bc.astype(BF),
            w_dt.astype(BF),
            norm_gain.astype(BF)[:, None],
            attn_gain.astype(BF)[:, None],
            mlp_gain.astype(BF)[:, None],
            jnp.zeros((rows, 128 - dt_width - 3), BF),
        ],
        axis=1,
    )
    bc_width = w_bc.shape[1]
    side_all, mark_s = gather_rows(grid, side, via_b)
    x_all, mark_x = gather_rows(grid, w_x.astype(BF), via_c)
    z_all, mark_z = gather_rows(grid, w_z.astype(BF), via_b, mark_x)
    out_all, mark_o = gather_rows(grid, w_out.T.astype(BF), via_e, mark_x)
    qkv = jnp.concatenate([w_q.astype(BF), w_k.astype(BF), w_v.astype(BF)], axis=1)
    qkv_all, mark_q = gather_rows(grid, qkv, via_d, mark_z)
    wo_all, mark_w = gather_rows(grid, w_o.T.astype(BF), via_b, mark_o)
    down_all, mark_d = gather_rows(grid, w_down.T.astype(BF), via_e, mark_q)
    gate_all, mark_g = gather_rows(grid, w_gate.astype(BF), via_b, mark_d)
    up_all, _ = gather_rows(grid, w_up.astype(BF), via_c, mark_g)

    bc_w = side_all[:, :bc_width]
    tail_w = side_all[:, bc_width:]
    dt_w = tail_w[:, :dt_width]
    gains = tail_w[:, dt_width : dt_width + 3].astype(F32).T
    norm_row, attn_row, mlp_row = gains[0], gains[1], gains[2]

    byte_rows = bytes_in.shape[0]
    patch_rows = byte_rows // PATCH
    model_width = bytes_in.shape[1]
    x_float = bytes_in.astype(F32)
    patch_in = jnp.mean(x_float.reshape(patch_rows, PATCH, model_width), axis=1)
    rstd_patch = rms_rows(patch_in)
    h_norm = (patch_in * rstd_patch * norm_row[None, :]).astype(BF)
    inner_local = w_x.shape[1]
    mixed_in = jnp.concatenate([bf_dot(h_norm, x_all), bf_dot(h_norm, bc_w)], axis=1).astype(BF)
    dt_raw = bf_dot(h_norm, dt_w)
    conv_width = conv_x.shape[0]
    state_size = conv_bc.shape[1] // 2
    rim_rows = lax.ppermute(
        mixed_in[patch_rows - (conv_width - 1) :], "seq", [(i, i + 1) for i in range(seq_count - 1)]
    )
    gate_z = bf_dot(h_norm, z_all)
    extended = jnp.concatenate([rim_rows, mixed_in], axis=0).astype(F32)
    first_row = lax.axis_index("seq") * patch_rows
    ids_padded = jnp.concatenate([jnp.full((conv_width - 1,), -1, jnp.int32), seq_ids])
    ids_ext = lax.dynamic_slice_in_dim(ids_padded, first_row, patch_rows + conv_width - 1)
    seg_rows = ids_ext[conv_width - 1 :]
    prev_seg = ids_ext[conv_width - 2]
    head_count = a_log.shape[0]
    head_size = inner_local // head_count

    def mixer_core(ext_in, raw_in, kernel_x, kernel_bc, bias_in, rate_in, skip_in):
        kernel = jnp.concatenate([kernel_x, kernel_bc], axis=1)
        activated = jax.nn.silu(conv_taps(ext_in, ids_ext, kernel))
        x_heads = activated[:, :inner_local].reshape(patch_rows, head_count, head_size)
        b_rows = activated[:, inner_local : inner_local + state_size]
        c_rows = activated[:, inner_local + state_size :]
        step_size = softplus_fn(raw_in + bias_in[None, :])
        log_decay = -step_size * jnp.exp(rate_in)[None, :]
        y_local, decay_in, state_local, total_decay = ssd_block(
            x_heads, b_rows, c_rows, step_size, log_decay, seg_rows, prev_seg, skip_in
        )
        return (y_local, c_rows, decay_in, state_local, total_decay)

    core_out, core_back = jax.vjp(
        mixer_core, extended, dt_raw, conv_x, conv_bc, dt_bias, a_log, d_skip
    )
    y_local, c_rows, decay_in, state_local, total_decay = core_out
    state_in = scan_states(grid, total_decay, state_local, False)[1]

    def finish_mix(y_part, c_part, decay_part, state_part, z_part):
        y_full = y_part + decay_part[:, :, None] * jnp.einsum(
            "tn,hpn->thp", c_part, state_part, precision=PRECISE
        )
        return y_full.reshape(patch_rows, inner_local) * jax.nn.silu(z_part)

    gated_out, finish_back = jax.vjp(finish_mix, y_local, c_rows, decay_in, state_in, gate_z)
    square_sum = mp_sum_exact(jnp.sum(gated_out * gated_out, axis=-1))
    inner_full = inner_local * lax.axis_size("mp")
    rstd_inner = lax.rsqrt(square_sum / inner_full + EPS)[:, None]
    y_norm = (gated_out * rstd_inner * inner_gain[None, :]).astype(BF)
    mixer_out = mp_sum(dot_t(y_norm, out_all))
    patch_out = patch_in + mixer_out
    rows_in = x_float + jnp.repeat(patch_out, PATCH, axis=0)
    rstd_attn = rms_rows(rows_in)
    normed = (rows_in * rstd_attn * attn_row[None, :]).astype(BF)
    attn_width = w_q.shape[1]
    qkv_rows = bf_dot(normed, qkv_all).astype(BF)
    queries = qkv_rows[:, :attn_width]
    key_rows = qkv_rows[:, attn_width : 2 * attn_width]
    value_rows = qkv_rows[:, 2 * attn_width :]
    shape_four = (patch_rows, PATCH, attn_width // LHD, LHD)
    soft_weights = soft_scores(queries, key_rows, shape_four)
    soft_low = soft_weights.astype(BF)
    attended = (
        jnp.einsum(
            "bhqk,bkhd->bqhd",
            soft_low,
            value_rows.reshape(shape_four),
            preferred_element_type=F32,
        )
        .astype(BF)
        .reshape(byte_rows, attn_width)
    )
    after_attn = rows_in + mp_sum(dot_t(attended, wo_all))
    rstd_mlp = rms_rows(after_attn)
    normed_mlp = (after_attn * rstd_mlp * mlp_row[None, :]).astype(BF)
    gate_val = bf_dot(normed_mlp, gate_all)
    up_val = bf_dot(normed_mlp, up_all)
    hidden = (jax.nn.silu(gate_val) * up_val).astype(BF)
    block_out = after_attn + mp_sum(dot_t(hidden, down_all))
    grad_float = out_grad.astype(F32)

    hidden_grad = bf_dot(out_grad, down_all)
    sigmoid_gate = jax.nn.sigmoid(gate_val)
    gate_grad = (
        hidden_grad * up_val * sigmoid_gate * (1.0 + gate_val * (1.0 - sigmoid_gate))
    ).astype(BF)
    up_grad = (hidden_grad * gate_val * sigmoid_gate).astype(BF)
    down_part = grad_dot(out_grad, hidden).astype(BF)
    gate_part = grad_dot(normed_mlp, gate_grad).astype(BF)
    up_part = grad_dot(normed_mlp, up_grad).astype(BF)
    w_down_grad = scatter_rows(grid, down_part, via_e[::-1]).T
    w_gate_grad = scatter_rows(grid, gate_part, via_b[::-1])
    w_up_grad = scatter_rows(grid, up_part, via_c[::-1])
    mlp_norm_grad = mp_sum(dot_t(gate_grad, gate_all) + dot_t(up_grad, up_all))
    mlp_in_grad, mlp_gain_grad = norm_back(mlp_norm_grad, after_attn, rstd_mlp, mlp_row)
    after_grad = grad_float + mlp_in_grad
    after_low = after_grad.astype(BF)
    wo_part = grad_dot(after_low, attended).astype(BF)
    w_o_grad = scatter_rows(grid, wo_part, via_b[::-1]).T
    attended_grad = bf_dot(after_low, wo_all).astype(BF)
    grad_four = attended_grad.reshape(shape_four)
    scale = LHD ** (-0.5)
    prob_grad = jnp.einsum(
        "bqhd,bkhd->bhqk",
        grad_four,
        value_rows.reshape(shape_four),
        preferred_element_type=F32,
    )
    score_grad = (
        soft_weights * (prob_grad - jnp.sum(soft_weights * prob_grad, axis=-1, keepdims=True))
    ).astype(BF)
    query_grad = (
        jnp.einsum(
            "bhqk,bkhd->bqhd",
            score_grad,
            key_rows.reshape(shape_four),
            preferred_element_type=F32,
        )
        * scale
    ).astype(BF)
    key_grad = (
        jnp.einsum(
            "bhqk,bqhd->bkhd",
            score_grad,
            queries.reshape(shape_four),
            preferred_element_type=F32,
        )
        * scale
    ).astype(BF)
    value_grad = jnp.einsum(
        "bhqk,bqhd->bkhd", soft_low, grad_four, preferred_element_type=F32
    ).astype(BF)
    qkv_grad = jnp.concatenate(
        [g.reshape(byte_rows, attn_width) for g in (query_grad, key_grad, value_grad)], axis=1
    )
    qkv_part = grad_dot(normed, qkv_grad).astype(BF)
    w_qkv_grad = scatter_rows(grid, qkv_part, via_d[::-1])
    attn_norm_grad = mp_sum(dot_t(qkv_grad, qkv_all))
    attn_in_grad, attn_gain_grad = norm_back(attn_norm_grad, rows_in, rstd_attn, attn_row)
    rows_grad = after_grad + attn_in_grad
    patch_grad = jnp.sum(rows_grad.reshape(patch_rows, PATCH, model_width), axis=1)
    patch_low = patch_grad.astype(BF)
    out_part = grad_dot(patch_low, y_norm).astype(BF)
    w_out_grad = scatter_rows(grid, out_part, via_e[::-1]).T
    y_norm_grad = bf_dot(patch_low, out_all)
    inner_gain_grad = jnp.sum(y_norm_grad * gated_out * rstd_inner, axis=0)
    scaled = y_norm_grad * inner_gain[None, :]
    cross_sum = mp_sum_exact(jnp.sum(scaled * gated_out, axis=-1))
    gated_grad = rstd_inner * scaled - gated_out * rstd_inner**3 * (cross_sum[:, None] / inner_full)
    y_grad, c_grad, decay_grad, state_in_grad, z_grad = finish_back(gated_grad)
    z_low = z_grad.astype(BF)
    z_part = grad_dot(h_norm, z_low).astype(BF)
    w_z_grad = scatter_rows(grid, z_part, via_b[::-1])
    state_grad = scan_states(grid, total_decay, state_in_grad, True)[1]
    total_grad = jnp.sum(state_grad * state_in, axis=(1, 2))
    ext_grad, raw_grad, conv_x_grad, conv_bc_part, dt_bias_grad, a_log_grad, d_skip_grad = (
        core_back((y_grad, c_grad, decay_grad, state_grad, total_grad))
    )
    bc_total = mp_sum(ext_grad[:, inner_local:])
    conv_bc_grad = mp_sum_exact(conv_bc_part)
    ext_full = jnp.concatenate([ext_grad[:, :inner_local], bc_total], axis=1)
    rim_back = lax.ppermute(
        ext_full[: conv_width - 1], "seq", [(i + 1, i) for i in range(seq_count - 1)]
    )
    mixed_grad = ext_full[conv_width - 1 :] + jnp.concatenate(
        [jnp.zeros((patch_rows - (conv_width - 1), ext_full.shape[1]), F32), rim_back],
        axis=0,
    )
    mixed_low = mixed_grad.astype(BF)
    x_in_grad = mixed_low[:, :inner_local]
    bc_grad = mixed_low[:, inner_local:]
    raw_low = raw_grad.astype(BF)
    x_part = grad_dot(h_norm, x_in_grad).astype(BF)
    w_x_grad = scatter_rows(grid, x_part, via_c[::-1])
    h_own = (
        dot_t(z_low, z_all)
        + dot_t(x_in_grad, x_all)
        + dot_t(raw_low, dt_w)
    )
    h_grad = mp_sum(h_own) + dot_t(bc_grad, bc_w)
    patch_in_grad, norm_gain_grad = norm_back(h_grad, patch_in, rstd_patch, norm_row)
    patch_total = patch_grad + patch_in_grad
    bytes_grad = rows_grad + jnp.repeat(patch_total / PATCH, PATCH, axis=0)
    side_part = jnp.concatenate(
        [
            grad_dot(h_norm, bc_grad),
            grad_dot(h_norm, raw_low),
            norm_gain_grad[:, None],
            attn_gain_grad[:, None],
            mlp_gain_grad[:, None],
            jnp.zeros((model_width, 128 - dt_width - 3), F32),
        ],
        axis=1,
    ).astype(BF)
    side_sum = scatter_rows(grid, side_part, via_b[::-1])
    small = (dt_bias_grad, a_log_grad, d_skip_grad, conv_x_grad, conv_bc_grad, inner_gain_grad)
    flat = jnp.concatenate([s.reshape(-1) for s in small])
    pad = (-flat.shape[0]) % 1024
    flat = seq_sum(jnp.pad(flat, (0, pad)).reshape(-1, 128)).reshape(-1)
    parts = []
    start = 0
    for s in small:
        parts.append(flat[start : start + s.size].reshape(s.shape))
        start += s.size
    return (
        block_out,
        bytes_grad,
        side_sum[:, bc_width + dt_width],
        w_z_grad,
        w_x_grad,
        side_sum[:, :bc_width],
        side_sum[:, bc_width : bc_width + dt_width],
        w_out_grad,
        side_sum[:, bc_width + dt_width + 1],
        w_qkv_grad[:, :attn_width],
        w_qkv_grad[:, attn_width : 2 * attn_width],
        w_qkv_grad[:, 2 * attn_width :],
        w_o_grad,
        side_sum[:, bc_width + dt_width + 2],
        w_gate_grad,
        w_up_grad,
        w_down_grad,
        parts[0],
        parts[1],
        parts[2],
        parts[3],
        parts[4],
        parts[5],
    )


def solution(mesh):
    rows, cols, both, rest = P("seq", None), P("seq", "mp"), P("mp", "seq"), P()
    vec, per = P("seq"), P("mp")
    weights = (vec, cols, cols, rows, cols, both, vec, cols, cols, cols, both, vec, cols, cols, both)
    small = (per, per, per, P(None, "mp"), rest, per)
    in_specs = (rows, rows, rest) + weights + small
    out_specs = (rows, rows) + weights + small
    body = functools.partial(local, mesh.shape["seq"])
    return jax.shard_map(body, mesh=mesh, in_specs=in_specs, out_specs=out_specs, check_vma=False)
```

time: 2580 us -> 958 us (0.37)
  waiting for transfers between devices: 1870 us -> 369 us
  blocking collectives: 287 us -> 0 us
  local copies, waits for them, and re-layouts: 67.5 us -> 173 us
  starting transfers between devices: 4.94 us -> 103 us
  matrix products: 197 us -> 136 us
  other arithmetic: 123 us -> 160 us
    reduce_scatter x11 -> x0, waiting for transfers between devices: 1150 us -> none  [the longest x1 183 us: local(): lax.psum_scatter(w_down_grad, 'seq', scatter_dimension=1, tiled=True)]
    all_gather x12 -> x0, waiting for transfers between devices: 574 us -> none  [the longest x1 73.9 us: fetch_first(): lax.all_gather(lowered[12], 'seq', axis=0, tiled=True)]
    ppermute x2 -> x116, waiting for transfers between devices: 4.42 us -> 369 us  [the longest x100 365 us: shift(): return lax.ppermute(value, 'seq', self.pairs(dim, by))]
    all_gather x4 -> x0, blocking collectives: 156 us -> none  [the longest x1 41.2 us: carried_in(): lax.all_gather(a.astype(kind), axis)]
    psum x6 -> x0, waiting for transfers between devices: 131 us -> none  [the longest x5 118 us: head_total(): return lax.psum(values, 'mp')]
    unnamed x2 -> x0, blocking collectives: 123 us -> none
    ppermute x2 -> x116, starting transfers between devices: 2.61 us -> 103 us  [the longest x100 88.8 us: shift(): return lax.ppermute(value, 'seq', self.pairs(dim, by))]
    dot_general x38 -> x35, matrix products: 161 us -> 107 us  [the longest x10 40.6 us: dot_t(): lax.dot_general(left, right, (((1,), (1,)), ((), ())), preferred_element_...]
  transfers between devices with their start and end apart: 32 -> 116, of which waited for: 30 -> 54; matrix products, arithmetic and copies ran while one was open for 9% -> 43% of each run, Pallas kernels for 0% -> 0%
where the time goes in v1:
time: 958 us; the launch traced here: 946 us
  waiting for transfers between devices  369 us (39%)
  local copies, waits for them, and re-layouts  173 us (18%)
  other arithmetic  160 us (17%)
  matrix products  136 us (14%)
  starting transfers between devices  103 us (11%)
    ppermute x100, waiting for transfers between devices, shift(): return lax.ppermute(value, 'seq', self.pairs(dim, by))  365 us
    ppermute x100, starting transfers between devices, shift(): return lax.ppermute(value, 'seq', self.pairs(dim, by))  88.8 us
    unnamed x468, local copies, waits for them, and re-layouts  48.6 us
    dot_general x10, matrix products, dot_t(): lax.dot_general(left, right, (((1,), (1,)), ((), ())), preferred_element_...  40.6 us
    dot_general x10, matrix products, bf_dot(): return jnp.dot(left, right, preferred_element_type=F32)  40 us
    another operation x21, other arithmetic, spread(): ring = jnp.stack(got[::-1] + got[:0:-1])  34.2 us
    convert_element_type x36, other arithmetic, fold(): moving = (moving.astype(F32) + pick(-1 - t).astype(F32)).astype(BF)  32.6 us
    dot_general x10, matrix products, grad_dot(): lax.dot_general(left, right, (((0,), (0,)), ((), ())), preferred_element_...  24.2 us
  transfers between devices with their start and end apart: 116, of which 54 were waited for; matrix products, arithmetic and copies ran while one was open for 43% of the time, Pallas kernels for 0%

profile of v1, /device:TPU:0, one launch (start us, length us, event | category | flops | bytes accessed | tf_op | source)
XLA Modules:
  0.0 946.0 jit_solution(10038026926038867810)
XLA Ops:
  38.2 6.1 collective-permute-done.3
  53.3 6.3 collective-permute-done.4
  75.3 7.2 collective-permute-done.17
  121.4 12.7 %collective-permute-done.33 = bf16[64,512]{1,0:T(8,128)(2,1)S(1)} collective-permute-done((bf16[64,512]{1,0:T(8,128)(2,1)S(1)}, bf16[64,512]{1,0:T(8,128)(2,1)S(1)}, u32[]{:S(2)}, u32[]{:S(2)}) %collective-permute-start.33) | collective-permute-done | bytes 65568 | tf_op jit(solution)/shard_map/ppermute | solution.py:44
  150.3 8.6 collective-permute-done.35
  250.3 12.1 %collective-permute-done.41 = bf16[2,64,2048]{2,1,0:T(8,128)(2,1)S(1)} collective-permute-done((bf16[2,64,2048]{2,1,0:T(8,128)(2,1)}, bf16[2,64,2048]{2,1,0:T(8,128)(2,1)S(1)}, u32[]{:S(2)}, u32[]{:S(2)}) %collective-permute-start.41) | collective-permute-done | bytes 524320 | tf_op jit(solution)/shard_map/ppermute | solution.py:44
  263.1 14.3 %collective-permute-done.42 = bf16[2,64,2048]{2,1,0:T(8,128)(2,1)S(1)} collective-permute-done((bf16[2,64,2048]{2,1,0:T(8,128)(2,1)S(1)}, bf16[2,64,2048]{2,1,0:T(8,128)(2,1)S(1)}, u32[]{:S(2)}, u32[]{:S(2)}) %collective-permute-start.42) | collective-permute-done | bytes 524320 | tf_op jit(solution)/shard_map/ppermute | solution.py:44
  305.6 5.5 fusion.57
  315.0 6.7 fusion.299
  346.9 5.7 collective-permute-done.48
  356.3 5.6 collective-permute-done.49
  362.9 7.4 collective-permute-done.50
  372.2 8.8 collective-permute-done.53
  383.3 33.5 %collective-permute-done.51 = bf16[4,64,2048]{2,1,0:T(8,128)(2,1)S(1)} collective-permute-done((bf16[4,64,2048]{2,1,0:T(8,128)(2,1)S(1)}, bf16[4,64,2048]{2,1,0:T(8,128)(2,1)S(1)}, u32[]{:S(2)}, u32[]{:S(2)}) %collective-permute-start.51) | collective-permute-done | bytes 1048608 | tf_op jit(solution)/shard_map/ppermute | solution.py:44
  418.4 6.7 fusion.303
  428.5 6.8 fusion.300
  435.3 29.2 %collective-permute-done.52 = bf16[2,4,64,2048]{3,2,0,1:T(8,128)(2,1)S(1)} collective-permute-done((bf16[2,4,64,2048]{3,2,0,1:T(8,128)(2,1)S(1)}, bf16[2,4,64,2048]{3,2,0,1:T(8,128)(2,1)S(1)}, u32[]{:S(2)}, u32[]{:S(2)}) %collective-permute-start.52) | collective-permute-done | bytes 2097184 | tf_op jit(solution)/shard_map/ppermute | solution.py:44
  468.1 15.2 %fusion.3 = (bf16[1024,2048]{1,0:T(8,128)(2,1)}, bf16[1024,2048]{1,0:T(8,128)(2,1)}, bf16[1024,2048]{1,0:T(8,128)(2,1)}) fusion(f32[2048,1024]{0,1:T(8,128)} %fusion.303, f32[1024,2048]{1,0:T(8,128)} %fusion.300, bf16[1024,1024]{1,0:T(8,128)(2,1)S(1)} %multiply_convert_fusion.4, bf16[1024,2048]{1,0:T(8,128)(2,1)} %bitcast.656), kind=kOutput, calls=%fused_computation.5 | convolution fusion | flops 4328521728 | bytes 35651584 | tf_op jit(solution)/shard_map/dot_general | solution.py:174
  483.3 7.1 convolution_convert_fusion.6
  495.6 9.7 %fusion.301 = f32[1024,1024]{1,0:T(8,128)} fusion(bf16[1024,2048]{1,0:T(8,128)(2,1)} %get-tuple-element.238, bf16[1024,2048]{1,0:T(8,128)(2,1)S(1)} %bitcast.657), kind=kOutput, calls=%fused_computation.709 | convolution fusion | flops 4294967296 | bytes 12582912 | tf_op jit(solution)/shard_map/dot_general | solution.py:178
  505.3 7.8 add_convert_fusion
  587.5 20.4 %collective-permute-done.101 = bf16[4,2,64,2048]{3,2,0,1:T(8,128)(2,1)} collective-permute-done((bf16[4,2,64,2048]{3,2,0,1:T(8,128)(2,1)}, bf16[4,2,64,2048]{3,2,0,1:T(8,128)(2,1)}, u32[]{:S(2)}, u32[]{:S(2)}) %collective-permute-start.101) | collective-permute-done | bytes 2097184 | tf_op jit(solution)/shard_map/ppermute | solution.py:44
  622.8 26.4 %collective-permute-done.91 = bf16[4,2,64,512]{3,2,1,0:T(8,128)(2,1)S(1)} collective-permute-done((bf16[4,2,64,512]{3,2,1,0:T(8,128)(2,1)S(1)}, bf16[4,2,64,512]{3,2,1,0:T(8,128)(2,1)S(1)}, u32[]{:S(2)}, u32[]{:S(2)}) %collective-permute-start.91) | collective-permute-done | bytes 524320 | tf_op jit(solution)/shard_map/ppermute | solution.py:44
  661.4 8.8 collective-permute-done.93
  672.3 5.4 collective-permute-done.94
  682.8 11.6 %collective-permute-done.108 = bf16[2,64,2048]{2,1,0:T(8,128)(2,1)S(1)} collective-permute-done((bf16[2,64,2048]{2,1,0:T(8,128)(2,1)S(1)}, bf16[2,64,2048]{2,1,0:T(8,128)(2,1)S(1)}, u32[]{:S(2)}, u32[]{:S(2)}) %collective-permute-start.108) | collective-permute-done | bytes 524320 | tf_op jit(solution)/shard_map/ppermute | solution.py:44
  696.4 9.1 collective-permute-done.98
  705.8 16.6 %collective-permute-done.103 = bf16[64,2048]{1,0:T(8,128)(2,1)S(1)} collective-permute-done((bf16[64,2048]{1,0:T(8,128)(2,1)S(1)}, bf16[64,2048]{1,0:T(8,128)(2,1)S(1)}, u32[]{:S(2)}, u32[]{:S(2)}) %collective-permute-start.103) | collective-permute-done | bytes 262176 | tf_op jit(solution)/shard_map/ppermute | solution.py:44
  724.2 11.3 %collective-permute-done.104 = bf16[64,2048]{1,0:T(8,128)(2,1)S(1)} collective-permute-done((bf16[64,2048]{1,0:T(8,128)(2,1)S(1)}, bf16[64,2048]{1,0:T(8,128)(2,1)S(1)}, u32[]{:S(2)}, u32[]{:S(2)}) %collective-permute-start.104) | collective-permute-done | bytes 262176 | tf_op jit(solution)/shard_map/ppermute | solution.py:44
  750.0 5.7 bitcast_reduce_fusion
  817.1 8.5 collective-permute-done.71
  914.1 6.3 collective-permute-done.67
  (1081 shorter events, 588.0 us)
Async XLA Ops:
  2.5 22.5 %collective-permute-start.5 = (bf16[64,1024]{1,0:T(8,128)(2,1)}, bf16[64,1024]{1,0:T(8,128)(2,1)S(1)}, u32[]{:S(2)}, u32[]{:S(2)}) collective-permute-start(bf16[64,1024]{1,0:T(8,128)(2,1)} %convert_element_type.861), channel_id=1, source_target_pairs={{0,8},{2,10},{4,12},{6,14},{8,16},{10,18},{12,20},{14,22},{16,24},... | collective-permute-start | bytes 393224 | tf_op jit(solution)/shard_map/ppermute | solution.py:44
  107.5 104.9 %collective-permute-start.20 = (bf16[4,2,64,1024]{3,2,1,0:T(8,128)(2,1)}, bf16[4,2,64,1024]{3,2,1,0:T(8,128)(2,1)}, u32[]{:S(2)}, u32[]{:S(2)}) collective-permute-start(bf16[4,2,64,1024]{3,2,1,0:T(8,128)(2,1)} %constant_dynamic-slice_fusion.12), channel_id=1, source_target_pairs={{0,2},{2,0},{4,6},{6,4},{8,10},{10,8},{12,14},{14,12},{16,18},{18,... | collective-permute-start | bytes 3145736 | tf_op jit(solution)/shard_map/ppermute | solution.py:44
  108.9 37.5 %collective-permute-start.28 = (bf16[64,1536]{1,0:T(8,128)(2,1)}, bf16[64,1536]{1,0:T(8,128)(2,1)}, u32[]{:S(2)}, u32[]{:S(2)}) collective-permute-start(bf16[64,1536]{1,0:T(8,128)(2,1)} %pad_maximum_fusion.6), channel_id=1, source_target_pairs={{0,8},{2,10},{4,12},{6,14},{8,16},{10,18},{12,20},{14,22},{16,24},... | collective-permute-start | bytes 589832 | tf_op jit(solution)/shard_map/ppermute | solution.py:44
  112.9 124.8 %collective-permute-start.26 = (bf16[4,2,64,1024]{3,2,1,0:T(8,128)(2,1)}, bf16[4,2,64,1024]{3,2,1,0:T(8,128)(2,1)}, u32[]{:S(2)}, u32[]{:S(2)}) collective-permute-start(bf16[4,2,64,1024]{3,2,1,0:T(8,128)(2,1)} %constant_dynamic-slice_fusion.11), channel_id=1, source_target_pairs={{0,4},{2,6},{4,0},{6,2},{8,12},{10,14},{12,8},{14,10},{16,20},{18,... | collective-permute-start | bytes 3145736 | tf_op jit(solution)/shard_map/ppermute | solution.py:44
  179.7 30.2 %collective-permute-start.37 = (bf16[4,2,64,512]{3,2,1,0:T(8,128)(2,1)}, bf16[4,2,64,512]{3,2,1,0:T(8,128)(2,1)}, u32[]{:S(2)}, u32[]{:S(2)}) collective-permute-start(bf16[4,2,64,512]{3,2,1,0:T(8,128)(2,1)} %constant_dynamic-slice_fusion.9), channel_id=1, source_target_pairs={{0,2},{2,0},{4,6},{6,4},{8,10},{10,8},{12,14},{14,12},{16,18},{18,... | collective-permute-start | bytes 1572872 | tf_op jit(solution)/shard_map/ppermute | solution.py:44
  243.7 41.8 %collective-permute-start.32 = (bf16[2,4,64,1536]{3,2,0,1:T(8,128)(2,1)}, bf16[2,4,64,1536]{3,2,0,1:T(8,128)(2,1)S(1)}, u32[]{:S(2)}, u32[]{:S(2)}) collective-permute-start(bf16[2,4,64,1536]{3,2,0,1:T(8,128)(2,1)} %fusion.68), channel_id=1, source_target_pairs={{0,2},{2,0},{4,6},{6,4},{8,10},{10,8},{12,14},{14,12},{16,18},{18,... | collective-permute-start | bytes 4718600 | tf_op jit(solution)/shard_map/ppermute | solution.py:44
  333.0 48.0 %collective-permute-start.53 = (bf16[4,2,64,2048]{3,2,1,0:T(8,128)(2,1)S(1)}, bf16[4,2,64,2048]{3,2,1,0:T(8,128)(2,1)S(1)}, u32[]{:S(2)}, u32[]{:S(2)}) collective-permute-start(bf16[4,2,64,2048]{3,2,1,0:T(8,128)(2,1)S(1)} %copy-done.103), channel_id=1, source_target_pairs={{0,4},{2,6},{4,0},{6,2},{8,12},{10,14},{12,8},{14,10},{16,20},{18,... | collective-permute-start | bytes 6291464 | tf_op jit(solution)/shard_map/ppermute | solution.py:44
  346.9 79.4 %collective-permute-start.47 = (bf16[4,2,64,2048]{3,2,1,0:T(8,128)(2,1)S(1)}, bf16[4,2,64,2048]{3,2,1,0:T(8,128)(2,1)S(1)}, u32[]{:S(2)}, u32[]{:S(2)}) collective-permute-start(bf16[4,2,64,2048]{3,2,1,0:T(8,128)(2,1)S(1)} %constant_dynamic-slice_fusion.7), channel_id=1, source_target_pairs={{0,2},{2,0},{4,6},{6,4},{8,10},{10,8},{12,14},{14,12},{16,18},{18,... | collective-permute-start | bytes 6291464 | tf_op jit(solution)/shard_map/ppermute | solution.py:44
  370.6 46.2 %collective-permute-start.51 = (bf16[4,64,2048]{2,1,0:T(8,128)(2,1)S(1)}, bf16[4,64,2048]{2,1,0:T(8,128)(2,1)S(1)}, u32[]{:S(2)}, u32[]{:S(2)}) collective-permute-start(bf16[4,64,2048]{2,1,0:T(8,128)(2,1)S(1)} %constant_dynamic-slice_fusion.6), channel_id=1, source_target_pairs={{0,2},{2,0},{4,6},{6,4},{8,10},{10,8},{12,14},{14,12},{16,18},{18,... | collective-permute-start | bytes 3145736 | tf_op jit(solution)/shard_map/ppermute | solution.py:44
  417.9 46.6 %collective-permute-start.52 = (bf16[2,4,64,2048]{3,2,0,1:T(8,128)(2,1)S(1)}, bf16[2,4,64,2048]{3,2,0,1:T(8,128)(2,1)S(1)}, u32[]{:S(2)}, u32[]{:S(2)}) collective-permute-start(bf16[2,4,64,2048]{3,2,0,1:T(8,128)(2,1)S(1)} %fusion.37), channel_id=1, source_target_pairs={{0,4},{2,6},{4,0},{6,2},{8,12},{10,14},{12,8},{14,10},{16,20},{18,... | collective-permute-start | bytes 6291464 | tf_op jit(solution)/shard_map/ppermute | solution.py:44
  495.5 39.9 %collective-permute-start.54 = (bf16[1024,1024]{1,0:T(8,128)(2,1)S(1)}, bf16[1024,1024]{1,0:T(8,128)(2,1)S(1)}, u32[]{:S(2)}, u32[]{:S(2)}) collective-permute-start(bf16[1024,1024]{1,0:T(8,128)(2,1)S(1)} %convolution_convert_fusion.6), channel_id=1, source_target_pairs={{0,1},{1,0},{2,3},{3,2},{4,5},{5,4},{6,7},{7,6},{8,9},{9,8},{10,11... | collective-permute-start | bytes 6291464 | tf_op jit(solution)/shard_map/ppermute | solution.py:102
  514.7 67.6 %collective-permute-start.106 = (bf16[4,2,64,2048]{3,2,1,0:T(8,128)(2,1)}, bf16[4,2,64,2048]{3,2,1,0:T(8,128)(2,1)}, u32[]{:S(2)}, u32[]{:S(2)}) collective-permute-start(bf16[4,2,64,2048]{3,2,1,0:T(8,128)(2,1)} %dynamic-slice_bitcast_fusion), channel_id=1, source_target_pairs={{0,4},{2,6},{4,0},{6,2},{8,12},{10,14},{12,8},{14,10},{16,20},{18,... | collective-permute-start | bytes 6291464 | tf_op jit(solution)/shard_map/ppermute | solution.py:44
  524.4 83.5 %collective-permute-start.101 = (bf16[4,2,64,2048]{3,2,0,1:T(8,128)(2,1)}, bf16[4,2,64,2048]{3,2,0,1:T(8,128)(2,1)}, u32[]{:S(2)}, u32[]{:S(2)}) collective-permute-start(bf16[4,2,64,2048]{3,2,0,1:T(8,128)(2,1)} %bitcast.619), channel_id=1, source_target_pairs={{0,4},{2,6},{4,0},{6,2},{8,12},{10,14},{12,8},{14,10},{16,20},{18,... | collective-permute-start | bytes 6291464 | tf_op jit(solution)/shard_map/ppermute | solution.py:44
  533.2 87.2 %collective-permute-start.96 = (bf16[4,2,64,2048]{3,2,1,0:T(8,128)(2,1)}, bf16[4,2,64,2048]{3,2,1,0:T(8,128)(2,1)}, u32[]{:S(2)}, u32[]{:S(2)}) collective-permute-start(bf16[4,2,64,2048]{3,2,1,0:T(8,128)(2,1)} %dynamic-slice_bitcast_fusion.1), channel_id=1, source_target_pairs={{0,2},{2,0},{4,6},{6,4},{8,10},{10,8},{12,14},{14,12},{16,18},{18,... | collective-permute-start | bytes 6291464 | tf_op jit(solution)/shard_map/ppermute | solution.py:44
  582.1 164.0 %collective-permute-start.56 = (bf16[1024,1024]{1,0:T(8,128)(2,1)}, bf16[1024,1024]{1,0:T(8,128)(2,1)}, u32[]{:S(2)}, u32[]{:S(2)}) collective-permute-start(bf16[1024,1024]{1,0:T(8,128)(2,1)} %convolution_convert_fusion.5), channel_id=1, source_target_pairs={{0,1},{1,0},{2,3},{3,2},{4,5},{5,4},{6,7},{7,6},{8,9},{9,8},{10,11... | collective-permute-start | bytes 6291464 | tf_op jit(solution)/shard_map/ppermute | solution.py:102
  585.7 85.1 %collective-permute-start.107 = (bf16[2,64,2048]{2,1,0:T(8,128)(2,1)}, bf16[2,64,2048]{2,1,0:T(8,128)(2,1)}, u32[]{:S(2)}, u32[]{:S(2)}) collective-permute-start(bf16[2,64,2048]{2,1,0:T(8,128)(2,1)} %dynamic-slice_bitcast_fusion.6), channel_id=1, source_target_pairs={{0,8},{2,10},{4,12},{6,14},{8,16},{10,18},{12,20},{14,22},{16,24},... | collective-permute-start | bytes 1572872 | tf_op jit(solution)/shard_map/ppermute | solution.py:44
  612.9 81.6 %collective-permute-start.102 = (bf16[4,64,2048]{2,1,0:T(8,128)(2,1)}, bf16[4,64,2048]{2,1,0:T(8,128)(2,1)}, u32[]{:S(2)}, u32[]{:S(2)}) collective-permute-start(bf16[4,64,2048]{2,1,0:T(8,128)(2,1)} %dynamic-slice_bitcast_fusion.2), channel_id=1, source_target_pairs={{0,2},{2,0},{4,6},{6,4},{8,10},{10,8},{12,14},{14,12},{16,18},{18,... | collective-permute-start | bytes 3145736 | tf_op jit(solution)/shard_map/ppermute | solution.py:44
  614.9 34.2 %collective-permute-start.91 = (bf16[4,2,64,512]{3,2,1,0:T(8,128)(2,1)S(1)}, bf16[4,2,64,512]{3,2,1,0:T(8,128)(2,1)S(1)}, u32[]{:S(2)}, u32[]{:S(2)}) collective-permute-start(bf16[4,2,64,512]{3,2,1,0:T(8,128)(2,1)S(1)} %dynamic-slice_bitcast_fusion.8), channel_id=1, source_target_pairs={{0,2},{2,0},{4,6},{6,4},{8,10},{10,8},{12,14},{14,12},{16,18},{18,... | collective-permute-start | bytes 1572872 | tf_op jit(solution)/shard_map/ppermute | solution.py:44
  652.0 25.7 %collective-permute-start.97 = (bf16[2,64,2048]{2,1,0:T(8,128)(2,1)}, bf16[2,64,2048]{2,1,0:T(8,128)(2,1)}, u32[]{:S(2)}, u32[]{:S(2)}) collective-permute-start(bf16[2,64,2048]{2,1,0:T(8,128)(2,1)} %dynamic-slice_bitcast_fusion.7), channel_id=1, source_target_pairs={{0,8},{2,10},{4,12},{6,14},{8,16},{10,18},{12,20},{14,22},{16,24},... | collective-permute-start | bytes 1572872 | tf_op jit(solution)/shard_map/ppermute | solution.py:44
  670.2 66.0 %collective-permute-start.86 = (bf16[4,2,64,1536]{3,2,0,1:T(8,128)(2,1)}, bf16[4,2,64,1536]{3,2,0,1:T(8,128)(2,1)S(1)}, u32[]{:S(2)}, u32[]{:S(2)}) collective-permute-start(bf16[4,2,64,1536]{3,2,0,1:T(8,128)(2,1)} %bitcast.685), channel_id=1, source_target_pairs={{0,2},{2,0},{4,6},{6,4},{8,10},{10,8},{12,14},{14,12},{16,18},{18,... | collective-permute-start | bytes 4718600 | tf_op jit(solution)/shard_map/ppermute | solution.py:44
  682.1 23.5 %collective-permute-start.98 = (bf16[2,64,2048]{2,1,0:T(8,128)(2,1)S(1)}, bf16[2,64,2048]{2,1,0:T(8,128)(2,1)S(1)}, u32[]{:S(2)}, u32[]{:S(2)}) collective-permute-start(bf16[2,64,2048]{2,1,0:T(8,128)(2,1)S(1)} %fusion.82), channel_id=1, source_target_pairs={{0,8},{2,10},{4,12},{6,14},{8,16},{10,18},{12,20},{14,22},{16,24},... | collective-permute-start | bytes 1572872 | tf_op jit(solution)/shard_map/ppermute | solution.py:44
  694.5 28.1 %collective-permute-start.109 = (bf16[2,64,2048]{2,1,0:T(8,128)(2,1)S(1)}, bf16[2,64,2048]{2,1,0:T(8,128)(2,1)S(1)}, u32[]{:S(2)}, u32[]{:S(2)}) collective-permute-start(bf16[2,64,2048]{2,1,0:T(8,128)(2,1)S(1)} %fusion.78), channel_id=1, source_target_pairs={{0,8},{2,10},{4,12},{6,14},{8,16},{10,18},{12,20},{14,22},{16,24},... | collective-permute-start | bytes 1572872 | tf_op jit(solution)/shard_map/ppermute | solution.py:44
  696.4 26.1 %collective-permute-start.103 = (bf16[64,2048]{1,0:T(8,128)(2,1)S(1)}, bf16[64,2048]{1,0:T(8,128)(2,1)S(1)}, u32[]{:S(2)}, u32[]{:S(2)}) collective-permute-start(bf16[64,2048]{1,0:T(8,128)(2,1)S(1)} %dynamic-slice_bitcast_fusion.12), channel_id=1, source_target_pairs={{0,8},{2,10},{4,12},{6,14},{8,16},{10,18},{12,20},{14,22},{16,24},... | collective-permute-start | bytes 786440 | tf_op jit(solution)/shard_map/ppermute | solution.py:44
  705.7 30.0 %collective-permute-start.99 = (bf16[2,64,2048]{2,1,0:T(8,128)(2,1)S(1)}, bf16[2,64,2048]{2,1,0:T(8,128)(2,1)S(1)}, u32[]{:S(2)}, u32[]{:S(2)}) collective-permute-start(bf16[2,64,2048]{2,1,0:T(8,128)(2,1)S(1)} %fusion.81), channel_id=1, source_target_pairs={{0,8},{2,10},{4,12},{6,14},{8,16},{10,18},{12,20},{14,22},{16,24},... | collective-permute-start | bytes 1572872 | tf_op jit(solution)/shard_map/ppermute | solution.py:44
  737.7 35.7 %collective-permute-start.87 = (bf16[4,64,1536]{2,1,0:T(8,128)(2,1)}, bf16[4,64,1536]{2,1,0:T(8,128)(2,1)}, u32[]{:S(2)}, u32[]{:S(2)}) collective-permute-start(bf16[4,64,1536]{2,1,0:T(8,128)(2,1)} %dynamic-slice_bitcast_fusion.5), channel_id=1, source_target_pairs={{0,4},{2,6},{4,0},{6,2},{8,12},{10,14},{12,8},{14,10},{16,20},{18,... | collective-permute-start | bytes 2359304 | tf_op jit(solution)/shard_map/ppermute | solution.py:44
  760.2 54.4 %collective-permute-start.81 = (bf16[4,2,64,1024]{3,2,1,0:T(8,128)(2,1)}, bf16[4,2,64,1024]{3,2,1,0:T(8,128)(2,1)}, u32[]{:S(2)}, u32[]{:S(2)}) collective-permute-start(bf16[4,2,64,1024]{3,2,1,0:T(8,128)(2,1)} %dynamic-slice_bitcast_fusion.3), channel_id=1, source_target_pairs={{0,4},{2,6},{4,0},{6,2},{8,12},{10,14},{12,8},{14,10},{16,20},{18,... | collective-permute-start | bytes 3145736 | tf_op jit(solution)/shard_map/ppermute | solution.py:44
  802.1 23.5 %collective-permute-start.71 = (bf16[4,2,64,1024]{3,2,1,0:T(8,128)(2,1)}, bf16[4,2,64,1024]{3,2,1,0:T(8,128)(2,1)}, u32[]{:S(2)}, u32[]{:S(2)}) collective-permute-start(bf16[4,2,64,1024]{3,2,1,0:T(8,128)(2,1)} %dynamic-slice_bitcast_fusion.4), channel_id=1, source_target_pairs={{0,2},{2,0},{4,6},{6,4},{8,10},{10,8},{12,14},{14,12},{16,18},{18,... | collective-permute-start | bytes 3145736 | tf_op jit(solution)/shard_map/ppermute | solution.py:44
  805.7 22.6 %collective-permute-start.61 = (bf16[1040,128]{1,0:T(8,128)(2,1)}, bf16[1040,128]{1,0:T(8,128)(2,1)S(1)}, u32[]{:S(2)}, u32[]{:S(2)}) collective-permute-start(bf16[1040,128]{1,0:T(8,128)(2,1)} %collective-permute-done.60), channel_id=1, source_target_pairs={{0,24},{2,26},{4,28},{6,30},{8,0},{10,2},{12,4},{14,6},{16,8},{18,... | collective-permute-start | bytes 798728 | tf_op jit(solution)/shard_map/ppermute | solution.py:44
  836.9 43.4 %collective-permute-start.83 = (bf16[2,64,1024]{2,1,0:T(8,128)(2,1)}, bf16[2,64,1024]{2,1,0:T(8,128)(2,1)}, u32[]{:S(2)}, u32[]{:S(2)}) collective-permute-start(bf16[2,64,1024]{2,1,0:T(8,128)(2,1)} %fusion.132), channel_id=1, source_target_pairs={{0,8},{2,10},{4,12},{6,14},{8,16},{10,18},{12,20},{14,22},{16,24},... | collective-permute-start | bytes 786440 | tf_op jit(solution)/shard_map/ppermute | solution.py:44
  841.1 41.4 %collective-permute-start.73 = (bf16[2,64,1024]{2,1,0:T(8,128)(2,1)}, bf16[2,64,1024]{2,1,0:T(8,128)(2,1)}, u32[]{:S(2)}, u32[]{:S(2)}) collective-permute-start(bf16[2,64,1024]{2,1,0:T(8,128)(2,1)} %fusion.135), channel_id=1, source_target_pairs={{0,8},{2,10},{4,12},{6,14},{8,16},{10,18},{12,20},{14,22},{16,24},... | collective-permute-start | bytes 786440 | tf_op jit(solution)/shard_map/ppermute | solution.py:44
  868.9 42.6 %collective-permute-start.76 = (bf16[4,2,64,1024]{3,2,0,1:T(8,128)(2,1)}, bf16[4,2,64,1024]{3,2,0,1:T(8,128)(2,1)}, u32[]{:S(2)}, u32[]{:S(2)}) collective-permute-start(bf16[4,2,64,1024]{3,2,0,1:T(8,128)(2,1)} %bitcast.621), channel_id=1, source_target_pairs={{0,4},{2,6},{4,0},{6,2},{8,12},{10,14},{12,8},{14,10},{16,20},{18,... | collective-permute-start | bytes 3145736 | tf_op jit(solution)/shard_map/ppermute | solution.py:44
  882.2 22.3 %collective-permute-start.84 = (bf16[2,64,1024]{2,1,0:T(8,128)(2,1)}, bf16[2,64,1024]{2,1,0:T(8,128)(2,1)}, u32[]{:S(2)}, u32[]{:S(2)}) collective-permute-start(bf16[2,64,1024]{2,1,0:T(8,128)(2,1)} %fusion.131), channel_id=1, source_target_pairs={{0,8},{2,10},{4,12},{6,14},{8,16},{10,18},{12,20},{14,22},{16,24},... | collective-permute-start | bytes 786440 | tf_op jit(solution)/shard_map/ppermute | solution.py:44
  (291 other events, 3255.0 us)

commit v2 on v1

v2 whole, which is shorter than its diff:
```python
import functools

import jax
import jax.numpy as jnp
from jax import lax
from jax.experimental import pallas as pl
from jax.experimental.pallas import tpu as pltpu
from jax.sharding import PartitionSpec as P

LHD = 64
PATCH = 8
EPS = 1e-05
BIG = 1e30
PRECISE = lax.Precision.HIGHEST
BF = jnp.bfloat16
F32 = jnp.float32


def factors(count):
    root = 1
    while (root * 2) ** 3 <= count:
        root *= 2
    rest = count // root
    middle = root if rest % root == 0 and rest // root >= root else 1
    return (rest // middle, middle, root)


class Grid:
    def __init__(self, count):
        self.count = count
        self.sizes = factors(count)
        self.place = lax.axis_index("seq")
        n0, n1, n2 = self.sizes
        self.coord = (self.place // (n1 * n2), (self.place // n2) % n1, self.place % n2)

    def pairs(self, dim, by):
        n0, n1, n2 = self.sizes
        out = []
        for i in range(self.count):
            c = [i // (n1 * n2), (i // n2) % n1, i % n2]
            c[dim] = (c[dim] + by) % self.sizes[dim]
            out.append((i, (c[0] * n1 + c[1]) * n2 + c[2]))
        return out

    def shift(self, value, dim, by=1):
        return lax.ppermute(value, "seq", self.pairs(dim, by))


def follow(value, *events):
    return lax.optimization_barrier((value,) + events)[0]


def spread(grid, block, dim, events=()):
    n = grid.sizes[dim]
    me = grid.coord[dim]
    got = [block] + [grid.shift(block, dim, k) for k in range(1, n)]
    if events:
        got = [got[0]] + [follow(g, *events) for g in got[1:]]
    if n == 1:
        return block[None]
    if n == 2:
        first = me == 0
        return jnp.stack([jnp.where(first, got[0], got[1]), jnp.where(first, got[1], got[0])])
    out = jnp.zeros((n,) + block.shape, block.dtype)
    for k, part in enumerate(got):
        out = lax.dynamic_update_index_in_dim(out, part, (me - k) % n, 0)
    return out


def gather_column(grid, block, *events):
    return spread(grid, block, 0, events)


def gather_plane_off(grid, column):
    n0, n1, n2 = grid.sizes
    flat = n1 * n2
    groups = [[z * flat + i for i in range(flat)] for z in range(n0)]
    return lax.all_gather(column, "seq", axis=1, tiled=False, axis_index_groups=groups)


def gather_plane(grid, column):
    n0, n1, n2 = grid.sizes
    _, rows, width = column.shape
    if (n1, n2) != (2, 2) or n0 % 2:
        block = spread(grid, spread(grid, column, 1), 2)
        block = jnp.transpose(block, (2, 1, 0, 3, 4))
        return block.reshape(grid.count * rows, width)
    half = n0 // 2
    parts = (column[:half], column[half:])
    by_x = [grid.shift(p, 2) for p in parts]
    by_y = [grid.shift(p, 1) for p in parts]
    across = [grid.shift(by_x[0], 1), grid.shift(by_y[1], 2)]
    own, by_x, by_y, across = [
        jnp.concatenate(p, axis=0) for p in (parts, by_x, by_y, across)
    ]
    me_y, me_x = grid.coord[1], grid.coord[2]
    tiles = []
    for y in range(2):
        row = []
        for x in range(2):
            same = jnp.where(me_x == x, own, by_x)
            other = jnp.where(me_x == x, by_y, across)
            row.append(jnp.where(me_y == y, same, other))
        tiles.append(jnp.stack(row, axis=1))
    return jnp.stack(tiles, axis=1).reshape(grid.count * rows, width)


def scatter_column(grid, total):
    n = grid.sizes[0]
    me = grid.coord[0]
    total = total.reshape(n, total.shape[0] // n, total.shape[1])
    summed = lax.dynamic_index_in_dim(total, me, 0, False).astype(F32)
    for k in range(1, n):
        block = lax.dynamic_index_in_dim(total, (me + k) % n, 0, False)
        summed = summed + grid.shift(block, 0, k).astype(F32)
    return summed


def scatter_plane(grid, partial):
    n0, n1, n2 = grid.sizes
    flat = n1 * n2
    groups = [[z * flat + i for i in range(flat)] for z in range(n0)]
    return lax.psum_scatter(
        partial, "seq", scatter_dimension=0, tiled=True, axis_index_groups=groups
    )


def scatter_plane_near(grid, partial):
    n0, n1, n2 = grid.sizes
    if (n1, n2) != (2, 2) or n0 % 2:
        return scatter_plane(grid, partial)
    width = partial.shape[1]
    blocks = partial.reshape(4, 2, -1, width)
    me = grid.coord[1] * 2 + grid.coord[2]
    own, by_x, by_y, across = [
        lax.dynamic_index_in_dim(blocks, lax.bitwise_xor(me, k), 0, False) for k in (0, 1, 2, 3)
    ]

    def plus(*terms):
        return sum(t.astype(F32) for t in terms).astype(BF)

    through_y, through_x = grid.shift(across[0], 1), grid.shift(across[1], 2)
    from_x = (grid.shift(plus(by_x[0], through_y), 2), grid.shift(by_x[1], 2))
    from_y = (grid.shift(by_y[0], 1), grid.shift(plus(by_y[1], through_x), 1))
    return jnp.concatenate([plus(own[j], from_x[j], from_y[j]) for j in (0, 1)], axis=0)


def plane_major(grid, values):
    n0, n1, n2 = grid.sizes
    width = values.shape[1]
    rows = width // grid.count
    flat = n1 * n2
    to = lax.broadcasted_iota(jnp.int32, (width, width), 0)
    of = lax.broadcasted_iota(jnp.int32, (width, width), 1)
    plane, z, row = to // (n0 * rows), (to // rows) % n0, to % rows
    pick = ((z * flat + plane) * rows + row == of).astype(BF)
    return rows_rows(pick, values).astype(BF)


def swap_mp(value):
    size = lax.axis_size("mp")
    return lax.ppermute(value, "mp", [(i, (i + 1) % size) for i in range(size)])


def mp_sum(value):
    low = value.astype(BF)
    return low.astype(F32) + swap_mp(low).astype(F32)


def mp_sum_exact(value):
    return value + swap_mp(value)


def seq_sum(value):
    count = lax.axis_size("seq")
    by = 1
    while by < count:
        value = value + lax.ppermute(value, "seq", [(i, i ^ by) for i in range(count)])
        by *= 2
    return value


def spread_small(grid, value):
    for dim in (2, 1, 0):
        n = grid.sizes[dim]
        me = grid.coord[dim]
        got = jnp.stack([value if k == 0 else grid.shift(value, dim, k) for k in range(n)])
        value = jnp.stack([lax.dynamic_index_in_dim(got, (me - j) % n, 0, False) for j in range(n)])
    return value


def scan_states(grid, table, state, reverse, event=None):
    heads = table.shape[-1]
    total = state.reshape(heads, state.shape[0] // heads, state.shape[1])
    enter = jnp.zeros_like(total)
    passed = jnp.ones((heads,), F32)
    levels = [d for d in (2, 1, 0) if grid.sizes[d] > 1]
    crossed = total
    for dim in levels:
        n = grid.sizes[dim]
        me = grid.coord[dim]
        group = table
        for slow in range(dim):
            group = lax.dynamic_index_in_dim(group, grid.coord[slow], 0, False)
        for _ in range(dim + 1, 3):
            group = jnp.prod(group, axis=1)
        index = lax.broadcasted_iota(jnp.int32, (n, 1), 0)

        def product(kept):
            return jnp.prod(jnp.where(kept, group, 1.0), axis=0)

        if event is not None and dim == levels[-1]:
            total = follow(total, event)
        low = total.astype(BF)
        summed = None
        for k in range(n):
            other = (me - k) % n
            ahead = (index < other) if reverse else (index > other)
            before = (index > me) if reverse else (index < me)
            got = total if k == 0 else grid.shift(low, dim, k).astype(F32)
            if k > 0:
                valid = (other > me) if reverse else (other < me)
                weight = jnp.where(valid, product(ahead & before) * passed, 0.0)
                enter = enter + weight[:, None, None] * got
            if dim != levels[-1]:
                term = product(ahead)[:, None, None] * got
                summed = term if summed is None else summed + term
        passed = passed * product((index > me) if reverse else (index < me))
        if dim != levels[-1]:
            crossed = total = summed
    return enter.reshape(state.shape), crossed


VMEM_ROOM = 60 * 2**20
SIDE = 128


def dims(a, b, exact=None):
    return functools.partial(
        lax.dot_general,
        dimension_numbers=(((a,), (b,)), ((), ())),
        precision=exact,
        preferred_element_type=F32,
    )


rows_cols = dims(1, 0)
rows_rows = dims(1, 1)
cols_cols = dims(0, 0)
exact_rc = dims(1, 0, PRECISE)
exact_rr = dims(1, 1, PRECISE)
exact_cc = dims(0, 0, PRECISE)


def call(body, name, shapes, flops, scratch=(), grid=None, in_specs=None, out_specs=None, moved=0):
    kw = {}
    if grid is not None:
        kw = dict(grid=grid, in_specs=in_specs, out_specs=out_specs)
    return pl.pallas_call(
        body,
        out_shape=shapes,
        scratch_shapes=list(scratch),
        name=name,
        compiler_params=pltpu.CompilerParams(vmem_limit_bytes=VMEM_ROOM),
        cost_estimate=pl.CostEstimate(flops=flops, bytes_accessed=moved, transcendentals=0),
        **kw,
    )


def half_lanes(n):
    return lax.broadcasted_iota(jnp.int32, (n, SIDE), 1) < LHD


def two_heads(values, low_half):
    none = jnp.zeros_like(values)
    return jnp.concatenate(
        [jnp.where(low_half, values, none), jnp.where(low_half, none, values)], axis=0
    )


def own_patch(n):
    row = lax.broadcasted_iota(jnp.int32, (n, n), 0)
    col = lax.broadcasted_iota(jnp.int32, (n, n), 1)
    return lax.div(row, PATCH) == lax.div(col, PATCH)


def gathered(values, mine):
    n = values.shape[0]
    kept = jnp.where(mine, values, 0.0).reshape(n // PATCH, PATCH, n)
    return jnp.sum(kept, axis=0)


def widened(values, mine):
    n = mine.shape[0]
    return jnp.where(mine, jnp.concatenate([values] * (n // PATCH), axis=0), 0.0).astype(BF)


def soft_block(scores, mine):
    n = scores.shape[0]
    key = lax.broadcasted_iota(jnp.int32, (PATCH, n), 0)
    query = lax.rem(lax.broadcasted_iota(jnp.int32, (PATCH, n), 1), PATCH)
    block = jnp.where(key <= query, gathered(scores, mine) * (LHD ** (-0.5)), -BIG)
    weights = jnp.exp(block - jnp.max(block, axis=0, keepdims=True))
    return weights / jnp.sum(weights, axis=0, keepdims=True)


def attend_body(width, qkv, out):
    n = qkv.shape[0]
    mine = own_patch(n)
    low_half = half_lanes(n)
    for p in range(width // SIDE):
        at = [slice(j * width + p * SIDE, j * width + (p + 1) * SIDE) for j in range(3)]
        q, k, v = qkv[:, at[0]], qkv[:, at[1]], qkv[:, at[2]]
        scores = rows_rows(two_heads(k, low_half), q)
        soft = [widened(soft_block(scores[j * n : (j + 1) * n], mine), mine) for j in range(2)]
        both = cols_cols(jnp.concatenate(soft, axis=0), two_heads(v, low_half))
        out[:, at[0]] = both.astype(BF)


def attend(qkv):
    rows, three = qkv.shape
    width = three // 3
    return call(
        functools.partial(attend_body, width),
        "attend",
        jax.ShapeDtypeStruct((rows, width), BF),
        rows * SIDE * width * 8,
        grid=(rows // SIDE,),
        in_specs=[pl.BlockSpec((SIDE, three), lambda i: (i, 0))],
        out_specs=pl.BlockSpec((SIDE, width), lambda i: (i, 0)),
        moved=rows * width * 8,
    )(qkv)


def attend_back_body(width, qkv, grad, out):
    n = qkv.shape[0]
    mine = own_patch(n)
    low_half = half_lanes(n)
    scale = LHD ** (-0.5)
    for p in range(width // SIDE):
        at = [slice(j * width + p * SIDE, j * width + (p + 1) * SIDE) for j in range(3)]
        q, k, v = qkv[:, at[0]], qkv[:, at[1]], qkv[:, at[2]]
        g = grad[:, at[0]]
        k_two = two_heads(k, low_half)
        scores = rows_rows(k_two, q)
        probs = rows_rows(two_heads(v, low_half), g)
        soft_wide, back_wide = [], []
        for j in range(2):
            rows = slice(j * n, (j + 1) * n)
            soft = soft_block(scores[rows], mine)
            prob = gathered(probs[rows], mine)
            back = soft * (prob - jnp.sum(soft * prob, axis=0, keepdims=True))
            soft_wide.append(widened(soft, mine))
            back_wide.append(widened(back, mine))
        q_grad = cols_cols(jnp.concatenate(back_wide, axis=0), k_two)
        k_grad = rows_cols(jnp.concatenate(back_wide, axis=1), two_heads(q, low_half))
        v_grad = rows_cols(jnp.concatenate(soft_wide, axis=1), two_heads(g, low_half))
        out[:, at[0]] = (q_grad * scale).astype(BF)
        out[:, at[1]] = (k_grad * scale).astype(BF)
        out[:, at[2]] = v_grad.astype(BF)


def attend_back(qkv, grad):
    rows, three = qkv.shape
    width = three // 3
    return call(
        functools.partial(attend_back_body, width),
        "attend_back",
        jax.ShapeDtypeStruct((rows, three), BF),
        rows * SIDE * width * 20,
        grid=(rows // SIDE,),
        in_specs=[
            pl.BlockSpec((SIDE, three), lambda i: (i, 0)),
            pl.BlockSpec((SIDE, width), lambda i: (i, 0)),
        ],
        out_specs=pl.BlockSpec((SIDE, three), lambda i: (i, 0)),
        moved=rows * width * 14,
    )(qkv, grad)


def middle_body(step, normed, grad, w_down, w_pair, hidden, pair):
    x = normed[...]
    gate = rows_cols(x, w_pair[:, :step])
    up = rows_cols(x, w_pair[:, step:])
    back = rows_cols(grad[...], w_down[...])
    sig = 1.0 / (1.0 + jnp.exp(-gate))
    act = gate * sig
    hidden[...] = (act * up).astype(BF)
    pair[:, step:] = (back * act).astype(BF)
    pair[:, :step] = (back * up * sig * (1.0 + gate * (1.0 - sig))).astype(BF)


def middle(normed, grad, w_all, ff, step):
    rows, width = normed.shape
    return call(
        functools.partial(middle_body, step),
        "middle",
        (jax.ShapeDtypeStruct((rows, ff), BF), jax.ShapeDtypeStruct((rows, 2 * ff), BF)),
        rows * width * ff * 6,
        grid=(ff // step,),
        in_specs=[
            pl.BlockSpec((rows, width), lambda i: (0, 0)),
            pl.BlockSpec((rows, width), lambda i: (0, 0)),
            pl.BlockSpec((width, step), lambda i: (0, i)),
            pl.BlockSpec((width, 2 * step), lambda i: (0, i + ff // (2 * step))),
        ],
        out_specs=(
            pl.BlockSpec((rows, step), lambda i: (0, i)),
            pl.BlockSpec((rows, 2 * step), lambda i: (0, i)),
        ),
        moved=rows * width * 4 + width * ff * 6 + rows * ff * 6,
    )(normed, grad, w_all, w_all)


def products_body(starts, *refs):
    count = len(starts) - 1
    out = refs[2 * count]
    for j in range(count):

        @pl.when((pl.program_id(0) >= starts[j]) & (pl.program_id(0) < starts[j + 1]))
        def _(j=j):
            out[...] = rows_cols(refs[2 * j][...], refs[2 * j + 1][...]).astype(out.dtype)


def products(pairs, step):
    starts = [0]
    in_specs, args, flops, moved = [], [], 0, 0
    for left, right in pairs:
        first, runs = starts[-1], right.shape[1] // step
        starts.append(first + runs)
        in_specs.append(pl.BlockSpec(left.shape, lambda i: (0, 0)))

        def column(i, first=first, runs=runs):
            return (0, jnp.clip(i - first, 0, runs - 1))

        in_specs.append(pl.BlockSpec((right.shape[0], step), column))
        args += [left, right]
        flops += 2 * left.shape[0] * right.shape[0] * right.shape[1]
        moved += 2 * (left.size + right.size)
    m = pairs[0][0].shape[0]
    return call(
        functools.partial(products_body, tuple(starts)),
        "products",
        jax.ShapeDtypeStruct((m, starts[-1] * step), BF),
        flops,
        grid=(starts[-1],),
        in_specs=in_specs,
        out_specs=pl.BlockSpec((m, step), lambda i: (0, i)),
        moved=moved + 2 * m * starts[-1] * step,
    )(*args)


def softplus_fn(values):
    return jnp.log1p(jnp.exp(-jnp.abs(values))) + jnp.maximum(values, 0.0)


def lower_ones(n):
    row = lax.broadcasted_iota(jnp.int32, (n, n), 0)
    col = lax.broadcasted_iota(jnp.int32, (n, n), 1)
    return row >= col


def taps_fill(rim, mixed, buf, taps):
    buf[0:8, :] = rim[...].astype(F32)
    buf[8 : 8 + mixed.shape[0], :] = mixed[...].astype(F32)


def conv_here(buf, k_x, k_bc, info, n, taps):
    wide = jnp.concatenate([k_x[...], k_bc[...]], axis=1)
    total = None
    for k in range(taps):
        at = 9 - taps + k
        term = buf[at : at + n, :] * wide[k : k + 1, :] * info[:, k : k + 1]
        total = term if total is None else total + term
    return total


def decays(raw, small, n):
    base = raw[...] + small[0:1, :]
    step = softplus_fn(base)
    rate = jnp.exp(small[1:2, :])
    log_decay = -step * rate
    tri = lower_ones(n).astype(F32)
    cum = exact_rc(tri, log_decay)
    return base, step, rate, log_decay, tri, cum


def mix_body(taps, inner, rim, mixed, raw, small, skip, k_x, k_bc, info, seg, y_out, c_out, din_out, state_out, buf):
    n = mixed.shape[0]
    taps_fill(rim, mixed, buf, taps)
    pre = conv_here(buf, k_x, k_bc, info, n, taps)
    act = pre / (1.0 + jnp.exp(-pre))
    b = act[:, inner : inner + SIDE]
    c = act[:, inner + SIDE :]
    _, step, _, _, _, cum = decays(raw, small, n)
    cum_t, step_t = cum.T, step.T
    live = lower_ones(n) & (info[:, 6:7] == seg[0:1, :])
    both = exact_rr(c, b)
    din_out[...] = info[:, 4:5] * jnp.exp(cum)
    tail = jnp.exp(jnp.where(info[:, 5:6] > 0.0, cum[n - 1 : n, :] - cum, -BIG)) * step
    low_half = half_lanes(n)
    c_out[...] = c
    for p in range(inner // SIDE):
        at = slice(p * SIDE, (p + 1) * SIDE)
        x = act[:, at]
        y = skip[0:1, at] * x
        for j, mine in enumerate((low_half, ~low_half)):
            h = 2 * p + j
            gaps = jnp.exp(jnp.where(live, cum[:, h : h + 1] - cum_t[h : h + 1, :], -BIG))
            mix = both * gaps * step_t[h : h + 1, :]
            y = y + exact_rc(mix, jnp.where(mine, x, 0.0))
        y_out[:, at] = y
        weighted = x * jnp.where(low_half, tail[:, 2 * p : 2 * p + 1], tail[:, 2 * p + 1 : 2 * p + 2])
        state_out[at, :] = exact_cc(weighted, b)


def mix(rim, mixed, raw, small, skip, k_x, k_bc, info, seg):
    n, wide = mixed.shape
    taps, inner = k_x.shape
    return call(
        functools.partial(mix_body, taps, inner),
        "mix",
        (
            jax.ShapeDtypeStruct((n, inner), F32),
            jax.ShapeDtypeStruct((n, SIDE), F32),
            jax.ShapeDtypeStruct((n, SIDE), F32),
            jax.ShapeDtypeStruct((inner, SIDE), F32),
        ),
        n * n * inner * 24,
        scratch=(pltpu.VMEM((n + 8, wide), F32),),
        moved=n * inner * 20,
    )(rim, mixed, raw, small, skip, k_x, k_bc, info, seg)


def pair_cols(values, p, low_half):
    return jnp.where(low_half, values[:, 2 * p : 2 * p + 1], values[:, 2 * p + 1 : 2 * p + 2])


def finish_body(inner, y_part, c, din, state, z, y_out, gated_out, square):
    n = y_part.shape[0]
    low_half = half_lanes(n)
    total = None
    for p in range(inner // SIDE):
        at = slice(p * SIDE, (p + 1) * SIDE)
        y = y_part[:, at] + pair_cols(din, p, low_half) * exact_rr(c[...], state[at, :])
        gate = z[:, at]
        gated = y * (gate / (1.0 + jnp.exp(-gate)))
        y_out[:, at] = y
        gated_out[:, at] = gated
        term = gated * gated
        total = term if total is None else total + term
    square[...] = jnp.broadcast_to(jnp.sum(total, axis=1, keepdims=True), square.shape)


def finish(y_part, c, din, state, z):
    n, inner = y_part.shape
    return call(
        functools.partial(finish_body, inner),
        "finish",
        (
            jax.ShapeDtypeStruct((n, inner), F32),
            jax.ShapeDtypeStruct((n, inner), F32),
            jax.ShapeDtypeStruct((n, SIDE), F32),
        ),
        n * SIDE * inner * 12,
        moved=n * inner * 20,
    )(y_part, c, din, state, z)


def unfinish_body(inner, y_norm_grad, gated, y_full, z, gain, stats, din, c, y_grad, z_grad, state_grad):
    n = gated.shape[0]
    low_half = half_lanes(n)
    for p in range(inner // SIDE):
        at = slice(p * SIDE, (p + 1) * SIDE)
        back = stats[:, 0:1] * (y_norm_grad[:, at] * gain[0:1, at]) - gated[:, at] * stats[:, 1:2]
        gate = z[:, at]
        sig = 1.0 / (1.0 + jnp.exp(-gate))
        y_back = back * gate * sig
        y_grad[:, at] = y_back
        z_grad[:, at] = (back * y_full[:, at] * sig * (1.0 + gate * (1.0 - sig))).astype(BF)
        state_grad[at, :] = exact_cc(y_back * pair_cols(din, p, low_half), c[...])


def unfinish(y_norm_grad, gated, y_full, z, gain, stats, din, c):
    n, inner = gated.shape
    return call(
        functools.partial(unfinish_body, inner),
        "unfinish",
        (
            jax.ShapeDtypeStruct((n, inner), F32),
            jax.ShapeDtypeStruct((n, inner), BF),
            jax.ShapeDtypeStruct((inner, SIDE), F32),
        ),
        n * SIDE * inner * 12,
        moved=n * inner * 24,
    )(y_norm_grad, gated, y_full, z, gain, stats, din, c)


def unmix_body(
    taps, inner, rim, mixed, raw, small, skip, k_x, k_bc, info, seg, y_grad, state_in, state_back,
    ext_out, raw_out, taps_out, heads_out, skip_out, buf, d_buf, d_act, cols, sums, steps,
):
    n = mixed.shape[0]
    taps_fill(rim, mixed, buf, taps)
    pre = conv_here(buf, k_x, k_bc, info, n, taps)
    sig_pre = 1.0 / (1.0 + jnp.exp(-pre))
    act = pre * sig_pre
    b = act[:, inner : inner + SIDE]
    c = act[:, inner + SIDE :]
    base, step, rate, log_decay, tri, cum = decays(raw, small, n)
    cum_t, step_t = cum.T, step.T
    live = lower_ones(n) & (info[:, 6:7] == seg[0:1, :])
    both = exact_rr(c, b)
    din = info[:, 4:5] * jnp.exp(cum)
    tail = jnp.exp(jnp.where(info[:, 5:6] > 0.0, cum[n - 1 : n, :] - cum, -BIG))
    low_half = half_lanes(n)
    cols[...] = jnp.zeros_like(cols)
    sums[...] = jnp.zeros_like(sums)
    steps[...] = jnp.zeros_like(steps)
    both_grad = jnp.zeros((n, n), F32)
    b_grad = jnp.zeros((n, SIDE), F32)
    c_grad = jnp.zeros((n, SIDE), F32)
    lane = lax.broadcasted_iota(jnp.int32, (1, SIDE), 1)
    total_grad = jnp.zeros((1, SIDE), F32)
    tail_grad = jnp.zeros((n, SIDE), F32)
    for p in range(inner // SIDE):
        at = slice(p * SIDE, (p + 1) * SIDE)
        x = act[:, at]
        dy = y_grad[:, at]
        s_in = state_in[at, :]
        s_back = state_back[at, :]
        out_b = exact_rr(b, s_back)
        weight = pair_cols(tail, p, low_half) * pair_cols(step, p, low_half)
        dx = skip[0:1, at] * dy + weight * out_b
        b_grad = b_grad + exact_rc(x * weight, s_back)
        dy_in = pair_cols(din, p, low_half) * dy
        in_c = exact_rr(c, s_in)
        c_grad = c_grad + exact_rc(dy_in, s_in)
        skip_out[0:1, at] = jnp.sum(dy * x, axis=0, keepdims=True)
        held = jnp.sum(s_in * s_back, axis=1, keepdims=True)
        for j, mine in enumerate((low_half, ~low_half)):
            h = 2 * p + j
            dy_mine = jnp.where(mine, dy, 0.0)
            gaps = jnp.exp(jnp.where(live, cum[:, h : h + 1] - cum_t[h : h + 1, :], -BIG))
            step_row = step_t[h : h + 1, :]
            back = exact_rr(dy_mine, x) * gaps
            both_grad = both_grad + back * step_row
            back = back * both
            each = back * step_row
            dx = dx + exact_cc(both * gaps * step_row, dy_mine)
            steps[h : h + 1, :] = jnp.sum(back, axis=0, keepdims=True)
            sums[h : h + 1, :] = -jnp.sum(each, axis=0, keepdims=True)
            from_in = jnp.sum(jnp.where(mine, dy_in * in_c, 0.0), axis=1, keepdims=True)
            cols[:, h : h + 1] = jnp.sum(each, axis=1, keepdims=True) + from_in
            from_tail = jnp.sum(jnp.where(mine, x * out_b, 0.0), axis=1, keepdims=True)
            tail_grad = tail_grad + jnp.where(lane == h, from_tail, 0.0)
            here = jnp.sum(held[j * LHD : (j + 1) * LHD, :], axis=0, keepdims=True)
            total_grad = total_grad + jnp.where(lane == h, here, 0.0)
        d_act[:, at] = dx
    d_act[:, inner : inner + SIDE] = b_grad + exact_cc(both_grad, c)
    d_act[:, inner + SIDE :] = c_grad + exact_rc(both_grad, b)
    tail_back = tail_grad * tail
    row = lax.broadcasted_iota(jnp.int32, (n, SIDE), 0)
    moved = tail_back * step
    last = jnp.sum(moved, axis=0, keepdims=True) + total_grad * din[n - 1 : n, :]
    cum_grad = cols[...] + sums[...].T - moved + jnp.where(row == n - 1, last, 0.0)
    decay_grad = exact_cc(tri, cum_grad)
    step_grad = steps[...].T + tail_back - decay_grad * rate
    raw_grad = step_grad / (1.0 + jnp.exp(-base))
    raw_out[...] = raw_grad
    heads_out[0:1, :] = jnp.sum(raw_grad, axis=0, keepdims=True)
    heads_out[1:2, :] = jnp.sum(decay_grad * log_decay, axis=0, keepdims=True)
    heads_out[2:8, :] = jnp.zeros((6, SIDE), F32)
    d_pre = d_act[...] * (sig_pre * (1.0 + pre * (1.0 - sig_pre)))
    d_buf[...] = jnp.zeros_like(d_buf)
    wide = jnp.concatenate([k_x[...], k_bc[...]], axis=1)
    for k in range(taps):
        at = 9 - taps + k
        masked = d_pre * info[:, k : k + 1]
        d_buf[at : at + n, :] = d_buf[at : at + n, :] + masked * wide[k : k + 1, :]
        taps_out[k : k + 1, :] = jnp.sum(masked * buf[at : at + n, :], axis=0, keepdims=True)
    ext_out[...] = d_buf[...]


def unmix(rim, mixed, raw, small, skip, k_x, k_bc, info, seg, y_grad, state_in, state_back):
    n, wide = mixed.shape
    taps, inner = k_x.shape
    return call(
        functools.partial(unmix_body, taps, inner),
        "unmix",
        (
            jax.ShapeDtypeStruct((n + 8, wide), F32),
            jax.ShapeDtypeStruct((n, SIDE), F32),
            jax.ShapeDtypeStruct((taps, wide), F32),
            jax.ShapeDtypeStruct((8, SIDE), F32),
            jax.ShapeDtypeStruct((1, inner), F32),
        ),
        n * n * inner * 96,
        scratch=(
            pltpu.VMEM((n + 8, wide), F32),
            pltpu.VMEM((n + 8, wide), F32),
            pltpu.VMEM((n, wide), F32),
            pltpu.VMEM((n, SIDE), F32),
            pltpu.VMEM((SIDE, n), F32),
            pltpu.VMEM((SIDE, n), F32),
        ),
        moved=n * inner * 30,
    )(rim, mixed, raw, small, skip, k_x, k_bc, info, seg, y_grad, state_in, state_back)


def bf_dot(left, right):
    return rows_cols(left, right)


def dot_t(left, right):
    return rows_rows(left, right)


def grad_dot(left, right):
    return cols_cols(left, right)


def rms_rows(values):
    return lax.rsqrt(jnp.mean(values * values, axis=-1, keepdims=True) + EPS)


def norm_back(grad_in, values, rstd_rows, gain_row):
    normed_rows = values * rstd_rows
    gain_grad = jnp.sum(grad_in * normed_rows, axis=0)
    scaled = grad_in * gain_row[None, :]
    input_grad = rstd_rows * (
        scaled - normed_rows * jnp.mean(scaled * normed_rows, axis=-1, keepdims=True)
    )
    return (input_grad, gain_grad)


def local(
    seq_count,
    bytes_in,
    out_grad,
    seq_ids,
    norm_gain,
    w_z,
    w_x,
    w_bc,
    w_dt,
    w_out,
    attn_gain,
    w_q,
    w_k,
    w_v,
    w_o,
    mlp_gain,
    w_gate,
    w_up,
    w_down,
    dt_bias,
    a_log,
    d_skip,
    conv_x,
    conv_bc,
    inner_gain,
):
    grid = Grid(seq_count)
    rows, ff = w_gate.shape
    inner = w_x.shape[1]
    bc_width = w_bc.shape[1]
    heads = w_dt.shape[1]
    attn_width = w_q.shape[1]
    step = min(256, ff)
    byte_rows, model_width = bytes_in.shape
    patch_rows = byte_rows // PATCH
    taps = conv_x.shape[0]
    inner_full = inner * lax.axis_size("mp")

    first = jnp.concatenate(
        [
            w_x.astype(BF),
            w_bc.astype(BF),
            w_dt.astype(BF),
            norm_gain.astype(BF)[:, None],
            attn_gain.astype(BF)[:, None],
            mlp_gain.astype(BF)[:, None],
            jnp.zeros((rows, SIDE - heads - 3), BF),
        ],
        axis=1,
    )
    first_column = gather_column(grid, first)
    first_all = gather_plane(grid, first_column)
    second = jnp.concatenate(
        [w.astype(BF) for w in (w_z, w_out.T, w_q, w_k, w_v, w_o.T)], axis=1
    )
    second = follow(second, first_column)
    pair = jnp.stack(
        [w.astype(BF).reshape(rows, ff // step, step) for w in (w_gate, w_up)], axis=2
    ).reshape(rows, 2 * ff)
    mlp = jnp.concatenate([w_down.T.astype(BF), pair], axis=1)

    tail_all = first_all[:, inner + bc_width :]
    gains = tail_all[:, heads : heads + 3].astype(F32).T
    norm_row, attn_row, mlp_row = gains[0], gains[1], gains[2]
    x_float = bytes_in.astype(F32)
    patch_in = jnp.mean(x_float.reshape(patch_rows, PATCH, model_width), axis=1)
    rstd_patch = rms_rows(patch_in)
    h_norm = (patch_in * rstd_patch * norm_row[None, :]).astype(BF)
    into = bf_dot(h_norm, first_all)
    mixed = into[:, : inner + bc_width].astype(BF)
    raw = into[:, inner + bc_width :]
    second_column = gather_column(grid, second, mixed)
    second_all = gather_plane_off(grid, second_column).reshape(model_width, -1)
    z_all, out_all = second_all[:, :inner], second_all[:, inner : 2 * inner]
    third_all = second_all[:, 2 * inner :]
    qkv_all, wo_all = third_all[:, : 3 * attn_width], third_all[:, 3 * attn_width :]
    rim = lax.ppermute(
        mixed[patch_rows - (taps - 1) :], "seq", [(i, i + 1) for i in range(seq_count - 1)]
    )
    rim = jnp.pad(rim, ((8 - (taps - 1), 0), (0, 0)))
    first_row = lax.axis_index("seq") * patch_rows
    ids_padded = jnp.concatenate([jnp.full((taps - 1,), -1, jnp.int32), seq_ids])
    ids_ext = lax.dynamic_slice_in_dim(ids_padded, first_row, patch_rows + taps - 1)
    ids = ids_ext[taps - 1 :]
    columns = [ids_ext[k : k + patch_rows] == ids for k in range(taps)]
    columns += [ids == ids_ext[taps - 2], ids == ids[patch_rows - 1], ids]
    info = jnp.stack([c.astype(F32) for c in columns], axis=1)
    info = jnp.pad(info, ((0, 0), (0, SIDE - info.shape[1])))
    seg = jnp.broadcast_to(ids.astype(F32)[None, :], (8, patch_rows))
    small = jnp.pad(jnp.stack([dt_bias, a_log]), ((0, 6), (0, SIDE - heads)))
    skip = jnp.repeat(d_skip, inner // heads)[None, :]
    whole = jnp.sum(softplus_fn(raw[:, :heads] + dt_bias), axis=0) * -jnp.exp(a_log)
    table = spread_small(grid, info[patch_rows - 1, taps] * jnp.exp(whole))
    known = (rim, mixed, raw, small, skip, conv_x, conv_bc, info, seg)
    y_part, c_rows, decay_in, state_own = mix(*known)
    state_in, crossed = scan_states(grid, table, state_own, False)
    mlp_column = gather_column(grid, follow(mlp, first_all, second_column), crossed)
    mlp_all = gather_plane_off(grid, follow(mlp_column, second_all)).reshape(model_width, -1)
    down_all, pair_all = mlp_all[:, :ff], mlp_all[:, ff:]
    gate_z = bf_dot(h_norm, z_all)
    y_full, gated, square = finish(y_part, c_rows, decay_in, state_in, gate_z)
    square_sum = mp_sum_exact(square[:, 0])
    rstd_inner = lax.rsqrt(square_sum / inner_full + EPS)[:, None]
    y_norm = (gated * rstd_inner * inner_gain[None, :]).astype(BF)
    mixer_out = mp_sum(dot_t(y_norm, out_all))
    patch_out = patch_in + mixer_out

    rows_in = x_float + jnp.repeat(patch_out, PATCH, axis=0)
    rstd_attn = rms_rows(rows_in)
    normed = (rows_in * rstd_attn * attn_row[None, :]).astype(BF)
    qkv = bf_dot(normed, qkv_all).astype(BF)
    attended = attend(qkv)
    after_attn = rows_in + mp_sum(dot_t(attended, wo_all))
    rstd_mlp = rms_rows(after_attn)
    normed_mlp = (after_attn * rstd_mlp * mlp_row[None, :]).astype(BF)
    hidden, pair_grad = middle(normed_mlp, out_grad, mlp_all, ff, step)
    block_out = after_attn + mp_sum(dot_t(hidden, down_all))

    mlp_part = products(
        (
            (plane_major(grid, normed_mlp), pair_grad),
            (plane_major(grid, out_grad), hidden),
        ),
        2 * step,
    )
    mlp_plane = scatter_plane(grid, mlp_part)
    pair_grad = follow(pair_grad, mlp_part)
    mlp_norm_grad = mp_sum(dot_t(pair_grad, pair_all))
    mlp_in_grad, mlp_gain_grad = norm_back(mlp_norm_grad, after_attn, rstd_mlp, mlp_row)
    after_grad = out_grad.astype(F32) + mlp_in_grad
    after_low = after_grad.astype(BF)
    attended_grad = bf_dot(after_low, wo_all).astype(BF)
    qkv_grad = attend_back(qkv, attended_grad)
    third_part = products(
        (
            (plane_major(grid, normed), qkv_grad),
            (plane_major(grid, after_low), attended),
        ),
        attn_width,
    )
    qkv_grad = follow(qkv_grad, third_part)
    attn_norm_grad = mp_sum(dot_t(qkv_grad, qkv_all))
    attn_in_grad, attn_gain_grad = norm_back(attn_norm_grad, rows_in, rstd_attn, attn_row)
    rows_grad = after_grad + attn_in_grad
    patch_grad = jnp.sum(rows_grad.reshape(patch_rows, PATCH, model_width), axis=1)
    patch_low = patch_grad.astype(BF)
    y_norm_grad = bf_dot(patch_low, out_all)
    shared = y_norm_grad * gated
    inner_gain_grad = jnp.sum(shared * rstd_inner, axis=0)
    cross_sum = mp_sum_exact(jnp.sum(shared * inner_gain[None, :], axis=-1))[:, None]
    stats = jnp.concatenate([rstd_inner, rstd_inner**3 * (cross_sum / inner_full)], axis=1)
    stats = jnp.pad(stats, ((0, 0), (0, SIDE - 2)))
    y_grad, z_low, state_in_grad = unfinish(
        y_norm_grad, gated, y_full, gate_z, inner_gain[None, :], stats, decay_in, c_rows
    )
    h_norm_t = plane_major(grid, h_norm)
    second_part = products(((h_norm_t, z_low), (plane_major(grid, patch_low), y_norm)), inner)
    state_in_grad = follow(state_in_grad, second_part)
    state_grad, crossed = scan_states(grid, table, state_in_grad, True, mlp_plane)
    third_plane = scatter_plane(grid, follow(third_part, mlp_plane, crossed))
    ext_grad, raw_grad, taps_grad, heads_grad, skip_grad = unmix(
        *known, y_grad, state_in, state_grad
    )
    bc_total = mp_sum(ext_grad[:, inner:])
    conv_bc_grad = mp_sum_exact(taps_grad[:, inner:])
    ext_full = jnp.concatenate([ext_grad[:, :inner], bc_total], axis=1)
    rim_back = lax.ppermute(
        ext_full[8 - (taps - 1) : 8], "seq", [(i + 1, i) for i in range(seq_count - 1)]
    )
    mixed_low = (
        ext_full[8:] + jnp.pad(rim_back, ((patch_rows - (taps - 1), 0), (0, 0)))
    ).astype(BF)
    first_grad = jnp.concatenate([mixed_low, raw_grad.astype(BF)], axis=1)
    first_part = bf_dot(h_norm_t, first_grad).astype(BF)
    first_grad = follow(first_grad, first_part)
    second_plane = scatter_plane(grid, follow(second_part, third_plane, first_part))
    first_plane = scatter_plane_near(grid, first_part)
    lane = lax.broadcasted_iota(jnp.int32, (1, first_grad.shape[1]), 1)
    twice = (lane >= inner) & (lane < inner + bc_width) & (lax.axis_index("mp") > 0)
    own_grad = jnp.where(twice, jnp.zeros_like(first_grad), first_grad)
    h_grad = mp_sum(dot_t(own_grad, first_all) + dot_t(z_low, z_all))
    patch_in_grad, norm_gain_grad = norm_back(h_grad, patch_in, rstd_patch, norm_row)
    patch_total = patch_grad + patch_in_grad
    bytes_grad = rows_grad + jnp.repeat(patch_total / PATCH, PATCH, axis=0)

    mlp_sum = scatter_column(grid, follow(mlp_plane, state_grad))
    pair_sum = mlp_sum[:, : 2 * ff].reshape(rows, ff // step, 2, step)
    w_gate_grad = pair_sum[:, :, 0].reshape(rows, ff)
    w_up_grad = pair_sum[:, :, 1].reshape(rows, ff)
    w_down_grad = mlp_sum[:, 2 * ff :].T
    third_sum = scatter_column(grid, third_plane)
    w_qkv_grad, w_o_grad = third_sum[:, : 3 * attn_width], third_sum[:, 3 * attn_width :].T
    second_sum = scatter_column(grid, second_plane)
    w_z_grad, w_out_grad = second_sum[:, :inner], second_sum[:, inner:].T
    first_sum = scatter_column(grid, first_plane)

    pieces = (
        heads_grad[:2],
        skip_grad,
        taps_grad[:, :inner],
        conv_bc_grad,
        inner_gain_grad,
        norm_gain_grad,
        attn_gain_grad,
        mlp_gain_grad,
    )
    flat = seq_sum(jnp.concatenate([p.reshape(-1, SIDE) for p in pieces], axis=0))
    parts, start = [], 0
    for p in pieces:
        stop = start + p.size // SIDE
        parts.append(flat[start:stop].reshape(p.shape))
        start = stop
    mine = lax.axis_index("seq") * rows
    gain_parts = [lax.dynamic_slice_in_dim(g, mine, rows) for g in parts[5:]]
    return (
        block_out,
        bytes_grad,
        gain_parts[0],
        w_z_grad,
        first_sum[:, :inner],
        first_sum[:, inner : inner + bc_width],
        first_sum[:, inner + bc_width : inner + bc_width + heads],
        w_out_grad,
        gain_parts[1],
        w_qkv_grad[:, :attn_width],
        w_qkv_grad[:, attn_width : 2 * attn_width],
        w_qkv_grad[:, 2 * attn_width :],
        w_o_grad,
        gain_parts[2],
        w_gate_grad,
        w_up_grad,
        w_down_grad,
        parts[0][0, :heads],
        parts[0][1, :heads],
        jnp.sum(parts[1].reshape(heads, inner // heads), axis=1),
        parts[2],
        parts[3],
        parts[4],
    )


def solution(mesh):
    rows, cols, both, rest = P("seq", None), P("seq", "mp"), P("mp", "seq"), P()
    vec, per = P("seq"), P("mp")
    weights = (vec, cols, cols, rows, cols, both, vec, cols, cols, cols, both, vec, cols, cols, both)
    small = (per, per, per, P(None, "mp"), rest, per)
    in_specs = (rows, rows, rest) + weights + small
    out_specs = (rows, rows) + weights + small
    body = functools.partial(local, mesh.shape["seq"])
    return jax.shard_map(body, mesh=mesh, in_specs=in_specs, out_specs=out_specs, check_vma=False)
```

time: 958 us -> 742 us (0.77)
  local copies, waits for them, and re-layouts: 173 us -> 59.9 us
  waiting for transfers between devices: 369 us -> 268 us
  other arithmetic: 160 us -> 61.1 us
  Pallas kernels: 0 us -> 96.9 us
  matrix products: 136 us -> 88.5 us
  starting transfers between devices: 103 us -> 143 us
  between operations: 4.95 us -> 15.8 us
    ppermute x100 -> x48, waiting for transfers between devices: 365 us -> 154 us  [shift(): return lax.ppermute(value, 'seq', self.pairs(dim, by))]
    pallas_call x0 -> x10, Pallas kernels: none -> 96.9 us  [the longest x3 34.7 us: products(): call(functools.partial(products_body, tuple(starts)), 'products', jax.Sha...]
    all_gather x0 -> x2, waiting for transfers between devices: none -> 51.7 us  [gather_plane_off(): lax.all_gather(column, 'seq', axis=1, tiled=False, axis_index_groups=groups)]
    dot_general x50 -> x19, matrix products: 136 us -> 88.5 us  [the longest x7 39.4 us: dot_t(): return rows_rows(left, right)]
    ppermute x4, waiting for transfers between devices: 4.02 us -> 46.8 us  [seq_sum(): lax.ppermute(value, 'seq', [(i, i ^ by) for i in range(count)])]
    convert_element_type x65 -> x15, other arithmetic: 54.5 us -> 12.2 us  [the longest x3 4.34 us: plus(): return sum((t.astype(F32) for t in terms)).astype(BF)]
    ppermute x100 -> x48, starting transfers between devices: 88.8 us -> 129 us  [shift(): return lax.ppermute(value, 'seq', self.pairs(dim, by))]
    another operation x29 -> x11, other arithmetic: 43.4 us -> 2.84 us  [the longest x1 1.36 us: local(): info = jnp.stack([c.astype(F32) for c in columns], axis=1)]
  transfers between devices with their start and end apart: 116 -> 69, of which waited for: 54 -> 34; matrix products, arithmetic and copies ran while one was open for 43% -> 26% of each run, Pallas kernels for 0% -> 8%
where the time goes in v2:
time: 742 us; the launch traced here: 733 us
  waiting for transfers between devices  268 us (36%)
  starting transfers between devices  143 us (19%)
  Pallas kernels  96.9 us (13%)
  matrix products  88.5 us (12%)
  other arithmetic  61.1 us (8%)
  local copies, waits for them, and re-layouts  59.9 us (8%)
  between operations  15.8 us (2%)
    ppermute x48, waiting for transfers between devices, shift(): return lax.ppermute(value, 'seq', self.pairs(dim, by))  154 us
    ppermute x48, starting transfers between devices, shift(): return lax.ppermute(value, 'seq', self.pairs(dim, by))  129 us
    all_gather x2, waiting for transfers between devices, gather_plane_off(): lax.all_gather(column, 'seq', axis=1, tiled=False, axis_index_groups=groups)  51.7 us
    ppermute x4, waiting for transfers between devices, seq_sum(): lax.ppermute(value, 'seq', [(i, i ^ by) for i in range(count)])  46.8 us
    dot_general x7, matrix products, dot_t(): return rows_rows(left, right)  39.4 us
    pallas_call x3, Pallas kernels, products(): call(functools.partial(products_body, tuple(starts)), 'products', jax.Sha...  34.7 us
    dot_general x6, matrix products, plane_major(): return rows_rows(pick, values).astype(BF)  28.7 us
    dot_general x6, matrix products, bf_dot(): return rows_cols(left, right)  20.4 us
  transfers between devices with their start and end apart: 69, of which 34 were waited for; matrix products, arithmetic and copies ran while one was open for 26% of the time, Pallas kernels for 8%

profile of v2, /device:TPU:0, one launch (start us, length us, event | category | flops | bytes accessed | tf_op | source)
XLA Modules:
  0.0 733.1 jit_solution(1108457080492903213)
XLA Ops:
  51.5 6.9 collective-permute-done.7
  64.4 7.8 %collective-permute-done.21 = bf16[64,4096]{1,0:T(8,128)(2,1)S(1)} collective-permute-done((bf16[64,4096]{1,0:T(8,128)(2,1)}, bf16[64,4096]{1,0:T(8,128)(2,1)S(1)}, u32[]{:S(2)}, u32[]{:S(2)}) %collective-permute-start.21) | collective-permute-done | bytes 524320 | tf_op jit(solution)/shard_map/ppermute | solution.py:46
  91.3 13.5 %collective-permute-start.14 = (f32[2,2,16]{2,1,0:T(2,128)S(1)}, f32[2,2,16]{2,1,0:T(2,128)S(1)}, u32[]{:S(2)}, u32[]{:S(2)}) collective-permute-start(f32[2,2,16]{2,1,0:T(2,128)S(1)} %get-tuple-element.292), channel_id=1, source_target_pairs={{0,24},{2,26},{4,28},{6,30},{8,0},{10,2},{12,4},{14,6},{16,8},{18,... | collective-permute-start | bytes 776 | tf_op jit(solution)/shard_map/ppermute | solution.py:46
  110.8 26.8 %collective-permute-done.13 = f32[2,2,16]{2,1,0:T(2,128)S(1)} collective-permute-done((f32[2,2,16]{2,1,0:T(2,128)S(1)}, f32[2,2,16]{2,1,0:T(2,128)S(1)}, u32[]{:S(2)}, u32[]{:S(2)}) %collective-permute-start.13) | collective-permute-done | bytes 288 | tf_op jit(solution)/shard_map/ppermute | solution.py:46
  152.5 9.3 %collective-permute-done.15 = bf16[16,64,128]{2,1,0:T(8,128)(2,1)S(1)} collective-permute-done((bf16[16,64,128]{2,1,0:T(8,128)(2,1)S(1)}, bf16[16,64,128]{2,1,0:T(8,128)(2,1)S(1)}, u32[]{:S(2)}, u32[]{:S(2)}) %collective-permute-start.15) | collective-permute-done | bytes 262176 | tf_op jit(solution)/shard_map/ppermute | solution.py:46
  163.0 13.4 %collective-permute-start.16 = (bf16[16,64,128]{2,1,0:T(8,128)(2,1)S(1)}, bf16[16,64,128]{2,1,0:T(8,128)(2,1)S(1)}, u32[]{:S(2)}, u32[]{:S(2)}) collective-permute-start(bf16[16,64,128]{2,1,0:T(8,128)(2,1)S(1)} %fusion.88), channel_id=1, source_target_pairs={{0,4},{2,6},{4,0},{6,2},{8,12},{10,14},{12,8},{14,10},{16,20},{18,... | collective-permute-start | bytes 786440 | tf_op jit(solution)/shard_map/ppermute | solution.py:46
  186.3 16.1 %collective-permute-start.18 = (bf16[16,64,128]{2,1,0:T(8,128)(2,1)S(1)}, bf16[16,64,128]{2,1,0:T(8,128)(2,1)S(1)}, u32[]{:S(2)}, u32[]{:S(2)}) collective-permute-start(bf16[16,64,128]{2,1,0:T(8,128)(2,1)S(1)} %fusion.71), channel_id=1, source_target_pairs={{0,16},{2,18},{4,20},{6,22},{8,24},{10,26},{12,28},{14,30},{16,0},... | collective-permute-start | bytes 786440 | tf_op jit(solution)/shard_map/ppermute | solution.py:46
  205.0 13.1 %collective-permute-done.18 = bf16[16,64,128]{2,1,0:T(8,128)(2,1)S(1)} collective-permute-done((bf16[16,64,128]{2,1,0:T(8,128)(2,1)S(1)}, bf16[16,64,128]{2,1,0:T(8,128)(2,1)S(1)}, u32[]{:S(2)}, u32[]{:S(2)}) %collective-permute-start.18) | collective-permute-done | bytes 262176 | tf_op jit(solution)/shard_map/ppermute | solution.py:46
  234.0 7.1 convolution_convert_fusion.1.qkv
  241.1 8.6 %attend.1.refs_3_ = bf16[1024,512]{1,0:T(8,128)(2,1)} custom-call(bf16[1024,1536]{1,0:T(8,128)(2,1)} %convolution_convert_fusion.1.qkv), custom_call_target="tpu_custom_call" | custom-call | flops 536870912 | bytes 4194304 | tf_op jit(solution)/shard_map/attend/pallas_call | solution.py:323
  268.9 51.7 %all-gather.7.cloned.1.call-done = bf16[4,256,6144]{2,1,0:T(8,128)(2,1)} async-done(((bf16[4,64,6144]{2,1,0:T(8,128)(2,1)}), bf16[4,256,6144]{2,1,0:T(8,128)(2,1)}) %all-gather.7.cloned.1.call-update) | async-done | bytes 12582928 | tf_op jit(solution)/shard_map/all_gather | solution.py:78
  320.6 19.2 %middle.1 = (bf16[1024,2048]{1,0:T(8,128)(2,1)}, bf16[1024,4096]{1,0:T(8,128)(2,1)}) custom-call(bf16[1024,1024]{1,0:T(8,128)(2,1)} %copy-done.22, bf16[1024,1024]{1,0:T(8,128)(2,1)} %grad.1, bf16[1024,6144]{1,0:T(8,128)(2,1)} %bitcast.309, bf16[1024,6144]{1,0:T(8,128)(2,1)} %bitcast.310), custom_call_target="tpu_custom_call" | custom-call | flops 12884901888 | bytes 29360128 | tf_op jit(solution)/shard_map/middle/pallas_call | solution.py:395
  339.8 21.1 %products.3 = bf16[1024,6144]{1,0:T(8,128)(2,1)} custom-call(bf16[1024,1024]{1,0:T(8,128)(2,1)} %convolution_convert_fusion.6.refs_0_, bf16[1024,4096]{1,0:T(8,128)(2,1)} %get-tuple-element.74.refs_1_, bf16[1024,1024]{1,0:T(8,128)(2,1)} %convolution_convert_fusion.5.refs_2_, bf16[1024,2048]{1,0:T(8,128)(2,1)} %get-tuple-element.72.refs_3_), custom_call_target="tpu_custom_call" | custom-call | flops 12884901888 | bytes 29360128 | tf_op jit(solution)/shard_map/products/pallas_call | solution.py:441
  361.0 14.3 %fusion.36 = bf16[1024,1024]{1,0:T(8,128)(2,1)S(1)} fusion(bf16[1024,4096]{1,0:T(8,128)(2,1)} %get-tuple-element.74.refs_1_, bf16[1024,6144]{1,0:T(8,128)(2,1)} %bitcast.311), kind=kOutput, calls=%fused_computation.57 | convolution fusion | flops 8590983168 | bytes 18874368 | tf_op jit(solution)/shard_map/dot_general | solution.py:716
  375.4 7.1 fusion.33
  398.9 12.5 %attend_back.1.refs_1_ = bf16[1024,1536]{1,0:T(8,128)(2,1)} custom-call(bf16[1024,1536]{1,0:T(8,128)(2,1)} %convolution_convert_fusion.1.qkv, bf16[1024,512]{1,0:T(8,128)(2,1)} %convolution_convert_fusion.7.grad), custom_call_target="tpu_custom_call" | custom-call | flops 1342177280 | bytes 7340032 | tf_op jit(solution)/shard_map/attend_back/pallas_call | solution.py:366
  411.4 7.1 convolution_convert_fusion.3.refs_2_
  418.5 9.4 %products.4 = bf16[1024,2048]{1,0:T(8,128)(2,1)} custom-call(bf16[1024,1024]{1,0:T(8,128)(2,1)} %convolution_convert_fusion.4.refs_0_, bf16[1024,1536]{1,0:T(8,128)(2,1)} %attend_back.1.refs_1_, bf16[1024,1024]{1,0:T(8,128)(2,1)} %convolution_convert_fusion.3.refs_2_, bf16[1024,512]{1,0:T(8,128)(2,1)} %attend.1.refs_3_), custom_call_target="tpu_custom_call" | custom-call | flops 4294967296 | bytes 12582912 | tf_op jit(solution)/shard_map/products/pallas_call | solution.py:441
  427.9 6.4 fusion.30
  461.8 13.0 %collective-permute-done.33 = bf16[16,64,128]{2,1,0:T(8,128)(2,1)S(1)} collective-permute-done((bf16[16,64,128]{2,1,0:T(8,128)(2,1)S(1)}, bf16[16,64,128]{2,1,0:T(8,128)(2,1)S(1)}, u32[]{:S(2)}, u32[]{:S(2)}) %collective-permute-start.33) | collective-permute-done | bytes 262176 | tf_op jit(solution)/shard_map/ppermute | solution.py:46
  476.5 9.0 %collective-permute-done.34 = bf16[16,64,128]{2,1,0:T(8,128)(2,1)S(1)} collective-permute-done((bf16[16,64,128]{2,1,0:T(8,128)(2,1)S(1)}, bf16[16,64,128]{2,1,0:T(8,128)(2,1)S(1)}, u32[]{:S(2)}, u32[]{:S(2)}) %collective-permute-start.34) | collective-permute-done | bytes 262176 | tf_op jit(solution)/shard_map/ppermute | solution.py:46
  497.5 15.7 %collective-permute-done.36 = bf16[16,64,128]{2,1,0:T(8,128)(2,1)S(1)} collective-permute-done((bf16[16,64,128]{2,1,0:T(8,128)(2,1)S(1)}, bf16[16,64,128]{2,1,0:T(8,128)(2,1)S(1)}, u32[]{:S(2)}, u32[]{:S(2)}) %collective-permute-start.36) | collective-permute-done | bytes 262176 | tf_op jit(solution)/shard_map/ppermute | solution.py:46
  514.3 10.0 %unmix.1 = (f32[136,1280]{1,0:T(8,128)}, f32[128,128]{1,0:T(8,128)}, f32[4,1280]{1,0:T(4,128)}, f32[8,128]{1,0:T(8,128)}, f32[1,1024]{1,0:T(1,128)}) custom-call(bf16[8,1280]{1,0:T(8,128)(2,1)} %pad.21.rim, bf16[128,1280]{1,0:T(8,128)(2,1)} %slice.279.mixed, f32[128,128]{1,0:T(8,128)} %slice.280.raw, f32[8,128]{1,0:T(8,128)} %select_maximum_fusion.small, ...), custom_call_target="tpu_custom_call" | custom-call | flops 1610612736 | bytes 3932160 | tf_op jit(solution)/shard_map/unmix/pallas_call | solution.py:688
  536.9 6.3 reduce-scatter.6.cloned.1.call-done
  569.0 11.4 %collective-permute-done.43 = f32[82,128]{1,0:T(8,128)S(1)} collective-permute-done((f32[82,128]{1,0:T(8,128)S(1)}, f32[82,128]{1,0:T(8,128)S(1)}, u32[]{:S(2)}, u32[]{:S(2)}) %collective-permute-start.43) | collective-permute-done | bytes 42016 | tf_op jit(solution)/shard_map/ppermute | solution.py:178
  587.9 18.1 %collective-permute-done.44 = f32[82,128]{1,0:T(8,128)S(1)} collective-permute-done((f32[82,128]{1,0:T(8,128)S(1)}, f32[82,128]{1,0:T(8,128)S(1)}, u32[]{:S(2)}, u32[]{:S(2)}) %collective-permute-start.44) | collective-permute-done | bytes 42016 | tf_op jit(solution)/shard_map/ppermute | solution.py:178
  611.4 12.8 %collective-permute-done.45 = f32[82,128]{1,0:T(8,128)S(1)} collective-permute-done((f32[82,128]{1,0:T(8,128)S(1)}, f32[82,128]{1,0:T(8,128)S(1)}, u32[]{:S(2)}, u32[]{:S(2)}) %collective-permute-start.45) | collective-permute-done | bytes 42016 | tf_op jit(solution)/shard_map/ppermute | solution.py:178
  654.8 5.8 collective-permute-done.54
  675.2 7.2 collective-permute-done.56
  691.5 7.3 collective-permute-start.47
  700.8 13.5 %collective-permute-done.59 = bf16[64,2048]{1,0:T(8,128)(2,1)S(1)} collective-permute-done((bf16[64,2048]{1,0:T(8,128)(2,1)S(1)}, bf16[64,2048]{1,0:T(8,128)(2,1)S(1)}, u32[]{:S(2)}, u32[]{:S(2)}) %collective-permute-start.59) | collective-permute-done | bytes 262176 | tf_op jit(solution)/shard_map/ppermute | solution.py:46
  716.2 8.1 %collective-permute-done.47 = bf16[64,2048]{1,0:T(8,128)(2,1)S(1)} collective-permute-done((bf16[64,2048]{1,0:T(8,128)(2,1)S(1)}, bf16[64,2048]{1,0:T(8,128)(2,1)S(1)}, u32[]{:S(2)}, u32[]{:S(2)}) %collective-permute-start.47) | collective-permute-done | bytes 262176 | tf_op jit(solution)/shard_map/ppermute | solution.py:46
  (458 shorter events, 307.7 us)
Async XLA Ops:
  7.2 178.8 %all-gather.5.cloned.1.call-start = ((), (), s32[]{:S(2)}) async-start(), calls=%async_computation.6 | async-start | bytes 10485760 | tf_op jit(solution)/shard_map/all_gather | solution.py:78
  34.2 30.3 %collective-permute-start.20 = (bf16[64,4096]{1,0:T(8,128)(2,1)}, bf16[64,4096]{1,0:T(8,128)(2,1)S(1)}, u32[]{:S(2)}, u32[]{:S(2)}) collective-permute-start(bf16[64,4096]{1,0:T(8,128)(2,1)} %bitcast_dynamic-update-slice_fusion.13), channel_id=1, source_target_pairs={{0,8},{2,10},{4,12},{6,14},{8,16},{10,18},{12,20},{14,22},{16,24},... | collective-permute-start | bytes 1572872 | tf_op jit(solution)/shard_map/ppermute | solution.py:46
  41.4 30.9 %collective-permute-start.21 = (bf16[64,4096]{1,0:T(8,128)(2,1)}, bf16[64,4096]{1,0:T(8,128)(2,1)S(1)}, u32[]{:S(2)}, u32[]{:S(2)}) collective-permute-start(bf16[64,4096]{1,0:T(8,128)(2,1)} %bitcast_dynamic-update-slice_fusion.13), channel_id=1, source_target_pairs={{0,16},{2,18},{4,20},{6,22},{8,24},{10,26},{12,28},{14,30},{16,0},... | collective-permute-start | bytes 1572872 | tf_op jit(solution)/shard_map/ppermute | solution.py:46
  44.7 27.6 %collective-permute-start.22 = (bf16[64,4096]{1,0:T(8,128)(2,1)}, bf16[64,4096]{1,0:T(8,128)(2,1)S(1)}, u32[]{:S(2)}, u32[]{:S(2)}) collective-permute-start(bf16[64,4096]{1,0:T(8,128)(2,1)} %bitcast_dynamic-update-slice_fusion.13), channel_id=1, source_target_pairs={{0,24},{2,26},{4,28},{6,30},{8,0},{10,2},{12,4},{14,6},{16,8},{18,... | collective-permute-start | bytes 1572872 | tf_op jit(solution)/shard_map/ppermute | solution.py:46
  73.8 246.8 %all-gather.7.cloned.1.call-start = ((), (), s32[]{:S(2)}) async-start(), calls=%async_computation.7 | async-start | bytes 15728640 | tf_op jit(solution)/shard_map/all_gather | solution.py:78
  104.9 32.7 %collective-permute-start.13 = (f32[2,2,16]{2,1,0:T(2,128)S(1)}, f32[2,2,16]{2,1,0:T(2,128)S(1)}, u32[]{:S(2)}, u32[]{:S(2)}) collective-permute-start(f32[2,2,16]{2,1,0:T(2,128)S(1)} %get-tuple-element.292), channel_id=1, source_target_pairs={{0,16},{2,18},{4,20},{6,22},{8,24},{10,26},{12,28},{14,30},{16,0},... | collective-permute-start | bytes 776 | tf_op jit(solution)/shard_map/ppermute | solution.py:46
  104.9 76.1 %collective-permute-start.26 = (bf16[64,6144]{1,0:T(8,128)(2,1)S(1)}, bf16[64,6144]{1,0:T(8,128)(2,1)S(1)}, u32[]{:S(2)}, u32[]{:S(2)}) collective-permute-start(bf16[64,6144]{1,0:T(8,128)(2,1)S(1)} %pad_maximum_fusion.1), channel_id=1, source_target_pairs={{0,8},{2,10},{4,12},{6,14},{8,16},{10,18},{12,20},{14,22},{16,24},... | collective-permute-start | bytes 2359304 | tf_op jit(solution)/shard_map/ppermute | solution.py:46
  105.5 35.8 %collective-permute-start.12 = (f32[2,2,16]{2,1,0:T(2,128)S(1)}, f32[2,2,16]{2,1,0:T(2,128)S(1)}, u32[]{:S(2)}, u32[]{:S(2)}) collective-permute-start(f32[2,2,16]{2,1,0:T(2,128)S(1)} %get-tuple-element.292), channel_id=1, source_target_pairs={{0,8},{2,10},{4,12},{6,14},{8,16},{10,18},{12,20},{14,22},{16,24},... | collective-permute-start | bytes 776 | tf_op jit(solution)/shard_map/ppermute | solution.py:46
  108.4 72.6 %collective-permute-start.27 = (bf16[64,6144]{1,0:T(8,128)(2,1)S(1)}, bf16[64,6144]{1,0:T(8,128)(2,1)}, u32[]{:S(2)}, u32[]{:S(2)}) collective-permute-start(bf16[64,6144]{1,0:T(8,128)(2,1)S(1)} %pad_maximum_fusion.1), channel_id=1, source_target_pairs={{0,16},{2,18},{4,20},{6,22},{8,24},{10,26},{12,28},{14,30},{16,0},... | collective-permute-start | bytes 2359304 | tf_op jit(solution)/shard_map/ppermute | solution.py:46
  109.3 71.7 %collective-permute-start.28 = (bf16[64,6144]{1,0:T(8,128)(2,1)S(1)}, bf16[64,6144]{1,0:T(8,128)(2,1)}, u32[]{:S(2)}, u32[]{:S(2)}) collective-permute-start(bf16[64,6144]{1,0:T(8,128)(2,1)S(1)} %pad_maximum_fusion.1), channel_id=1, source_target_pairs={{0,24},{2,26},{4,28},{6,30},{8,0},{10,2},{12,4},{14,6},{16,8},{18,... | collective-permute-start | bytes 2359304 | tf_op jit(solution)/shard_map/ppermute | solution.py:46
  186.1 301.2 %reduce-scatter.4.cloned.1.call-start = ((), (), s32[]{:S(2)}) async-start(), calls=%async_computation.3 | async-start | bytes 15728640 | tf_op jit(solution)/shard_map/reduce_scatter | solution.py:123
  186.2 18.8 %collective-permute-start.19 = (bf16[16,64,128]{2,1,0:T(8,128)(2,1)S(1)}, bf16[16,64,128]{2,1,0:T(8,128)(2,1)S(1)}, u32[]{:S(2)}, u32[]{:S(2)}) collective-permute-start(bf16[16,64,128]{2,1,0:T(8,128)(2,1)S(1)} %fusion.71), channel_id=1, source_target_pairs={{0,24},{2,26},{4,28},{6,30},{8,0},{10,2},{12,4},{14,6},{16,8},{18,... | collective-permute-start | bytes 786440 | tf_op jit(solution)/shard_map/ppermute | solution.py:46
  186.3 31.9 %collective-permute-start.18 = (bf16[16,64,128]{2,1,0:T(8,128)(2,1)S(1)}, bf16[16,64,128]{2,1,0:T(8,128)(2,1)S(1)}, u32[]{:S(2)}, u32[]{:S(2)}) collective-permute-start(bf16[16,64,128]{2,1,0:T(8,128)(2,1)S(1)} %fusion.71), channel_id=1, source_target_pairs={{0,16},{2,18},{4,20},{6,22},{8,24},{10,26},{12,28},{14,30},{16,0},... | collective-permute-start | bytes 786440 | tf_op jit(solution)/shard_map/ppermute | solution.py:46
  360.9 182.3 %reduce-scatter.6.cloned.1.call-start = ((), (), s32[]{:S(2)}) async-start(), calls=%async_computation.4 | async-start | bytes 5242880 | tf_op jit(solution)/shard_map/reduce_scatter | solution.py:123
  487.3 197.2 %reduce-scatter.8.cloned.1.call-start = ((), (), s32[]{:S(2)}) async-start(), calls=%async_computation.5 | async-start | bytes 5242880 | tf_op jit(solution)/shard_map/reduce_scatter | solution.py:123
  490.7 22.5 %collective-permute-start.36 = (bf16[16,64,128]{2,1,0:T(8,128)(2,1)S(1)}, bf16[16,64,128]{2,1,0:T(8,128)(2,1)S(1)}, u32[]{:S(2)}, u32[]{:S(2)}) collective-permute-start(bf16[16,64,128]{2,1,0:T(8,128)(2,1)S(1)} %fusion.77), channel_id=1, source_target_pairs={{0,16},{2,18},{4,20},{6,22},{8,24},{10,26},{12,28},{14,30},{16,0},... | collective-permute-start | bytes 786440 | tf_op jit(solution)/shard_map/ppermute | solution.py:46
  490.7 22.5 %collective-permute-start.35 = (bf16[16,64,128]{2,1,0:T(8,128)(2,1)S(1)}, bf16[16,64,128]{2,1,0:T(8,128)(2,1)S(1)}, u32[]{:S(2)}, u32[]{:S(2)}) collective-permute-start(bf16[16,64,128]{2,1,0:T(8,128)(2,1)S(1)} %fusion.77), channel_id=1, source_target_pairs={{0,8},{2,10},{4,12},{6,14},{8,16},{10,18},{12,20},{14,22},{16,24},... | collective-permute-start | bytes 786440 | tf_op jit(solution)/shard_map/ppermute | solution.py:46
  550.5 79.9 %collective-permute-start.63 = (bf16[64,6144]{1,0:T(8,128)(2,1)}, bf16[64,6144]{1,0:T(8,128)(2,1)}, u32[]{:S(2)}, u32[]{:S(2)}) collective-permute-start(bf16[64,6144]{1,0:T(8,128)(2,1)} %get-tuple-element.250), channel_id=1, source_target_pairs={{0,24},{2,26},{4,28},{6,30},{8,0},{10,2},{12,4},{14,6},{16,8},{18,... | collective-permute-start | bytes 2359304 | tf_op jit(solution)/shard_map/ppermute | solution.py:46
  553.6 77.4 %collective-permute-start.62 = (bf16[64,6144]{1,0:T(8,128)(2,1)}, bf16[64,6144]{1,0:T(8,128)(2,1)}, u32[]{:S(2)}, u32[]{:S(2)}) collective-permute-start(bf16[64,6144]{1,0:T(8,128)(2,1)} %get-tuple-element.251), channel_id=1, source_target_pairs={{0,16},{2,18},{4,20},{6,22},{8,24},{10,26},{12,28},{14,30},{16,0},... | collective-permute-start | bytes 2359304 | tf_op jit(solution)/shard_map/ppermute | solution.py:46
  553.6 78.9 %collective-permute-start.61 = (bf16[64,6144]{1,0:T(8,128)(2,1)}, bf16[64,6144]{1,0:T(8,128)(2,1)}, u32[]{:S(2)}, u32[]{:S(2)}) collective-permute-start(bf16[64,6144]{1,0:T(8,128)(2,1)} %get-tuple-element.249), channel_id=1, source_target_pairs={{0,8},{2,10},{4,12},{6,14},{8,16},{10,18},{12,20},{14,22},{16,24},... | collective-permute-start | bytes 2359304 | tf_op jit(solution)/shard_map/ppermute | solution.py:46
  559.5 47.9 %collective-permute-start.49 = (bf16[128,1408]{1,0:T(8,128)(2,1)}, bf16[128,1408]{1,0:T(8,128)(2,1)}, u32[]{:S(2)}, u32[]{:S(2)}) collective-permute-start(bf16[128,1408]{1,0:T(8,128)(2,1)} %get-tuple-element.254), channel_id=1, source_target_pairs={{0,4},{2,6},{4,0},{6,2},{8,12},{10,14},{12,8},{14,10},{16,20},{18,... | collective-permute-start | bytes 1081352 | tf_op jit(solution)/shard_map/ppermute | solution.py:46
  580.4 25.6 %collective-permute-start.44 = (f32[82,128]{1,0:T(8,128)S(1)}, f32[82,128]{1,0:T(8,128)S(1)}, u32[]{:S(2)}, u32[]{:S(2)}) collective-permute-start(f32[82,128]{1,0:T(8,128)S(1)} %add.584), channel_id=1, source_target_pairs={{0,8},{2,10},{4,12},{6,14},{8,0},{10,2},{12,4},{14,6},{16,24},{18,... | collective-permute-start | bytes 125960 | tf_op jit(solution)/shard_map/ppermute | solution.py:178
  606.0 40.4 %collective-permute-start.51 = (bf16[128,1408]{1,0:T(8,128)(2,1)}, bf16[128,1408]{1,0:T(8,128)(2,1)}, u32[]{:S(2)}, u32[]{:S(2)}) collective-permute-start(bf16[128,1408]{1,0:T(8,128)(2,1)} %get-tuple-element.255), channel_id=1, source_target_pairs={{0,4},{2,6},{4,0},{6,2},{8,12},{10,14},{12,8},{14,10},{16,20},{18,... | collective-permute-start | bytes 1081352 | tf_op jit(solution)/shard_map/ppermute | solution.py:46
  624.2 22.3 %collective-permute-start.53 = (bf16[128,1408]{1,0:T(8,128)(2,1)}, bf16[128,1408]{1,0:T(8,128)(2,1)}, u32[]{:S(2)}, u32[]{:S(2)}) collective-permute-start(bf16[128,1408]{1,0:T(8,128)(2,1)} %get-tuple-element.256), channel_id=1, source_target_pairs={{0,2},{2,0},{4,6},{6,4},{8,10},{10,8},{12,14},{14,12},{16,18},{18,... | collective-permute-start | bytes 1081352 | tf_op jit(solution)/shard_map/ppermute | solution.py:46
  630.4 24.4 %collective-permute-start.52 = (bf16[128,1408]{1,0:T(8,128)(2,1)S(1)}, bf16[128,1408]{1,0:T(8,128)(2,1)}, u32[]{:S(2)}, u32[]{:S(2)}) collective-permute-start(bf16[128,1408]{1,0:T(8,128)(2,1)S(1)} %get-tuple-element.257), channel_id=1, source_target_pairs={{0,2},{2,0},{4,6},{6,4},{8,10},{10,8},{12,14},{14,12},{16,18},{18,... | collective-permute-start | bytes 1081352 | tf_op jit(solution)/shard_map/ppermute | solution.py:46
  631.0 19.0 %collective-permute-start.50 = (bf16[128,1408]{1,0:T(8,128)(2,1)}, bf16[128,1408]{1,0:T(8,128)(2,1)}, u32[]{:S(2)}, u32[]{:S(2)}) collective-permute-start(bf16[128,1408]{1,0:T(8,128)(2,1)} %fusion.60), channel_id=1, source_target_pairs={{0,2},{2,0},{4,6},{6,4},{8,10},{10,8},{12,14},{14,12},{16,18},{18,... | collective-permute-start | bytes 1081352 | tf_op jit(solution)/shard_map/ppermute | solution.py:46
  666.3 32.5 %collective-permute-start.60 = (bf16[64,2048]{1,0:T(8,128)(2,1)S(1)}, bf16[64,2048]{1,0:T(8,128)(2,1)S(1)}, u32[]{:S(2)}, u32[]{:S(2)}) collective-permute-start(bf16[64,2048]{1,0:T(8,128)(2,1)S(1)} %get-tuple-element.263), channel_id=1, source_target_pairs={{0,24},{2,26},{4,28},{6,30},{8,0},{10,2},{12,4},{14,6},{16,8},{18,... | collective-permute-start | bytes 786440 | tf_op jit(solution)/shard_map/ppermute | solution.py:46
  669.6 44.7 %collective-permute-start.59 = (bf16[64,2048]{1,0:T(8,128)(2,1)S(1)}, bf16[64,2048]{1,0:T(8,128)(2,1)S(1)}, u32[]{:S(2)}, u32[]{:S(2)}) collective-permute-start(bf16[64,2048]{1,0:T(8,128)(2,1)S(1)} %get-tuple-element.264), channel_id=1, source_target_pairs={{0,16},{2,18},{4,20},{6,22},{8,24},{10,26},{12,28},{14,30},{16,0},... | collective-permute-start | bytes 786440 | tf_op jit(solution)/shard_map/ppermute | solution.py:46
  670.7 43.6 %collective-permute-start.58 = (bf16[64,2048]{1,0:T(8,128)(2,1)S(1)}, bf16[64,2048]{1,0:T(8,128)(2,1)S(1)}, u32[]{:S(2)}, u32[]{:S(2)}) collective-permute-start(bf16[64,2048]{1,0:T(8,128)(2,1)S(1)} %get-tuple-element.262), channel_id=1, source_target_pairs={{0,8},{2,10},{4,12},{6,14},{8,16},{10,18},{12,20},{14,22},{16,24},... | collective-permute-start | bytes 786440 | tf_op jit(solution)/shard_map/ppermute | solution.py:46
  685.7 30.5 %collective-permute-start.48 = (bf16[64,2048]{1,0:T(8,128)(2,1)S(1)}, bf16[64,2048]{1,0:T(8,128)(2,1)S(1)}, u32[]{:S(2)}, u32[]{:S(2)}) collective-permute-start(bf16[64,2048]{1,0:T(8,128)(2,1)S(1)} %get-tuple-element.266), channel_id=1, source_target_pairs={{0,24},{2,26},{4,28},{6,30},{8,0},{10,2},{12,4},{14,6},{16,8},{18,... | collective-permute-start | bytes 786440 | tf_op jit(solution)/shard_map/ppermute | solution.py:46
  691.5 32.8 %collective-permute-start.47 = (bf16[64,2048]{1,0:T(8,128)(2,1)S(1)}, bf16[64,2048]{1,0:T(8,128)(2,1)S(1)}, u32[]{:S(2)}, u32[]{:S(2)}) collective-permute-start(bf16[64,2048]{1,0:T(8,128)(2,1)S(1)} %get-tuple-element.267), channel_id=1, source_target_pairs={{0,16},{2,18},{4,20},{6,22},{8,24},{10,26},{12,28},{14,30},{16,0},... | collective-permute-start | bytes 786440 | tf_op jit(solution)/shard_map/ppermute | solution.py:46
  698.8 25.4 %collective-permute-start.46 = (bf16[64,2048]{1,0:T(8,128)(2,1)S(1)}, bf16[64,2048]{1,0:T(8,128)(2,1)S(1)}, u32[]{:S(2)}, u32[]{:S(2)}) collective-permute-start(bf16[64,2048]{1,0:T(8,128)(2,1)S(1)} %get-tuple-element.265), channel_id=1, source_target_pairs={{0,8},{2,10},{4,12},{6,14},{8,16},{10,18},{12,20},{14,22},{16,24},... | collective-permute-start | bytes 786440 | tf_op jit(solution)/shard_map/ppermute | solution.py:46
  (98 other events, 1573.6 us)
Sparse Core Ops, SparseCore 0:
  73.9 104.4 all-gather.4
  186.2 134.3 all-gather.6
  361.0 126.1 reduce-scatter.3
  490.1 53.0 reduce-scatter.5
  546.3 60.9 reduce-scatter.7

commit v3 on v2

--- a/solution.py
+++ b/solution.py
@@ -212,6 +212,8 @@
         if event is not None and dim == levels[-1]:
             total = follow(total, event)
         low = total.astype(BF)
+        if dim == levels[-1]:
+            crossed = (crossed, low)
         summed = None
         for k in range(n):
             other = (me - k) % n
@@ -830,7 +832,7 @@
     table = spread_small(grid, info[patch_rows - 1, taps] * jnp.exp(whole))
     known = (rim, mixed, raw, small, skip, conv_x, conv_bc, info, seg)
     y_part, c_rows, decay_in, state_own = mix(*known)
-    state_in, crossed = scan_states(grid, table, state_own, False)
+    state_in, (crossed, _) = scan_states(grid, table, state_own, False)
     mlp_column = gather_column(grid, follow(mlp, first_all, second_column), crossed)
     mlp_all = gather_plane_off(grid, follow(mlp_column, second_all)).reshape(model_width, -1)
     down_all, pair_all = mlp_all[:, :ff], mlp_all[:, ff:]
@@ -868,14 +870,6 @@
     after_low = after_grad.astype(BF)
     attended_grad = bf_dot(after_low, wo_all).astype(BF)
     qkv_grad = attend_back(qkv, attended_grad)
-    third_part = products(
-        (
-            (plane_major(grid, normed), qkv_grad),
-            (plane_major(grid, after_low), attended),
-        ),
-        attn_width,
-    )
-    qkv_grad = follow(qkv_grad, third_part)
     attn_norm_grad = mp_sum(dot_t(qkv_grad, qkv_all))
     attn_in_grad, attn_gain_grad = norm_back(attn_norm_grad, rows_in, rstd_attn, attn_row)
     rows_grad = after_grad + attn_in_grad
@@ -891,10 +885,21 @@
         y_norm_grad, gated, y_full, gate_z, inner_gain[None, :], stats, decay_in, c_rows
     )
     h_norm_t = plane_major(grid, h_norm)
-    second_part = products(((h_norm_t, z_low), (plane_major(grid, patch_low), y_norm)), inner)
-    state_in_grad = follow(state_in_grad, second_part)
-    state_grad, crossed = scan_states(grid, table, state_in_grad, True, mlp_plane)
-    third_plane = scatter_plane(grid, follow(third_part, mlp_plane, crossed))
+    rest_part = products(
+        (
+            (plane_major(grid, normed), qkv_grad),
+            (plane_major(grid, after_low), attended),
+            (h_norm_t, z_low),
+            (plane_major(grid, patch_low), y_norm),
+        ),
+        attn_width,
+    )
+    state_in_grad = follow(state_in_grad, rest_part)
+    state_grad, (crossed, sent) = scan_states(grid, table, state_in_grad, True, mlp_plane)
+    rest_plane = scatter_plane(grid, follow(rest_part, mlp_plane, crossed))
+    mlp_sums = [
+        scatter_column(grid, follow(mlp_plane[:, i : i + ff], sent)) for i in (0, ff, 2 * ff)
+    ]
     ext_grad, raw_grad, taps_grad, heads_grad, skip_grad = unmix(
         *known, y_grad, state_in, state_grad
     )
@@ -908,28 +913,33 @@
         ext_full[8:] + jnp.pad(rim_back, ((patch_rows - (taps - 1), 0), (0, 0)))
     ).astype(BF)
     first_grad = jnp.concatenate([mixed_low, raw_grad.astype(BF)], axis=1)
+    first_grad = follow(first_grad, mlp_sums[0])
     first_part = bf_dot(h_norm_t, first_grad).astype(BF)
     first_grad = follow(first_grad, first_part)
-    second_plane = scatter_plane(grid, follow(second_part, third_plane, first_part))
-    first_plane = scatter_plane_near(grid, first_part)
+    first_plane = scatter_plane(grid, follow(first_part, rest_plane))
     lane = lax.broadcasted_iota(jnp.int32, (1, first_grad.shape[1]), 1)
     twice = (lane >= inner) & (lane < inner + bc_width) & (lax.axis_index("mp") > 0)
+    cut = 4 * attn_width
+    rest_sums = [
+        scatter_column(grid, part) for part in (rest_plane[:, :cut], rest_plane[:, cut:])
+    ]
+    first_grad = follow(first_grad, mlp_sums[1])
     own_grad = jnp.where(twice, jnp.zeros_like(first_grad), first_grad)
     h_grad = mp_sum(dot_t(own_grad, first_all) + dot_t(z_low, z_all))
     patch_in_grad, norm_gain_grad = norm_back(h_grad, patch_in, rstd_patch, norm_row)
-    patch_total = patch_grad + patch_in_grad
+    patch_total = follow(patch_grad + patch_in_grad, rest_sums[1])
     bytes_grad = rows_grad + jnp.repeat(patch_total / PATCH, PATCH, axis=0)
 
-    mlp_sum = scatter_column(grid, follow(mlp_plane, state_grad))
-    pair_sum = mlp_sum[:, : 2 * ff].reshape(rows, ff // step, 2, step)
+    pair_sum = jnp.concatenate(mlp_sums[:2], axis=1).reshape(rows, ff // step, 2, step)
     w_gate_grad = pair_sum[:, :, 0].reshape(rows, ff)
     w_up_grad = pair_sum[:, :, 1].reshape(rows, ff)
-    w_down_grad = mlp_sum[:, 2 * ff :].T
-    third_sum = scatter_column(grid, third_plane)
-    w_qkv_grad, w_o_grad = third_sum[:, : 3 * attn_width], third_sum[:, 3 * attn_width :].T
-    second_sum = scatter_column(grid, second_plane)
-    w_z_grad, w_out_grad = second_sum[:, :inner], second_sum[:, inner:].T
+    w_down_grad = mlp_sums[2].T
     first_sum = scatter_column(grid, first_plane)
+    w_qkv_grad, w_o_grad = (
+        rest_sums[0][:, : 3 * attn_width],
+        rest_sums[0][:, 3 * attn_width :].T,
+    )
+    w_z_grad, w_out_grad = rest_sums[1][:, :inner], rest_sums[1][:, inner:].T
 
     pieces = (
         heads_grad[:2],

time: 742 us -> 714 us (0.962)
  waiting for transfers between devices: 268 us -> 237 us
  starting transfers between devices: 143 us -> 156 us
    ppermute x4, waiting for transfers between devices: 46.8 us -> 6.52 us  [seq_sum(): lax.ppermute(value, 'seq', [(i, i ^ by) for i in range(count)])]
    ppermute x48, waiting for transfers between devices: 154 us -> 168 us  [shift(): return lax.ppermute(value, 'seq', self.pairs(dim, by))]
    ppermute x48, starting transfers between devices: 129 us -> 138 us  [shift(): return lax.ppermute(value, 'seq', self.pairs(dim, by))]
    pallas_call x3 -> x2, Pallas kernels: 34.7 us -> 34.7 us  [products(): call(functools.partial(products_body, tuple(starts)), 'products', jax.Sha...]
  transfers between devices with their start and end apart: 69 -> 69, of which waited for: 34 -> 31; matrix products, arithmetic and copies ran while one was open for 26% -> 26% of each run, Pallas kernels for 8% -> 8%
where the time goes in v3:
time: 714 us; the launch traced here: 705 us
  waiting for transfers between devices  237 us (33%)
  starting transfers between devices  156 us (22%)
  Pallas kernels  97.3 us (14%)
  matrix products  86.9 us (12%)
  other arithmetic  57.3 us (8%)
  local copies, waits for them, and re-layouts  53.9 us (8%)
  between operations  15.8 us (2%)
    ppermute x48, waiting for transfers between devices, shift(): return lax.ppermute(value, 'seq', self.pairs(dim, by))  168 us
    ppermute x48, starting transfers between devices, shift(): return lax.ppermute(value, 'seq', self.pairs(dim, by))  138 us
    all_gather x2, waiting for transfers between devices, gather_plane_off(): lax.all_gather(column, 'seq', axis=1, tiled=False, axis_index_groups=groups)  51.2 us
    dot_general x7, matrix products, dot_t(): return rows_rows(left, right)  39.9 us
    pallas_call x2, Pallas kernels, products(): call(functools.partial(products_body, tuple(starts)), 'products', jax.Sha...  34.7 us
    dot_general x6, matrix products, plane_major(): return rows_rows(pick, values).astype(BF)  26.4 us
    dot_general x6, matrix products, bf_dot(): return rows_cols(left, right)  20.6 us
    pallas_call x1, Pallas kernels, middle(): call(functools.partial(middle_body, step), 'middle', (jax.ShapeDtypeStruc...  19.2 us
  transfers between devices with their start and end apart: 69, of which 31 were waited for; matrix products, arithmetic and copies ran while one was open for 26% of the time, Pallas kernels for 8%

profile of v3, /device:TPU:0, one launch (start us, length us, event | category | flops | bytes accessed | tf_op | source)
XLA Modules:
  0.0 704.7 jit_solution(9966200732649814878)
XLA Ops:
  51.5 6.9 collective-permute-done.7
  64.4 7.8 %collective-permute-done.21 = bf16[64,4096]{1,0:T(8,128)(2,1)S(1)} collective-permute-done((bf16[64,4096]{1,0:T(8,128)(2,1)}, bf16[64,4096]{1,0:T(8,128)(2,1)S(1)}, u32[]{:S(2)}, u32[]{:S(2)}) %collective-permute-start.21) | collective-permute-done | bytes 524320 | tf_op jit(solution)/shard_map/ppermute | solution.py:46
  91.3 13.5 %collective-permute-start.14 = (f32[2,2,16]{2,1,0:T(2,128)S(1)}, f32[2,2,16]{2,1,0:T(2,128)S(1)}, u32[]{:S(2)}, u32[]{:S(2)}) collective-permute-start(f32[2,2,16]{2,1,0:T(2,128)S(1)} %get-tuple-element.306), channel_id=1, source_target_pairs={{0,24},{2,26},{4,28},{6,30},{8,0},{10,2},{12,4},{14,6},{16,8},{18,... | collective-permute-start | bytes 776 | tf_op jit(solution)/shard_map/ppermute | solution.py:46
  110.8 26.8 %collective-permute-done.13 = f32[2,2,16]{2,1,0:T(2,128)S(1)} collective-permute-done((f32[2,2,16]{2,1,0:T(2,128)S(1)}, f32[2,2,16]{2,1,0:T(2,128)S(1)}, u32[]{:S(2)}, u32[]{:S(2)}) %collective-permute-start.13) | collective-permute-done | bytes 288 | tf_op jit(solution)/shard_map/ppermute | solution.py:46
  152.5 9.3 %collective-permute-done.15 = bf16[16,64,128]{2,1,0:T(8,128)(2,1)S(1)} collective-permute-done((bf16[16,64,128]{2,1,0:T(8,128)(2,1)S(1)}, bf16[16,64,128]{2,1,0:T(8,128)(2,1)S(1)}, u32[]{:S(2)}, u32[]{:S(2)}) %collective-permute-start.15) | collective-permute-done | bytes 262176 | tf_op jit(solution)/shard_map/ppermute | solution.py:46
  163.0 13.4 %collective-permute-start.16 = (bf16[16,64,128]{2,1,0:T(8,128)(2,1)S(1)}, bf16[16,64,128]{2,1,0:T(8,128)(2,1)S(1)}, u32[]{:S(2)}, u32[]{:S(2)}) collective-permute-start(bf16[16,64,128]{2,1,0:T(8,128)(2,1)S(1)} %fusion.87), channel_id=1, source_target_pairs={{0,4},{2,6},{4,0},{6,2},{8,12},{10,14},{12,8},{14,10},{16,20},{18,... | collective-permute-start | bytes 786440 | tf_op jit(solution)/shard_map/ppermute | solution.py:46
  186.3 16.1 %collective-permute-start.18 = (bf16[16,64,128]{2,1,0:T(8,128)(2,1)S(1)}, bf16[16,64,128]{2,1,0:T(8,128)(2,1)S(1)}, u32[]{:S(2)}, u32[]{:S(2)}) collective-permute-start(bf16[16,64,128]{2,1,0:T(8,128)(2,1)S(1)} %fusion.65), channel_id=1, source_target_pairs={{0,16},{2,18},{4,20},{6,22},{8,24},{10,26},{12,28},{14,30},{16,0},... | collective-permute-start | bytes 786440 | tf_op jit(solution)/shard_map/ppermute | solution.py:46
  205.1 13.1 %collective-permute-done.18 = bf16[16,64,128]{2,1,0:T(8,128)(2,1)S(1)} collective-permute-done((bf16[16,64,128]{2,1,0:T(8,128)(2,1)S(1)}, bf16[16,64,128]{2,1,0:T(8,128)(2,1)S(1)}, u32[]{:S(2)}, u32[]{:S(2)}) %collective-permute-start.18) | collective-permute-done | bytes 262176 | tf_op jit(solution)/shard_map/ppermute | solution.py:46
  234.0 7.3 %convolution_convert_fusion.1.qkv = bf16[1024,1536]{1,0:T(8,128)(2,1)} fusion(bf16[1024,4096]{1,0:T(8,128)(2,1)} %bitcast.273, bf16[1024,1024]{1,0:T(8,128)(2,1)S(1)} %copy-done.2, f32[1024]{0:T(1024)S(1)} %get-tuple-element.225, f32[1024]{0:T(1024)S(1)} %add_rsqrt_fusion.1, f32[128,1024]{1,0:T(8,128)S(1)} %add_add_fusion.1), kind=kOutput, calls=%fused_computation.45 | convolution fusion | flops 3228041216 | bytes 8921088 | tf_op jit(solution)/shard_map/dot_general | solution.py:714
  241.4 8.6 %attend.1.refs_3_ = bf16[1024,512]{1,0:T(8,128)(2,1)} custom-call(bf16[1024,1536]{1,0:T(8,128)(2,1)} %convolution_convert_fusion.1.qkv), custom_call_target="tpu_custom_call" | custom-call | flops 536870912 | bytes 4194304 | tf_op jit(solution)/shard_map/attend/pallas_call | solution.py:325
  253.9 5.3 convolution_convert_fusion.5.refs_2_
  264.2 5.2 convolution_convert_fusion.6.refs_0_
  269.4 51.2 %all-gather.7.cloned.1.call-done = bf16[4,256,6144]{2,1,0:T(8,128)(2,1)} async-done(((bf16[4,64,6144]{2,1,0:T(8,128)(2,1)}), bf16[4,256,6144]{2,1,0:T(8,128)(2,1)}) %all-gather.7.cloned.1.call-update) | async-done | bytes 12582928 | tf_op jit(solution)/shard_map/all_gather | solution.py:78
  320.6 19.2 %middle.1 = (bf16[1024,2048]{1,0:T(8,128)(2,1)}, bf16[1024,4096]{1,0:T(8,128)(2,1)}) custom-call(bf16[1024,1024]{1,0:T(8,128)(2,1)} %copy-done.21, bf16[1024,1024]{1,0:T(8,128)(2,1)} %grad.1, bf16[1024,6144]{1,0:T(8,128)(2,1)} %bitcast.300, bf16[1024,6144]{1,0:T(8,128)(2,1)} %bitcast.301), custom_call_target="tpu_custom_call" | custom-call | flops 12884901888 | bytes 29360128 | tf_op jit(solution)/shard_map/middle/pallas_call | solution.py:397
  339.8 21.1 %products.2 = bf16[1024,6144]{1,0:T(8,128)(2,1)} custom-call(bf16[1024,1024]{1,0:T(8,128)(2,1)} %convolution_convert_fusion.6.refs_0_, bf16[1024,4096]{1,0:T(8,128)(2,1)} %get-tuple-element.78.refs_1_, bf16[1024,1024]{1,0:T(8,128)(2,1)} %convolution_convert_fusion.5.refs_2_, bf16[1024,2048]{1,0:T(8,128)(2,1)} %get-tuple-element.76.refs_3_), custom_call_target="tpu_custom_call" | custom-call | flops 12884901888 | bytes 29360128 | tf_op jit(solution)/shard_map/products/pallas_call | solution.py:443
  361.0 14.1 %fusion.36 = bf16[1024,1024]{1,0:T(8,128)(2,1)S(1)} fusion(bf16[1024,4096]{1,0:T(8,128)(2,1)} %get-tuple-element.78.refs_1_, bf16[1024,6144]{1,0:T(8,128)(2,1)} %bitcast.302), kind=kOutput, calls=%fused_computation.57 | convolution fusion | flops 8590983168 | bytes 18874368 | tf_op jit(solution)/shard_map/dot_general | solution.py:718
  375.1 7.3 %fusion.33 = bf16[1024,1024]{1,0:T(8,128)(2,1)S(1)} fusion(bf16[1024,2048]{1,0:T(8,128)(2,1)S(1)} %copy-done.58, bf16[1024,6144]{1,0:T(8,128)(2,1)} %bitcast.303), kind=kOutput, calls=%fused_computation.51 | convolution fusion | flops 4296015872 | bytes 10485760 | tf_op jit(solution)/shard_map/dot_general | solution.py:718
  396.6 13.0 %attend_back.1.refs_1_ = bf16[1024,1536]{1,0:T(8,128)(2,1)} custom-call(bf16[1024,1536]{1,0:T(8,128)(2,1)} %convolution_convert_fusion.1.qkv, bf16[1024,512]{1,0:T(8,128)(2,1)} %convolution_convert_fusion.7.grad), custom_call_target="tpu_custom_call" | custom-call | flops 1342177280 | bytes 7340032 | tf_op jit(solution)/shard_map/attend_back/pallas_call | solution.py:368
  409.6 6.3 fusion.30
  416.2 4.8 convolution_convert_fusion.4.refs_0_
  421.0 4.9 convolution_convert_fusion.3.refs_2_
  443.1 13.6 %products.3 = bf16[1024,4096]{1,0:T(8,128)(2,1)} custom-call(bf16[1024,1024]{1,0:T(8,128)(2,1)} %convolution_convert_fusion.4.refs_0_, bf16[1024,1536]{1,0:T(8,128)(2,1)} %attend_back.1.refs_1_, bf16[1024,1024]{1,0:T(8,128)(2,1)} %convolution_convert_fusion.3.refs_2_, bf16[1024,512]{1,0:T(8,128)(2,1)} %attend.1.refs_3_, ...), custom_call_target="tpu_custom_call" | custom-call | flops 4831838208 | bytes 17825792 | tf_op jit(solution)/shard_map/products/pallas_call | solution.py:443
  458.3 13.1 %collective-permute-done.33 = bf16[16,64,128]{2,1,0:T(8,128)(2,1)S(1)} collective-permute-done((bf16[16,64,128]{2,1,0:T(8,128)(2,1)S(1)}, bf16[16,64,128]{2,1,0:T(8,128)(2,1)S(1)}, u32[]{:S(2)}, u32[]{:S(2)}) %collective-permute-start.33) | collective-permute-done | bytes 262176 | tf_op jit(solution)/shard_map/ppermute | solution.py:46
  473.0 12.6 %collective-permute-done.34 = bf16[16,64,128]{2,1,0:T(8,128)(2,1)S(1)} collective-permute-done((bf16[16,64,128]{2,1,0:T(8,128)(2,1)S(1)}, bf16[16,64,128]{2,1,0:T(8,128)(2,1)S(1)}, u32[]{:S(2)}, u32[]{:S(2)}) %collective-permute-start.34) | collective-permute-done | bytes 262176 | tf_op jit(solution)/shard_map/ppermute | solution.py:46
  504.0 7.9 %collective-permute-start.40 = (bf16[64,2048]{1,0:T(8,128)(2,1)S(1)}, bf16[64,2048]{1,0:T(8,128)(2,1)}, u32[]{:S(2)}, u32[]{:S(2)}) collective-permute-start(bf16[64,2048]{1,0:T(8,128)(2,1)S(1)} %get-tuple-element.278), channel_id=1, source_target_pairs={{0,8},{2,10},{4,12},{6,14},{8,16},{10,18},{12,20},{14,22},{16,24},... | collective-permute-start | bytes 786440 | tf_op jit(solution)/shard_map/ppermute | solution.py:46
  511.9 16.2 %collective-permute-done.36 = bf16[16,64,128]{2,1,0:T(8,128)(2,1)S(1)} collective-permute-done((bf16[16,64,128]{2,1,0:T(8,128)(2,1)S(1)}, bf16[16,64,128]{2,1,0:T(8,128)(2,1)S(1)}, u32[]{:S(2)}, u32[]{:S(2)}) %collective-permute-start.36) | collective-permute-done | bytes 262176 | tf_op jit(solution)/shard_map/ppermute | solution.py:46
  528.1 11.7 %collective-permute-start.44 = (bf16[64,2048]{1,0:T(8,128)(2,1)S(1)}, bf16[64,2048]{1,0:T(8,128)(2,1)S(1)}, u32[]{:S(2)}, u32[]{:S(2)}) collective-permute-start(bf16[64,2048]{1,0:T(8,128)(2,1)S(1)} %get-tuple-element.277), channel_id=1, source_target_pairs={{0,16},{2,18},{4,20},{6,22},{8,24},{10,26},{12,28},{14,30},{16,0},... | collective-permute-start | bytes 786440 | tf_op jit(solution)/shard_map/ppermute | solution.py:46
  540.9 10.0 %unmix.1 = (f32[136,1280]{1,0:T(8,128)}, f32[128,128]{1,0:T(8,128)}, f32[4,1280]{1,0:T(4,128)}, f32[8,128]{1,0:T(8,128)}, f32[1,1024]{1,0:T(1,128)}) custom-call(bf16[8,1280]{1,0:T(8,128)(2,1)} %pad.21.rim, bf16[128,1280]{1,0:T(8,128)(2,1)} %slice.251.mixed, f32[128,128]{1,0:T(8,128)} %slice.252.raw, f32[8,128]{1,0:T(8,128)} %select_maximum_fusion.small, ...), custom_call_target="tpu_custom_call" | custom-call | flops 1610612736 | bytes 3932160 | tf_op jit(solution)/shard_map/unmix/pallas_call | solution.py:690
  599.5 7.9 %collective-permute-start.53 = (f32[82,128]{1,0:T(8,128)S(1)}, f32[82,128]{1,0:T(8,128)S(1)}, u32[]{:S(2)}, u32[]{:S(2)}) collective-permute-start(f32[82,128]{1,0:T(8,128)S(1)} %add.605), channel_id=1, source_target_pairs={{0,8},{2,10},{4,12},{6,14},{8,0},{10,2},{12,4},{14,6},{16,24},{18,... | collective-permute-start | bytes 125960 | tf_op jit(solution)/shard_map/ppermute | solution.py:178
  627.0 11.0 %collective-permute-start.58 = (bf16[64,2048]{1,0:T(8,128)(2,1)S(1)}, bf16[64,2048]{1,0:T(8,128)(2,1)S(1)}, u32[]{:S(2)}, u32[]{:S(2)}) collective-permute-start(bf16[64,2048]{1,0:T(8,128)(2,1)S(1)} %get-tuple-element.269), channel_id=1, source_target_pairs={{0,8},{2,10},{4,12},{6,14},{8,16},{10,18},{12,20},{14,22},{16,24},... | collective-permute-start | bytes 786440 | tf_op jit(solution)/shard_map/ppermute | solution.py:46
  638.0 15.6 %collective-permute-done.48 = bf16[64,2048]{1,0:T(8,128)(2,1)} collective-permute-done((bf16[64,2048]{1,0:T(8,128)(2,1)S(1)}, bf16[64,2048]{1,0:T(8,128)(2,1)}, u32[]{:S(2)}, u32[]{:S(2)}) %collective-permute-start.48) | collective-permute-done | bytes 262176 | tf_op jit(solution)/shard_map/ppermute | solution.py:46
  672.9 22.6 %collective-permute-done.56 = bf16[64,1408]{0,1:T(8,128)(2,1)S(1)} collective-permute-done((bf16[64,1408]{0,1:T(8,128)(2,1)S(1)}, bf16[64,1408]{0,1:T(8,128)(2,1)S(1)}, u32[]{:S(2)}, u32[]{:S(2)}) %collective-permute-start.56) | collective-permute-done | bytes 180256 | tf_op jit(solution)/shard_map/ppermute | solution.py:46
  (459 shorter events, 271.6 us)
Async XLA Ops:
  7.2 178.8 %all-gather.5.cloned.1.call-start = ((), (), s32[]{:S(2)}) async-start(), calls=%async_computation.6 | async-start | bytes 10485760 | tf_op jit(solution)/shard_map/all_gather | solution.py:78
  34.2 30.3 %collective-permute-start.20 = (bf16[64,4096]{1,0:T(8,128)(2,1)}, bf16[64,4096]{1,0:T(8,128)(2,1)S(1)}, u32[]{:S(2)}, u32[]{:S(2)}) collective-permute-start(bf16[64,4096]{1,0:T(8,128)(2,1)} %bitcast_dynamic-update-slice_fusion.13), channel_id=1, source_target_pairs={{0,8},{2,10},{4,12},{6,14},{8,16},{10,18},{12,20},{14,22},{16,24},... | collective-permute-start | bytes 1572872 | tf_op jit(solution)/shard_map/ppermute | solution.py:46
  41.4 30.9 %collective-permute-start.21 = (bf16[64,4096]{1,0:T(8,128)(2,1)}, bf16[64,4096]{1,0:T(8,128)(2,1)S(1)}, u32[]{:S(2)}, u32[]{:S(2)}) collective-permute-start(bf16[64,4096]{1,0:T(8,128)(2,1)} %bitcast_dynamic-update-slice_fusion.13), channel_id=1, source_target_pairs={{0,16},{2,18},{4,20},{6,22},{8,24},{10,26},{12,28},{14,30},{16,0},... | collective-permute-start | bytes 1572872 | tf_op jit(solution)/shard_map/ppermute | solution.py:46
  44.7 27.6 %collective-permute-start.22 = (bf16[64,4096]{1,0:T(8,128)(2,1)}, bf16[64,4096]{1,0:T(8,128)(2,1)S(1)}, u32[]{:S(2)}, u32[]{:S(2)}) collective-permute-start(bf16[64,4096]{1,0:T(8,128)(2,1)} %bitcast_dynamic-update-slice_fusion.13), channel_id=1, source_target_pairs={{0,24},{2,26},{4,28},{6,30},{8,0},{10,2},{12,4},{14,6},{16,8},{18,... | collective-permute-start | bytes 1572872 | tf_op jit(solution)/shard_map/ppermute | solution.py:46
  73.8 246.8 %all-gather.7.cloned.1.call-start = ((), (), s32[]{:S(2)}) async-start(), calls=%async_computation.7 | async-start | bytes 15728640 | tf_op jit(solution)/shard_map/all_gather | solution.py:78
  104.9 32.7 %collective-permute-start.13 = (f32[2,2,16]{2,1,0:T(2,128)S(1)}, f32[2,2,16]{2,1,0:T(2,128)S(1)}, u32[]{:S(2)}, u32[]{:S(2)}) collective-permute-start(f32[2,2,16]{2,1,0:T(2,128)S(1)} %get-tuple-element.306), channel_id=1, source_target_pairs={{0,16},{2,18},{4,20},{6,22},{8,24},{10,26},{12,28},{14,30},{16,0},... | collective-permute-start | bytes 776 | tf_op jit(solution)/shard_map/ppermute | solution.py:46
  104.9 76.1 %collective-permute-start.26 = (bf16[64,6144]{1,0:T(8,128)(2,1)S(1)}, bf16[64,6144]{1,0:T(8,128)(2,1)S(1)}, u32[]{:S(2)}, u32[]{:S(2)}) collective-permute-start(bf16[64,6144]{1,0:T(8,128)(2,1)S(1)} %pad_maximum_fusion.2), channel_id=1, source_target_pairs={{0,8},{2,10},{4,12},{6,14},{8,16},{10,18},{12,20},{14,22},{16,24},... | collective-permute-start | bytes 2359304 | tf_op jit(solution)/shard_map/ppermute | solution.py:46
  105.5 35.9 %collective-permute-start.12 = (f32[2,2,16]{2,1,0:T(2,128)S(1)}, f32[2,2,16]{2,1,0:T(2,128)S(1)}, u32[]{:S(2)}, u32[]{:S(2)}) collective-permute-start(f32[2,2,16]{2,1,0:T(2,128)S(1)} %get-tuple-element.306), channel_id=1, source_target_pairs={{0,8},{2,10},{4,12},{6,14},{8,16},{10,18},{12,20},{14,22},{16,24},... | collective-permute-start | bytes 776 | tf_op jit(solution)/shard_map/ppermute | solution.py:46
  108.4 72.6 %collective-permute-start.27 = (bf16[64,6144]{1,0:T(8,128)(2,1)S(1)}, bf16[64,6144]{1,0:T(8,128)(2,1)}, u32[]{:S(2)}, u32[]{:S(2)}) collective-permute-start(bf16[64,6144]{1,0:T(8,128)(2,1)S(1)} %pad_maximum_fusion.2), channel_id=1, source_target_pairs={{0,16},{2,18},{4,20},{6,22},{8,24},{10,26},{12,28},{14,30},{16,0},... | collective-permute-start | bytes 2359304 | tf_op jit(solution)/shard_map/ppermute | solution.py:46
  109.3 71.7 %collective-permute-start.28 = (bf16[64,6144]{1,0:T(8,128)(2,1)S(1)}, bf16[64,6144]{1,0:T(8,128)(2,1)}, u32[]{:S(2)}, u32[]{:S(2)}) collective-permute-start(bf16[64,6144]{1,0:T(8,128)(2,1)S(1)} %pad_maximum_fusion.2), channel_id=1, source_target_pairs={{0,24},{2,26},{4,28},{6,30},{8,0},{10,2},{12,4},{14,6},{16,8},{18,... | collective-permute-start | bytes 2359304 | tf_op jit(solution)/shard_map/ppermute | solution.py:46
  186.1 301.3 %reduce-scatter.4.cloned.1.call-start = ((), (), s32[]{:S(2)}) async-start(), calls=%async_computation.3 | async-start | bytes 15728640 | tf_op jit(solution)/shard_map/reduce_scatter | solution.py:123
  186.3 31.9 %collective-permute-start.18 = (bf16[16,64,128]{2,1,0:T(8,128)(2,1)S(1)}, bf16[16,64,128]{2,1,0:T(8,128)(2,1)S(1)}, u32[]{:S(2)}, u32[]{:S(2)}) collective-permute-start(bf16[16,64,128]{2,1,0:T(8,128)(2,1)S(1)} %fusion.65), channel_id=1, source_target_pairs={{0,16},{2,18},{4,20},{6,22},{8,24},{10,26},{12,28},{14,30},{16,0},... | collective-permute-start | bytes 786440 | tf_op jit(solution)/shard_map/ppermute | solution.py:46
  360.9 216.2 %reduce-scatter.6.cloned.1.call-start = ((), (), s32[]{:S(2)}) async-start(), calls=%async_computation.4 | async-start | bytes 10485760 | tf_op jit(solution)/shard_map/reduce_scatter | solution.py:123
  487.4 175.0 %reduce-scatter.8.cloned.1.call-start = ((), (), s32[]{:S(2)}) async-start(), calls=%async_computation.5 | async-start | bytes 3604480 | tf_op jit(solution)/shard_map/reduce_scatter | solution.py:123
  494.2 33.9 %collective-permute-start.36 = (bf16[16,64,128]{2,1,0:T(8,128)(2,1)S(1)}, bf16[16,64,128]{2,1,0:T(8,128)(2,1)S(1)}, u32[]{:S(2)}, u32[]{:S(2)}) collective-permute-start(bf16[16,64,128]{2,1,0:T(8,128)(2,1)S(1)} %fusion.71), channel_id=1, source_target_pairs={{0,16},{2,18},{4,20},{6,22},{8,24},{10,26},{12,28},{14,30},{16,0},... | collective-permute-start | bytes 786440 | tf_op jit(solution)/shard_map/ppermute | solution.py:46
  494.2 33.9 %collective-permute-start.35 = (bf16[16,64,128]{2,1,0:T(8,128)(2,1)S(1)}, bf16[16,64,128]{2,1,0:T(8,128)(2,1)S(1)}, u32[]{:S(2)}, u32[]{:S(2)}) collective-permute-start(bf16[16,64,128]{2,1,0:T(8,128)(2,1)S(1)} %fusion.71), channel_id=1, source_target_pairs={{0,8},{2,10},{4,12},{6,14},{8,16},{10,18},{12,20},{14,22},{16,24},... | collective-permute-start | bytes 786440 | tf_op jit(solution)/shard_map/ppermute | solution.py:46
  498.8 53.1 %collective-permute-start.42 = (bf16[64,2048]{1,0:T(8,128)(2,1)}, bf16[64,2048]{1,0:T(8,128)(2,1)}, u32[]{:S(2)}, u32[]{:S(2)}) collective-permute-start(bf16[64,2048]{1,0:T(8,128)(2,1)} %get-tuple-element.279), channel_id=1, source_target_pairs={{0,24},{2,26},{4,28},{6,30},{8,0},{10,2},{12,4},{14,6},{16,8},{18,... | collective-permute-start | bytes 786440 | tf_op jit(solution)/shard_map/ppermute | solution.py:46
  501.2 50.8 %collective-permute-start.41 = (bf16[64,2048]{1,0:T(8,128)(2,1)}, bf16[64,2048]{1,0:T(8,128)(2,1)}, u32[]{:S(2)}, u32[]{:S(2)}) collective-permute-start(bf16[64,2048]{1,0:T(8,128)(2,1)} %get-tuple-element.280), channel_id=1, source_target_pairs={{0,16},{2,18},{4,20},{6,22},{8,24},{10,26},{12,28},{14,30},{16,0},... | collective-permute-start | bytes 786440 | tf_op jit(solution)/shard_map/ppermute | solution.py:46
  504.0 51.8 %collective-permute-start.40 = (bf16[64,2048]{1,0:T(8,128)(2,1)S(1)}, bf16[64,2048]{1,0:T(8,128)(2,1)}, u32[]{:S(2)}, u32[]{:S(2)}) collective-permute-start(bf16[64,2048]{1,0:T(8,128)(2,1)S(1)} %get-tuple-element.278), channel_id=1, source_target_pairs={{0,8},{2,10},{4,12},{6,14},{8,16},{10,18},{12,20},{14,22},{16,24},... | collective-permute-start | bytes 786440 | tf_op jit(solution)/shard_map/ppermute | solution.py:46
  528.1 33.5 %collective-permute-start.45 = (bf16[64,2048]{1,0:T(8,128)(2,1)S(1)}, bf16[64,2048]{1,0:T(8,128)(2,1)}, u32[]{:S(2)}, u32[]{:S(2)}) collective-permute-start(bf16[64,2048]{1,0:T(8,128)(2,1)S(1)} %get-tuple-element.276), channel_id=1, source_target_pairs={{0,24},{2,26},{4,28},{6,30},{8,0},{10,2},{12,4},{14,6},{16,8},{18,... | collective-permute-start | bytes 786440 | tf_op jit(solution)/shard_map/ppermute | solution.py:46
  528.1 35.4 %collective-permute-start.44 = (bf16[64,2048]{1,0:T(8,128)(2,1)S(1)}, bf16[64,2048]{1,0:T(8,128)(2,1)S(1)}, u32[]{:S(2)}, u32[]{:S(2)}) collective-permute-start(bf16[64,2048]{1,0:T(8,128)(2,1)S(1)} %get-tuple-element.277), channel_id=1, source_target_pairs={{0,16},{2,18},{4,20},{6,22},{8,24},{10,26},{12,28},{14,30},{16,0},... | collective-permute-start | bytes 786440 | tf_op jit(solution)/shard_map/ppermute | solution.py:46
  552.0 28.0 %collective-permute-start.63 = (bf16[64,2048]{1,0:T(8,128)(2,1)}, bf16[64,2048]{1,0:T(8,128)(2,1)}, u32[]{:S(2)}, u32[]{:S(2)}) collective-permute-start(bf16[64,2048]{1,0:T(8,128)(2,1)} %get-tuple-element.267), channel_id=1, source_target_pairs={{0,24},{2,26},{4,28},{6,30},{8,0},{10,2},{12,4},{14,6},{16,8},{18,... | collective-permute-start | bytes 786440 | tf_op jit(solution)/shard_map/ppermute | solution.py:46
  559.6 24.8 %collective-permute-start.62 = (bf16[64,2048]{1,0:T(8,128)(2,1)}, bf16[64,2048]{1,0:T(8,128)(2,1)}, u32[]{:S(2)}, u32[]{:S(2)}) collective-permute-start(bf16[64,2048]{1,0:T(8,128)(2,1)} %get-tuple-element.268), channel_id=1, source_target_pairs={{0,16},{2,18},{4,20},{6,22},{8,24},{10,26},{12,28},{14,30},{16,0},... | collective-permute-start | bytes 786440 | tf_op jit(solution)/shard_map/ppermute | solution.py:46
  561.6 22.8 %collective-permute-start.61 = (bf16[64,2048]{1,0:T(8,128)(2,1)}, bf16[64,2048]{1,0:T(8,128)(2,1)}, u32[]{:S(2)}, u32[]{:S(2)}) collective-permute-start(bf16[64,2048]{1,0:T(8,128)(2,1)} %get-tuple-element.266), channel_id=1, source_target_pairs={{0,8},{2,10},{4,12},{6,14},{8,16},{10,18},{12,20},{14,22},{16,24},... | collective-permute-start | bytes 786440 | tf_op jit(solution)/shard_map/ppermute | solution.py:46
  563.5 23.7 %collective-permute-start.50 = (f32[4,256]{1,0:T(4,128)S(1)}, f32[4,256]{1,0:T(4,128)S(1)}, u32[]{:S(2)}, u32[]{:S(2)}) collective-permute-start(f32[4,256]{1,0:T(4,128)S(1)} %slice.223), channel_id=1, source_target_pairs={{0,1},{1,0},{2,3},{3,2},{4,5},{5,4},{6,7},{7,6},{8,9},{9,8},{10,11... | collective-permute-start | bytes 12296 | tf_op jit(solution)/shard_map/ppermute | solution.py:162
  617.0 36.7 %collective-permute-start.48 = (bf16[64,2048]{1,0:T(8,128)(2,1)S(1)}, bf16[64,2048]{1,0:T(8,128)(2,1)}, u32[]{:S(2)}, u32[]{:S(2)}) collective-permute-start(bf16[64,2048]{1,0:T(8,128)(2,1)S(1)} %get-tuple-element.274), channel_id=1, source_target_pairs={{0,16},{2,18},{4,20},{6,22},{8,24},{10,26},{12,28},{14,30},{16,0},... | collective-permute-start | bytes 786440 | tf_op jit(solution)/shard_map/ppermute | solution.py:46
  618.9 34.8 %collective-permute-start.47 = (bf16[64,2048]{1,0:T(8,128)(2,1)S(1)}, bf16[64,2048]{1,0:T(8,128)(2,1)}, u32[]{:S(2)}, u32[]{:S(2)}) collective-permute-start(bf16[64,2048]{1,0:T(8,128)(2,1)S(1)} %get-tuple-element.272), channel_id=1, source_target_pairs={{0,8},{2,10},{4,12},{6,14},{8,16},{10,18},{12,20},{14,22},{16,24},... | collective-permute-start | bytes 786440 | tf_op jit(solution)/shard_map/ppermute | solution.py:46
  623.1 35.4 %collective-permute-start.60 = (bf16[64,2048]{1,0:T(8,128)(2,1)S(1)}, bf16[64,2048]{1,0:T(8,128)(2,1)S(1)}, u32[]{:S(2)}, u32[]{:S(2)}) collective-permute-start(bf16[64,2048]{1,0:T(8,128)(2,1)S(1)} %get-tuple-element.270), channel_id=1, source_target_pairs={{0,24},{2,26},{4,28},{6,30},{8,0},{10,2},{12,4},{14,6},{16,8},{18,... | collective-permute-start | bytes 786440 | tf_op jit(solution)/shard_map/ppermute | solution.py:46
  627.0 35.2 %collective-permute-start.59 = (bf16[64,2048]{1,0:T(8,128)(2,1)S(1)}, bf16[64,2048]{1,0:T(8,128)(2,1)S(1)}, u32[]{:S(2)}, u32[]{:S(2)}) collective-permute-start(bf16[64,2048]{1,0:T(8,128)(2,1)S(1)} %get-tuple-element.271), channel_id=1, source_target_pairs={{0,16},{2,18},{4,20},{6,22},{8,24},{10,26},{12,28},{14,30},{16,0},... | collective-permute-start | bytes 786440 | tf_op jit(solution)/shard_map/ppermute | solution.py:46
  627.0 35.2 %collective-permute-start.58 = (bf16[64,2048]{1,0:T(8,128)(2,1)S(1)}, bf16[64,2048]{1,0:T(8,128)(2,1)S(1)}, u32[]{:S(2)}, u32[]{:S(2)}) collective-permute-start(bf16[64,2048]{1,0:T(8,128)(2,1)S(1)} %get-tuple-element.269), channel_id=1, source_target_pairs={{0,8},{2,10},{4,12},{6,14},{8,16},{10,18},{12,20},{14,22},{16,24},... | collective-permute-start | bytes 786440 | tf_op jit(solution)/shard_map/ppermute | solution.py:46
  664.2 31.3 %collective-permute-start.56 = (bf16[64,1408]{0,1:T(8,128)(2,1)S(1)}, bf16[64,1408]{0,1:T(8,128)(2,1)S(1)}, u32[]{:S(2)}, u32[]{:S(2)}) collective-permute-start(bf16[64,1408]{0,1:T(8,128)(2,1)S(1)} %bitcast.282), channel_id=1, source_target_pairs={{0,16},{2,18},{4,20},{6,22},{8,24},{10,26},{12,28},{14,30},{16,0},... | collective-permute-start | bytes 540680 | tf_op jit(solution)/shard_map/ppermute | solution.py:46
  665.1 30.3 %collective-permute-start.55 = (bf16[64,1408]{0,1:T(8,128)(2,1)S(1)}, bf16[64,1408]{0,1:T(8,128)(2,1)S(1)}, u32[]{:S(2)}, u32[]{:S(2)}) collective-permute-start(bf16[64,1408]{0,1:T(8,128)(2,1)S(1)} %bitcast.283), channel_id=1, source_target_pairs={{0,8},{2,10},{4,12},{6,14},{8,16},{10,18},{12,20},{14,22},{16,24},... | collective-permute-start | bytes 540680 | tf_op jit(solution)/shard_map/ppermute | solution.py:46
  (96 other events, 1299.7 us)
Sparse Core Ops, SparseCore 0:
  73.9 104.4 all-gather.4
  186.2 134.3 all-gather.6
  361.0 126.3 reduce-scatter.3
  490.3 86.7 reduce-scatter.5
  580.3 48.5 reduce-scatter.7

commit v4 on v3

--- a/solution.py
+++ b/solution.py
@@ -860,7 +860,7 @@
             (plane_major(grid, normed_mlp), pair_grad),
             (plane_major(grid, out_grad), hidden),
         ),
-        2 * step,
+        4 * step,
     )
     mlp_plane = scatter_plane(grid, mlp_part)
     pair_grad = follow(pair_grad, mlp_part)

time: 714 us -> 711 us (level)
  no operation moved by 1% of the time
where the time goes in v4:
time: 711 us; the launch traced here: 703 us
  waiting for transfers between devices  237 us (33%)
  starting transfers between devices  156 us (22%)
  Pallas kernels  95.2 us (13%)
  matrix products  86.9 us (12%)
  other arithmetic  57.3 us (8%)
  local copies, waits for them, and re-layouts  53.9 us (8%)
  between operations  15.8 us (2%)
    ppermute x48, waiting for transfers between devices, shift(): return lax.ppermute(value, 'seq', self.pairs(dim, by))  168 us
    ppermute x48, starting transfers between devices, shift(): return lax.ppermute(value, 'seq', self.pairs(dim, by))  139 us
    all_gather x2, waiting for transfers between devices, gather_plane_off(): lax.all_gather(column, 'seq', axis=1, tiled=False, axis_index_groups=groups)  51.2 us
    dot_general x7, matrix products, dot_t(): return rows_rows(left, right)  39.9 us
    pallas_call x2, Pallas kernels, products(): call(functools.partial(products_body, tuple(starts)), 'products', jax.Sha...  32.7 us
    dot_general x6, matrix products, plane_major(): return rows_rows(pick, values).astype(BF)  26.4 us
    dot_general x6, matrix products, bf_dot(): return rows_cols(left, right)  20.6 us
    pallas_call x1, Pallas kernels, middle(): call(functools.partial(middle_body, step), 'middle', (jax.ShapeDtypeStruc...  19.2 us
  transfers between devices with their start and end apart: 69, of which 31 were waited for; matrix products, arithmetic and copies ran while one was open for 26% of the time, Pallas kernels for 8%

profile of v4, /device:TPU:0, one launch (start us, length us, event | category | flops | bytes accessed | tf_op | source)
XLA Modules:
  0.0 702.6 jit_solution(9465654051207997270)
XLA Ops:
  51.5 6.9 collective-permute-done.7
  64.4 7.8 %collective-permute-done.21 = bf16[64,4096]{1,0:T(8,128)(2,1)S(1)} collective-permute-done((bf16[64,4096]{1,0:T(8,128)(2,1)}, bf16[64,4096]{1,0:T(8,128)(2,1)S(1)}, u32[]{:S(2)}, u32[]{:S(2)}) %collective-permute-start.21) | collective-permute-done | bytes 524320 | tf_op jit(solution)/shard_map/ppermute | solution.py:46
  91.3 13.5 %collective-permute-start.14 = (f32[2,2,16]{2,1,0:T(2,128)S(1)}, f32[2,2,16]{2,1,0:T(2,128)S(1)}, u32[]{:S(2)}, u32[]{:S(2)}) collective-permute-start(f32[2,2,16]{2,1,0:T(2,128)S(1)} %get-tuple-element.306), channel_id=1, source_target_pairs={{0,24},{2,26},{4,28},{6,30},{8,0},{10,2},{12,4},{14,6},{16,8},{18,... | collective-permute-start | bytes 776 | tf_op jit(solution)/shard_map/ppermute | solution.py:46
  110.8 26.8 %collective-permute-done.13 = f32[2,2,16]{2,1,0:T(2,128)S(1)} collective-permute-done((f32[2,2,16]{2,1,0:T(2,128)S(1)}, f32[2,2,16]{2,1,0:T(2,128)S(1)}, u32[]{:S(2)}, u32[]{:S(2)}) %collective-permute-start.13) | collective-permute-done | bytes 288 | tf_op jit(solution)/shard_map/ppermute | solution.py:46
  152.5 9.3 %collective-permute-done.15 = bf16[16,64,128]{2,1,0:T(8,128)(2,1)S(1)} collective-permute-done((bf16[16,64,128]{2,1,0:T(8,128)(2,1)S(1)}, bf16[16,64,128]{2,1,0:T(8,128)(2,1)S(1)}, u32[]{:S(2)}, u32[]{:S(2)}) %collective-permute-start.15) | collective-permute-done | bytes 262176 | tf_op jit(solution)/shard_map/ppermute | solution.py:46
  163.0 13.4 %collective-permute-start.16 = (bf16[16,64,128]{2,1,0:T(8,128)(2,1)S(1)}, bf16[16,64,128]{2,1,0:T(8,128)(2,1)S(1)}, u32[]{:S(2)}, u32[]{:S(2)}) collective-permute-start(bf16[16,64,128]{2,1,0:T(8,128)(2,1)S(1)} %fusion.87), channel_id=1, source_target_pairs={{0,4},{2,6},{4,0},{6,2},{8,12},{10,14},{12,8},{14,10},{16,20},{18,... | collective-permute-start | bytes 786440 | tf_op jit(solution)/shard_map/ppermute | solution.py:46
  186.3 16.1 %collective-permute-start.18 = (bf16[16,64,128]{2,1,0:T(8,128)(2,1)S(1)}, bf16[16,64,128]{2,1,0:T(8,128)(2,1)S(1)}, u32[]{:S(2)}, u32[]{:S(2)}) collective-permute-start(bf16[16,64,128]{2,1,0:T(8,128)(2,1)S(1)} %fusion.65), channel_id=1, source_target_pairs={{0,16},{2,18},{4,20},{6,22},{8,24},{10,26},{12,28},{14,30},{16,0},... | collective-permute-start | bytes 786440 | tf_op jit(solution)/shard_map/ppermute | solution.py:46
  205.1 13.1 %collective-permute-done.18 = bf16[16,64,128]{2,1,0:T(8,128)(2,1)S(1)} collective-permute-done((bf16[16,64,128]{2,1,0:T(8,128)(2,1)S(1)}, bf16[16,64,128]{2,1,0:T(8,128)(2,1)S(1)}, u32[]{:S(2)}, u32[]{:S(2)}) %collective-permute-start.18) | collective-permute-done | bytes 262176 | tf_op jit(solution)/shard_map/ppermute | solution.py:46
  234.0 7.3 %convolution_convert_fusion.1.qkv = bf16[1024,1536]{1,0:T(8,128)(2,1)} fusion(bf16[1024,4096]{1,0:T(8,128)(2,1)} %bitcast.273, bf16[1024,1024]{1,0:T(8,128)(2,1)S(1)} %copy-done.2, f32[1024]{0:T(1024)S(1)} %get-tuple-element.225, f32[1024]{0:T(1024)S(1)} %add_rsqrt_fusion.1, f32[128,1024]{1,0:T(8,128)S(1)} %add_add_fusion.1), kind=kOutput, calls=%fused_computation.45 | convolution fusion | flops 3228041216 | bytes 8921088 | tf_op jit(solution)/shard_map/dot_general | solution.py:714
  241.4 8.6 %attend.1.refs_3_ = bf16[1024,512]{1,0:T(8,128)(2,1)} custom-call(bf16[1024,1536]{1,0:T(8,128)(2,1)} %convolution_convert_fusion.1.qkv), custom_call_target="tpu_custom_call" | custom-call | flops 536870912 | bytes 4194304 | tf_op jit(solution)/shard_map/attend/pallas_call | solution.py:325
  253.9 5.3 convolution_convert_fusion.5.refs_2_
  264.2 5.2 convolution_convert_fusion.6.refs_0_
  269.4 51.2 %all-gather.7.cloned.1.call-done = bf16[4,256,6144]{2,1,0:T(8,128)(2,1)} async-done(((bf16[4,64,6144]{2,1,0:T(8,128)(2,1)}), bf16[4,256,6144]{2,1,0:T(8,128)(2,1)}) %all-gather.7.cloned.1.call-update) | async-done | bytes 12582928 | tf_op jit(solution)/shard_map/all_gather | solution.py:78
  320.6 19.2 %middle.1 = (bf16[1024,2048]{1,0:T(8,128)(2,1)}, bf16[1024,4096]{1,0:T(8,128)(2,1)}) custom-call(bf16[1024,1024]{1,0:T(8,128)(2,1)} %copy-done.21, bf16[1024,1024]{1,0:T(8,128)(2,1)} %grad.1, bf16[1024,6144]{1,0:T(8,128)(2,1)} %bitcast.300, bf16[1024,6144]{1,0:T(8,128)(2,1)} %bitcast.301), custom_call_target="tpu_custom_call" | custom-call | flops 12884901888 | bytes 29360128 | tf_op jit(solution)/shard_map/middle/pallas_call | solution.py:397
  339.8 19.1 %products.2 = bf16[1024,6144]{1,0:T(8,128)(2,1)} custom-call(bf16[1024,1024]{1,0:T(8,128)(2,1)} %convolution_convert_fusion.6.refs_0_, bf16[1024,4096]{1,0:T(8,128)(2,1)} %get-tuple-element.78.refs_1_, bf16[1024,1024]{1,0:T(8,128)(2,1)} %convolution_convert_fusion.5.refs_2_, bf16[1024,2048]{1,0:T(8,128)(2,1)} %get-tuple-element.76.refs_3_), custom_call_target="tpu_custom_call" | custom-call | flops 12884901888 | bytes 29360128 | tf_op jit(solution)/shard_map/products/pallas_call | solution.py:443
  358.9 14.1 %fusion.36 = bf16[1024,1024]{1,0:T(8,128)(2,1)S(1)} fusion(bf16[1024,4096]{1,0:T(8,128)(2,1)} %get-tuple-element.78.refs_1_, bf16[1024,6144]{1,0:T(8,128)(2,1)} %bitcast.302), kind=kOutput, calls=%fused_computation.57 | convolution fusion | flops 8590983168 | bytes 18874368 | tf_op jit(solution)/shard_map/dot_general | solution.py:718
  373.1 7.3 %fusion.33 = bf16[1024,1024]{1,0:T(8,128)(2,1)S(1)} fusion(bf16[1024,2048]{1,0:T(8,128)(2,1)S(1)} %copy-done.58, bf16[1024,6144]{1,0:T(8,128)(2,1)} %bitcast.303), kind=kOutput, calls=%fused_computation.51 | convolution fusion | flops 4296015872 | bytes 10485760 | tf_op jit(solution)/shard_map/dot_general | solution.py:718
  394.6 13.0 %attend_back.1.refs_1_ = bf16[1024,1536]{1,0:T(8,128)(2,1)} custom-call(bf16[1024,1536]{1,0:T(8,128)(2,1)} %convolution_convert_fusion.1.qkv, bf16[1024,512]{1,0:T(8,128)(2,1)} %convolution_convert_fusion.7.grad), custom_call_target="tpu_custom_call" | custom-call | flops 1342177280 | bytes 7340032 | tf_op jit(solution)/shard_map/attend_back/pallas_call | solution.py:368
  407.6 6.3 fusion.30
  414.2 4.8 convolution_convert_fusion.4.refs_0_
  419.0 4.9 convolution_convert_fusion.3.refs_2_
  441.0 13.6 %products.3 = bf16[1024,4096]{1,0:T(8,128)(2,1)} custom-call(bf16[1024,1024]{1,0:T(8,128)(2,1)} %convolution_convert_fusion.4.refs_0_, bf16[1024,1536]{1,0:T(8,128)(2,1)} %attend_back.1.refs_1_, bf16[1024,1024]{1,0:T(8,128)(2,1)} %convolution_convert_fusion.3.refs_2_, bf16[1024,512]{1,0:T(8,128)(2,1)} %attend.1.refs_3_, ...), custom_call_target="tpu_custom_call" | custom-call | flops 4831838208 | bytes 17825792 | tf_op jit(solution)/shard_map/products/pallas_call | solution.py:443
  456.2 13.0 %collective-permute-done.33 = bf16[16,64,128]{2,1,0:T(8,128)(2,1)S(1)} collective-permute-done((bf16[16,64,128]{2,1,0:T(8,128)(2,1)S(1)}, bf16[16,64,128]{2,1,0:T(8,128)(2,1)S(1)}, u32[]{:S(2)}, u32[]{:S(2)}) %collective-permute-start.33) | collective-permute-done | bytes 262176 | tf_op jit(solution)/shard_map/ppermute | solution.py:46
  471.0 12.5 %collective-permute-done.34 = bf16[16,64,128]{2,1,0:T(8,128)(2,1)S(1)} collective-permute-done((bf16[16,64,128]{2,1,0:T(8,128)(2,1)S(1)}, bf16[16,64,128]{2,1,0:T(8,128)(2,1)S(1)}, u32[]{:S(2)}, u32[]{:S(2)}) %collective-permute-start.34) | collective-permute-done | bytes 262176 | tf_op jit(solution)/shard_map/ppermute | solution.py:46
  501.9 7.9 %collective-permute-start.40 = (bf16[64,2048]{1,0:T(8,128)(2,1)S(1)}, bf16[64,2048]{1,0:T(8,128)(2,1)}, u32[]{:S(2)}, u32[]{:S(2)}) collective-permute-start(bf16[64,2048]{1,0:T(8,128)(2,1)S(1)} %get-tuple-element.278), channel_id=1, source_target_pairs={{0,8},{2,10},{4,12},{6,14},{8,16},{10,18},{12,20},{14,22},{16,24},... | collective-permute-start | bytes 786440 | tf_op jit(solution)/shard_map/ppermute | solution.py:46
  509.9 16.2 %collective-permute-done.36 = bf16[16,64,128]{2,1,0:T(8,128)(2,1)S(1)} collective-permute-done((bf16[16,64,128]{2,1,0:T(8,128)(2,1)S(1)}, bf16[16,64,128]{2,1,0:T(8,128)(2,1)S(1)}, u32[]{:S(2)}, u32[]{:S(2)}) %collective-permute-start.36) | collective-permute-done | bytes 262176 | tf_op jit(solution)/shard_map/ppermute | solution.py:46
  526.1 11.7 %collective-permute-start.44 = (bf16[64,2048]{1,0:T(8,128)(2,1)S(1)}, bf16[64,2048]{1,0:T(8,128)(2,1)S(1)}, u32[]{:S(2)}, u32[]{:S(2)}) collective-permute-start(bf16[64,2048]{1,0:T(8,128)(2,1)S(1)} %get-tuple-element.277), channel_id=1, source_target_pairs={{0,16},{2,18},{4,20},{6,22},{8,24},{10,26},{12,28},{14,30},{16,0},... | collective-permute-start | bytes 786440 | tf_op jit(solution)/shard_map/ppermute | solution.py:46
  538.9 10.0 %unmix.1 = (f32[136,1280]{1,0:T(8,128)}, f32[128,128]{1,0:T(8,128)}, f32[4,1280]{1,0:T(4,128)}, f32[8,128]{1,0:T(8,128)}, f32[1,1024]{1,0:T(1,128)}) custom-call(bf16[8,1280]{1,0:T(8,128)(2,1)} %pad.21.rim, bf16[128,1280]{1,0:T(8,128)(2,1)} %slice.251.mixed, f32[128,128]{1,0:T(8,128)} %slice.252.raw, f32[8,128]{1,0:T(8,128)} %select_maximum_fusion.small, ...), custom_call_target="tpu_custom_call" | custom-call | flops 1610612736 | bytes 3932160 | tf_op jit(solution)/shard_map/unmix/pallas_call | solution.py:690
  597.5 7.9 %collective-permute-start.53 = (f32[82,128]{1,0:T(8,128)S(1)}, f32[82,128]{1,0:T(8,128)S(1)}, u32[]{:S(2)}, u32[]{:S(2)}) collective-permute-start(f32[82,128]{1,0:T(8,128)S(1)} %add.605), channel_id=1, source_target_pairs={{0,8},{2,10},{4,12},{6,14},{8,0},{10,2},{12,4},{14,6},{16,24},{18,... | collective-permute-start | bytes 125960 | tf_op jit(solution)/shard_map/ppermute | solution.py:178
  625.0 11.0 %collective-permute-start.58 = (bf16[64,2048]{1,0:T(8,128)(2,1)S(1)}, bf16[64,2048]{1,0:T(8,128)(2,1)S(1)}, u32[]{:S(2)}, u32[]{:S(2)}) collective-permute-start(bf16[64,2048]{1,0:T(8,128)(2,1)S(1)} %get-tuple-element.269), channel_id=1, source_target_pairs={{0,8},{2,10},{4,12},{6,14},{8,16},{10,18},{12,20},{14,22},{16,24},... | collective-permute-start | bytes 786440 | tf_op jit(solution)/shard_map/ppermute | solution.py:46
  636.0 15.6 %collective-permute-done.48 = bf16[64,2048]{1,0:T(8,128)(2,1)} collective-permute-done((bf16[64,2048]{1,0:T(8,128)(2,1)S(1)}, bf16[64,2048]{1,0:T(8,128)(2,1)}, u32[]{:S(2)}, u32[]{:S(2)}) %collective-permute-start.48) | collective-permute-done | bytes 262176 | tf_op jit(solution)/shard_map/ppermute | solution.py:46
  670.9 22.6 %collective-permute-done.56 = bf16[64,1408]{0,1:T(8,128)(2,1)S(1)} collective-permute-done((bf16[64,1408]{0,1:T(8,128)(2,1)S(1)}, bf16[64,1408]{0,1:T(8,128)(2,1)S(1)}, u32[]{:S(2)}, u32[]{:S(2)}) %collective-permute-start.56) | collective-permute-done | bytes 180256 | tf_op jit(solution)/shard_map/ppermute | solution.py:46
  (459 shorter events, 271.6 us)
Async XLA Ops:
  7.2 178.8 %all-gather.5.cloned.1.call-start = ((), (), s32[]{:S(2)}) async-start(), calls=%async_computation.6 | async-start | bytes 10485760 | tf_op jit(solution)/shard_map/all_gather | solution.py:78
  34.2 30.3 %collective-permute-start.20 = (bf16[64,4096]{1,0:T(8,128)(2,1)}, bf16[64,4096]{1,0:T(8,128)(2,1)S(1)}, u32[]{:S(2)}, u32[]{:S(2)}) collective-permute-start(bf16[64,4096]{1,0:T(8,128)(2,1)} %bitcast_dynamic-update-slice_fusion.13), channel_id=1, source_target_pairs={{0,8},{2,10},{4,12},{6,14},{8,16},{10,18},{12,20},{14,22},{16,24},... | collective-permute-start | bytes 1572872 | tf_op jit(solution)/shard_map/ppermute | solution.py:46
  41.4 30.9 %collective-permute-start.21 = (bf16[64,4096]{1,0:T(8,128)(2,1)}, bf16[64,4096]{1,0:T(8,128)(2,1)S(1)}, u32[]{:S(2)}, u32[]{:S(2)}) collective-permute-start(bf16[64,4096]{1,0:T(8,128)(2,1)} %bitcast_dynamic-update-slice_fusion.13), channel_id=1, source_target_pairs={{0,16},{2,18},{4,20},{6,22},{8,24},{10,26},{12,28},{14,30},{16,0},... | collective-permute-start | bytes 1572872 | tf_op jit(solution)/shard_map/ppermute | solution.py:46
  44.7 27.6 %collective-permute-start.22 = (bf16[64,4096]{1,0:T(8,128)(2,1)}, bf16[64,4096]{1,0:T(8,128)(2,1)S(1)}, u32[]{:S(2)}, u32[]{:S(2)}) collective-permute-start(bf16[64,4096]{1,0:T(8,128)(2,1)} %bitcast_dynamic-update-slice_fusion.13), channel_id=1, source_target_pairs={{0,24},{2,26},{4,28},{6,30},{8,0},{10,2},{12,4},{14,6},{16,8},{18,... | collective-permute-start | bytes 1572872 | tf_op jit(solution)/shard_map/ppermute | solution.py:46
  73.8 246.8 %all-gather.7.cloned.1.call-start = ((), (), s32[]{:S(2)}) async-start(), calls=%async_computation.7 | async-start | bytes 15728640 | tf_op jit(solution)/shard_map/all_gather | solution.py:78
  104.9 32.7 %collective-permute-start.13 = (f32[2,2,16]{2,1,0:T(2,128)S(1)}, f32[2,2,16]{2,1,0:T(2,128)S(1)}, u32[]{:S(2)}, u32[]{:S(2)}) collective-permute-start(f32[2,2,16]{2,1,0:T(2,128)S(1)} %get-tuple-element.306), channel_id=1, source_target_pairs={{0,16},{2,18},{4,20},{6,22},{8,24},{10,26},{12,28},{14,30},{16,0},... | collective-permute-start | bytes 776 | tf_op jit(solution)/shard_map/ppermute | solution.py:46
  104.9 76.1 %collective-permute-start.26 = (bf16[64,6144]{1,0:T(8,128)(2,1)S(1)}, bf16[64,6144]{1,0:T(8,128)(2,1)S(1)}, u32[]{:S(2)}, u32[]{:S(2)}) collective-permute-start(bf16[64,6144]{1,0:T(8,128)(2,1)S(1)} %pad_maximum_fusion.2), channel_id=1, source_target_pairs={{0,8},{2,10},{4,12},{6,14},{8,16},{10,18},{12,20},{14,22},{16,24},... | collective-permute-start | bytes 2359304 | tf_op jit(solution)/shard_map/ppermute | solution.py:46
  105.5 35.9 %collective-permute-start.12 = (f32[2,2,16]{2,1,0:T(2,128)S(1)}, f32[2,2,16]{2,1,0:T(2,128)S(1)}, u32[]{:S(2)}, u32[]{:S(2)}) collective-permute-start(f32[2,2,16]{2,1,0:T(2,128)S(1)} %get-tuple-element.306), channel_id=1, source_target_pairs={{0,8},{2,10},{4,12},{6,14},{8,16},{10,18},{12,20},{14,22},{16,24},... | collective-permute-start | bytes 776 | tf_op jit(solution)/shard_map/ppermute | solution.py:46
  108.4 72.6 %collective-permute-start.27 = (bf16[64,6144]{1,0:T(8,128)(2,1)S(1)}, bf16[64,6144]{1,0:T(8,128)(2,1)}, u32[]{:S(2)}, u32[]{:S(2)}) collective-permute-start(bf16[64,6144]{1,0:T(8,128)(2,1)S(1)} %pad_maximum_fusion.2), channel_id=1, source_target_pairs={{0,16},{2,18},{4,20},{6,22},{8,24},{10,26},{12,28},{14,30},{16,0},... | collective-permute-start | bytes 2359304 | tf_op jit(solution)/shard_map/ppermute | solution.py:46
  109.3 71.7 %collective-permute-start.28 = (bf16[64,6144]{1,0:T(8,128)(2,1)S(1)}, bf16[64,6144]{1,0:T(8,128)(2,1)}, u32[]{:S(2)}, u32[]{:S(2)}) collective-permute-start(bf16[64,6144]{1,0:T(8,128)(2,1)S(1)} %pad_maximum_fusion.2), channel_id=1, source_target_pairs={{0,24},{2,26},{4,28},{6,30},{8,0},{10,2},{12,4},{14,6},{16,8},{18,... | collective-permute-start | bytes 2359304 | tf_op jit(solution)/shard_map/ppermute | solution.py:46
  186.1 299.3 %reduce-scatter.4.cloned.1.call-start = ((), (), s32[]{:S(2)}) async-start(), calls=%async_computation.3 | async-start | bytes 15728640 | tf_op jit(solution)/shard_map/reduce_scatter | solution.py:123
  186.3 31.9 %collective-permute-start.18 = (bf16[16,64,128]{2,1,0:T(8,128)(2,1)S(1)}, bf16[16,64,128]{2,1,0:T(8,128)(2,1)S(1)}, u32[]{:S(2)}, u32[]{:S(2)}) collective-permute-start(bf16[16,64,128]{2,1,0:T(8,128)(2,1)S(1)} %fusion.65), channel_id=1, source_target_pairs={{0,16},{2,18},{4,20},{6,22},{8,24},{10,26},{12,28},{14,30},{16,0},... | collective-permute-start | bytes 786440 | tf_op jit(solution)/shard_map/ppermute | solution.py:46
  358.9 216.2 %reduce-scatter.6.cloned.1.call-start = ((), (), s32[]{:S(2)}) async-start(), calls=%async_computation.4 | async-start | bytes 10485760 | tf_op jit(solution)/shard_map/reduce_scatter | solution.py:123
  485.4 175.0 %reduce-scatter.8.cloned.1.call-start = ((), (), s32[]{:S(2)}) async-start(), calls=%async_computation.5 | async-start | bytes 3604480 | tf_op jit(solution)/shard_map/reduce_scatter | solution.py:123
  492.2 33.9 %collective-permute-start.36 = (bf16[16,64,128]{2,1,0:T(8,128)(2,1)S(1)}, bf16[16,64,128]{2,1,0:T(8,128)(2,1)S(1)}, u32[]{:S(2)}, u32[]{:S(2)}) collective-permute-start(bf16[16,64,128]{2,1,0:T(8,128)(2,1)S(1)} %fusion.71), channel_id=1, source_target_pairs={{0,16},{2,18},{4,20},{6,22},{8,24},{10,26},{12,28},{14,30},{16,0},... | collective-permute-start | bytes 786440 | tf_op jit(solution)/shard_map/ppermute | solution.py:46
  492.2 33.9 %collective-permute-start.35 = (bf16[16,64,128]{2,1,0:T(8,128)(2,1)S(1)}, bf16[16,64,128]{2,1,0:T(8,128)(2,1)S(1)}, u32[]{:S(2)}, u32[]{:S(2)}) collective-permute-start(bf16[16,64,128]{2,1,0:T(8,128)(2,1)S(1)} %fusion.71), channel_id=1, source_target_pairs={{0,8},{2,10},{4,12},{6,14},{8,16},{10,18},{12,20},{14,22},{16,24},... | collective-permute-start | bytes 786440 | tf_op jit(solution)/shard_map/ppermute | solution.py:46
  496.8 53.1 %collective-permute-start.42 = (bf16[64,2048]{1,0:T(8,128)(2,1)}, bf16[64,2048]{1,0:T(8,128)(2,1)}, u32[]{:S(2)}, u32[]{:S(2)}) collective-permute-start(bf16[64,2048]{1,0:T(8,128)(2,1)} %get-tuple-element.279), channel_id=1, source_target_pairs={{0,24},{2,26},{4,28},{6,30},{8,0},{10,2},{12,4},{14,6},{16,8},{18,... | collective-permute-start | bytes 786440 | tf_op jit(solution)/shard_map/ppermute | solution.py:46
  499.2 50.8 %collective-permute-start.41 = (bf16[64,2048]{1,0:T(8,128)(2,1)}, bf16[64,2048]{1,0:T(8,128)(2,1)}, u32[]{:S(2)}, u32[]{:S(2)}) collective-permute-start(bf16[64,2048]{1,0:T(8,128)(2,1)} %get-tuple-element.280), channel_id=1, source_target_pairs={{0,16},{2,18},{4,20},{6,22},{8,24},{10,26},{12,28},{14,30},{16,0},... | collective-permute-start | bytes 786440 | tf_op jit(solution)/shard_map/ppermute | solution.py:46
  501.9 51.8 %collective-permute-start.40 = (bf16[64,2048]{1,0:T(8,128)(2,1)S(1)}, bf16[64,2048]{1,0:T(8,128)(2,1)}, u32[]{:S(2)}, u32[]{:S(2)}) collective-permute-start(bf16[64,2048]{1,0:T(8,128)(2,1)S(1)} %get-tuple-element.278), channel_id=1, source_target_pairs={{0,8},{2,10},{4,12},{6,14},{8,16},{10,18},{12,20},{14,22},{16,24},... | collective-permute-start | bytes 786440 | tf_op jit(solution)/shard_map/ppermute | solution.py:46
  526.1 33.5 %collective-permute-start.45 = (bf16[64,2048]{1,0:T(8,128)(2,1)S(1)}, bf16[64,2048]{1,0:T(8,128)(2,1)}, u32[]{:S(2)}, u32[]{:S(2)}) collective-permute-start(bf16[64,2048]{1,0:T(8,128)(2,1)S(1)} %get-tuple-element.276), channel_id=1, source_target_pairs={{0,24},{2,26},{4,28},{6,30},{8,0},{10,2},{12,4},{14,6},{16,8},{18,... | collective-permute-start | bytes 786440 | tf_op jit(solution)/shard_map/ppermute | solution.py:46
  526.1 35.4 %collective-permute-start.44 = (bf16[64,2048]{1,0:T(8,128)(2,1)S(1)}, bf16[64,2048]{1,0:T(8,128)(2,1)S(1)}, u32[]{:S(2)}, u32[]{:S(2)}) collective-permute-start(bf16[64,2048]{1,0:T(8,128)(2,1)S(1)} %get-tuple-element.277), channel_id=1, source_target_pairs={{0,16},{2,18},{4,20},{6,22},{8,24},{10,26},{12,28},{14,30},{16,0},... | collective-permute-start | bytes 786440 | tf_op jit(solution)/shard_map/ppermute | solution.py:46
  550.0 28.1 %collective-permute-start.63 = (bf16[64,2048]{1,0:T(8,128)(2,1)}, bf16[64,2048]{1,0:T(8,128)(2,1)}, u32[]{:S(2)}, u32[]{:S(2)}) collective-permute-start(bf16[64,2048]{1,0:T(8,128)(2,1)} %get-tuple-element.267), channel_id=1, source_target_pairs={{0,24},{2,26},{4,28},{6,30},{8,0},{10,2},{12,4},{14,6},{16,8},{18,... | collective-permute-start | bytes 786440 | tf_op jit(solution)/shard_map/ppermute | solution.py:46
  557.6 24.8 %collective-permute-start.62 = (bf16[64,2048]{1,0:T(8,128)(2,1)}, bf16[64,2048]{1,0:T(8,128)(2,1)}, u32[]{:S(2)}, u32[]{:S(2)}) collective-permute-start(bf16[64,2048]{1,0:T(8,128)(2,1)} %get-tuple-element.268), channel_id=1, source_target_pairs={{0,16},{2,18},{4,20},{6,22},{8,24},{10,26},{12,28},{14,30},{16,0},... | collective-permute-start | bytes 786440 | tf_op jit(solution)/shard_map/ppermute | solution.py:46
  559.6 22.8 %collective-permute-start.61 = (bf16[64,2048]{1,0:T(8,128)(2,1)}, bf16[64,2048]{1,0:T(8,128)(2,1)}, u32[]{:S(2)}, u32[]{:S(2)}) collective-permute-start(bf16[64,2048]{1,0:T(8,128)(2,1)} %get-tuple-element.266), channel_id=1, source_target_pairs={{0,8},{2,10},{4,12},{6,14},{8,16},{10,18},{12,20},{14,22},{16,24},... | collective-permute-start | bytes 786440 | tf_op jit(solution)/shard_map/ppermute | solution.py:46
  561.5 23.7 %collective-permute-start.50 = (f32[4,256]{1,0:T(4,128)S(1)}, f32[4,256]{1,0:T(4,128)S(1)}, u32[]{:S(2)}, u32[]{:S(2)}) collective-permute-start(f32[4,256]{1,0:T(4,128)S(1)} %slice.223), channel_id=1, source_target_pairs={{0,1},{1,0},{2,3},{3,2},{4,5},{5,4},{6,7},{7,6},{8,9},{9,8},{10,11... | collective-permute-start | bytes 12296 | tf_op jit(solution)/shard_map/ppermute | solution.py:162
  614.9 36.7 %collective-permute-start.48 = (bf16[64,2048]{1,0:T(8,128)(2,1)S(1)}, bf16[64,2048]{1,0:T(8,128)(2,1)}, u32[]{:S(2)}, u32[]{:S(2)}) collective-permute-start(bf16[64,2048]{1,0:T(8,128)(2,1)S(1)} %get-tuple-element.274), channel_id=1, source_target_pairs={{0,16},{2,18},{4,20},{6,22},{8,24},{10,26},{12,28},{14,30},{16,0},... | collective-permute-start | bytes 786440 | tf_op jit(solution)/shard_map/ppermute | solution.py:46
  616.8 34.8 %collective-permute-start.47 = (bf16[64,2048]{1,0:T(8,128)(2,1)S(1)}, bf16[64,2048]{1,0:T(8,128)(2,1)}, u32[]{:S(2)}, u32[]{:S(2)}) collective-permute-start(bf16[64,2048]{1,0:T(8,128)(2,1)S(1)} %get-tuple-element.272), channel_id=1, source_target_pairs={{0,8},{2,10},{4,12},{6,14},{8,16},{10,18},{12,20},{14,22},{16,24},... | collective-permute-start | bytes 786440 | tf_op jit(solution)/shard_map/ppermute | solution.py:46
  621.1 35.4 %collective-permute-start.60 = (bf16[64,2048]{1,0:T(8,128)(2,1)S(1)}, bf16[64,2048]{1,0:T(8,128)(2,1)S(1)}, u32[]{:S(2)}, u32[]{:S(2)}) collective-permute-start(bf16[64,2048]{1,0:T(8,128)(2,1)S(1)} %get-tuple-element.270), channel_id=1, source_target_pairs={{0,24},{2,26},{4,28},{6,30},{8,0},{10,2},{12,4},{14,6},{16,8},{18,... | collective-permute-start | bytes 786440 | tf_op jit(solution)/shard_map/ppermute | solution.py:46
  625.0 35.2 %collective-permute-start.59 = (bf16[64,2048]{1,0:T(8,128)(2,1)S(1)}, bf16[64,2048]{1,0:T(8,128)(2,1)S(1)}, u32[]{:S(2)}, u32[]{:S(2)}) collective-permute-start(bf16[64,2048]{1,0:T(8,128)(2,1)S(1)} %get-tuple-element.271), channel_id=1, source_target_pairs={{0,16},{2,18},{4,20},{6,22},{8,24},{10,26},{12,28},{14,30},{16,0},... | collective-permute-start | bytes 786440 | tf_op jit(solution)/shard_map/ppermute | solution.py:46
  625.0 35.2 %collective-permute-start.58 = (bf16[64,2048]{1,0:T(8,128)(2,1)S(1)}, bf16[64,2048]{1,0:T(8,128)(2,1)S(1)}, u32[]{:S(2)}, u32[]{:S(2)}) collective-permute-start(bf16[64,2048]{1,0:T(8,128)(2,1)S(1)} %get-tuple-element.269), channel_id=1, source_target_pairs={{0,8},{2,10},{4,12},{6,14},{8,16},{10,18},{12,20},{14,22},{16,24},... | collective-permute-start | bytes 786440 | tf_op jit(solution)/shard_map/ppermute | solution.py:46
  662.2 31.3 %collective-permute-start.56 = (bf16[64,1408]{0,1:T(8,128)(2,1)S(1)}, bf16[64,1408]{0,1:T(8,128)(2,1)S(1)}, u32[]{:S(2)}, u32[]{:S(2)}) collective-permute-start(bf16[64,1408]{0,1:T(8,128)(2,1)S(1)} %bitcast.282), channel_id=1, source_target_pairs={{0,16},{2,18},{4,20},{6,22},{8,24},{10,26},{12,28},{14,30},{16,0},... | collective-permute-start | bytes 540680 | tf_op jit(solution)/shard_map/ppermute | solution.py:46
  663.1 30.3 %collective-permute-start.55 = (bf16[64,1408]{0,1:T(8,128)(2,1)S(1)}, bf16[64,1408]{0,1:T(8,128)(2,1)S(1)}, u32[]{:S(2)}, u32[]{:S(2)}) collective-permute-start(bf16[64,1408]{0,1:T(8,128)(2,1)S(1)} %bitcast.283), channel_id=1, source_target_pairs={{0,8},{2,10},{4,12},{6,14},{8,16},{10,18},{12,20},{14,22},{16,24},... | collective-permute-start | bytes 540680 | tf_op jit(solution)/shard_map/ppermute | solution.py:46
  (96 other events, 1299.7 us)
Sparse Core Ops, SparseCore 0:
  73.9 104.4 all-gather.4
  186.2 134.3 all-gather.6
  359.0 126.3 reduce-scatter.3
  488.3 86.7 reduce-scatter.5
  578.3 48.5 reduce-scatter.7
